TPU v7x, 32 devices: a whole 2x2x4 slice. The times are simulated.
32 devices in a mesh: dp: 2 (over y), fsdp: 16 (over z, x, core).
Axes of the slice: x: 2, y: 2, z: 4, core: 2. Of those that a mesh axis runs over, the one named last changes fastest.
Arguments:
- images: bfloat16 [256, 257, 1280], P(('dp', 'fsdp')), may hold values from -6 to 6
- cotangent: bfloat16 [256, 257, 1280], P(('dp', 'fsdp')), may hold values from -6 to 6
- w_qkv: bfloat16 [1280, 3840], P('fsdp')
- w_out: bfloat16 [1280, 1280], P('fsdp'), may hold values from -3 to 3
- w_up: bfloat16 [1280, 5120], P('fsdp'), may hold values from -0.15625 to 0.15625
- w_down: bfloat16 [5120, 1280], P('fsdp'), may hold values from -0.078125 to 0.078125
- b_qv: bfloat16 [2560], P('fsdp'), may hold values from -3 to 3
- b_out: bfloat16 [1280], P('fsdp'), may hold values from -3 to 3
- b_up: bfloat16 [5120], P('fsdp'), may hold values from -3 to 3
- b_down: bfloat16 [1280], P('fsdp'), may hold values from -3 to 3
- first_norm_scale: bfloat16 [1280], P('fsdp'), may hold values from 0.099609375 to 1.8984375
- first_norm_bias: bfloat16 [1280], P('fsdp'), may hold values from -3 to 3
- second_norm_scale: bfloat16 [1280], P('fsdp'), may hold values from 0.099609375 to 1.8984375
- second_norm_bias: bfloat16 [1280], P('fsdp'), may hold values from -3 to 3
Outputs:
- result: float32 [256, 257, 1280], P(('dp', 'fsdp'))
- d_images: float32 [256, 257, 1280], P(('dp', 'fsdp'))
- g_qkv: float32 [1280, 3840], P('fsdp')
- g_out: float32 [1280, 1280], P('fsdp')
- g_up: float32 [1280, 5120], P('fsdp')
- g_down: float32 [5120, 1280], P('fsdp')
- g_b_qv: float32 [2560], P('fsdp')
- g_b_out: float32 [1280], P('fsdp')
- g_b_up: float32 [5120], P('fsdp')
- g_b_down: float32 [1280], P('fsdp')
- g_gain_one: float32 [1280], P('fsdp')
- g_shift_one: float32 [1280], P('fsdp')
- g_gain_two: float32 [1280], P('fsdp')
- g_shift_two: float32 [1280], P('fsdp')
All inputs are finite; a program needn't handle non-finite values.
Results may differ from a plain program's by a relative error of at most 0.012.
Values may be sent and summed in bfloat16 or wider, within the bound.
No kernel may reach another device: no remote copies, remote signals or barrier semaphores. Data moves between devices by JAX's collectives and lax.ppermute only.
A program may use at most 512 MiB of HBM per device.

v0:
```python
import jax
import jax.numpy as jnp
from jax import lax
from jax.sharding import PartitionSpec as P

D = 1280
H = 16
HD = 80
MB = 2


EPS = 1e-06


def matmul(left, right):
    return jnp.dot(left, right, preferred_element_type=jnp.float32)


def batched(form, left, right):
    return jnp.einsum(form, left, right, preferred_element_type=jnp.float32)


def layer_norm_forward(token_rows, norm_scale, norm_bias):
    centered_rows = token_rows - jnp.mean(token_rows, -1, keepdims=True)
    inverse_deviation = lax.rsqrt(jnp.mean(centered_rows * centered_rows, -1, keepdims=True) + EPS)
    standardized_rows = centered_rows * inverse_deviation
    normalized_rows = (
        standardized_rows * norm_scale.astype(jnp.float32) + norm_bias.astype(jnp.float32)
    ).astype(jnp.bfloat16)
    return (standardized_rows, inverse_deviation, normalized_rows)


def layer_norm_backward(incoming_gradient, standardized_rows, inverse_deviation, norm_scale):
    scaled_rows = incoming_gradient * norm_scale.astype(jnp.float32)
    first_residual = jnp.mean(scaled_rows, -1, keepdims=True)
    second_residual = jnp.mean(scaled_rows * standardized_rows, -1, keepdims=True)
    input_gradient = inverse_deviation * (
        scaled_rows - first_residual - standardized_rows * second_residual
    )
    return (
        input_gradient,
        jnp.sum(incoming_gradient * standardized_rows, 0),
        jnp.sum(incoming_gradient, 0),
    )


def split_heads(packed_projection, count, length):
    query = packed_projection[:, :D].reshape(count, length, H, HD)
    keys_all = packed_projection[:, D : 2 * D].reshape(count, length, H, HD)
    values = packed_projection[:, 2 * D :].reshape(count, length, H, HD)
    return (query, keys_all, values)


def forward(block, params):
    (
        w_qkv,
        w_out,
        w_up,
        w_down,
        b_qv,
        b_out,
        b_up,
        b_down,
        first_norm_scale,
        first_norm_bias,
        second_norm_scale,
        second_norm_bias,
    ) = params
    count, length, width = block.shape
    token_rows = block.reshape(count * length, width).astype(jnp.float32)
    first_standardized, first_inverse_deviation, first_normalized = layer_norm_forward(
        token_rows, first_norm_scale, first_norm_bias
    )
    bias_all = jnp.concatenate(
        [b_qv[:D].astype(jnp.float32), jnp.zeros((D,), jnp.float32), b_qv[D:].astype(jnp.float32)]
    )
    packed_projection = (matmul(first_normalized, w_qkv) + bias_all).astype(jnp.bfloat16)
    query, keys_all, values = split_heads(packed_projection, count, length)
    scores = batched("bqhd,bkhd->bhqk", query, keys_all) * HD ** (-0.5)
    top = jnp.max(scores, -1, keepdims=True)
    log_exponent_sum = top + jnp.log(jnp.sum(jnp.exp(scores - top), -1, keepdims=True))
    probs = jnp.exp(scores - log_exponent_sum).astype(jnp.bfloat16)
    attention_mixture = (
        batched("bhqk,bkhd->bqhd", probs, values)
        .astype(jnp.bfloat16)
        .reshape(count * length, width)
    )
    hidden_state = token_rows + matmul(attention_mixture, w_out) + b_out.astype(jnp.float32)
    second_standardized, second_inverse_deviation, second_normalized = layer_norm_forward(
        hidden_state, second_norm_scale, second_norm_bias
    )
    inner_activation = matmul(second_normalized, w_up) + b_up.astype(jnp.float32)
    activation_input = jax.nn.gelu(inner_activation, approximate=False).astype(jnp.bfloat16)
    result = hidden_state + matmul(activation_input, w_down) + b_down.astype(jnp.float32)
    saved_residuals = (
        first_standardized,
        first_inverse_deviation,
        first_normalized,
        packed_projection,
        log_exponent_sum,
        attention_mixture,
        second_standardized,
        second_inverse_deviation,
        second_normalized,
        inner_activation,
        activation_input,
    )
    return (result.reshape(count, length, width), saved_residuals)


def backward(cotangent, saved_residuals, params):
    (
        w_qkv,
        w_out,
        w_up,
        w_down,
        b_qv,
        b_out,
        b_up,
        b_down,
        first_norm_scale,
        first_norm_bias,
        second_norm_scale,
        second_norm_bias,
    ) = params
    (
        first_standardized,
        first_inverse_deviation,
        first_normalized,
        packed_projection,
        log_exponent_sum,
        attention_mixture,
        second_standardized,
        second_inverse_deviation,
        second_normalized,
        inner_activation,
        activation_input,
    ) = saved_residuals
    count, length, width = cotangent.shape
    grad_rows = cotangent.reshape(count * length, width)
    grad_wide = grad_rows.astype(jnp.float32)
    g_down = matmul(activation_input.T, grad_rows)
    gb_down = jnp.sum(grad_wide, 0)
    d_active = matmul(grad_rows, w_down.T)
    slope = (
        0.5 * (1.0 + jax.scipy.special.erf(inner_activation * 0.7071067811865476))
        + inner_activation
        * jnp.exp(-0.5 * inner_activation * inner_activation)
        * 0.3989422804014327
    )
    d_inner = d_active * slope
    gb_up = jnp.sum(d_inner, 0)
    d_inner_b = d_inner.astype(jnp.bfloat16)
    g_up = matmul(second_normalized.T, d_inner_b)
    second_normalized_gradient = matmul(d_inner_b, w_up.T)
    hidden_norm_gradient, second_scale_gradient, second_bias_gradient = layer_norm_backward(
        second_normalized_gradient, second_standardized, second_inverse_deviation, second_norm_scale
    )
    d_hidden = grad_wide + hidden_norm_gradient
    d_hidden_b = d_hidden.astype(jnp.bfloat16)
    g_out = matmul(attention_mixture.T, d_hidden_b)
    gb_out = jnp.sum(d_hidden, 0)
    d_mixed = matmul(d_hidden_b, w_out.T).astype(jnp.bfloat16)
    query, keys_all, values = split_heads(packed_projection, count, length)
    d_heads = d_mixed.reshape(count, length, H, HD)
    mixed_heads = attention_mixture.reshape(count, length, H, HD)
    scores = batched("bqhd,bkhd->bhqk", query, keys_all) * HD ** (-0.5)
    probs_wide = jnp.exp(scores - log_exponent_sum)
    probs = probs_wide.astype(jnp.bfloat16)
    d_values = batched("bhqk,bqhd->bkhd", probs, d_heads)
    d_probs = batched("bqhd,bkhd->bhqk", d_heads, values)
    delta = jnp.sum(d_heads.astype(jnp.float32) * mixed_heads.astype(jnp.float32), -1)
    delta = jnp.transpose(delta, (0, 2, 1))[..., None]
    d_scores = (probs_wide * (d_probs - delta) * HD ** (-0.5)).astype(jnp.bfloat16)
    d_query = batched("bhqk,bkhd->bqhd", d_scores, keys_all).reshape(count * length, width)
    d_keys = batched("bhqk,bqhd->bkhd", d_scores, query).reshape(count * length, width)
    d_values = d_values.reshape(count * length, width)
    gb_qv = jnp.concatenate([jnp.sum(d_query, 0), jnp.sum(d_values, 0)])
    d_packed = jnp.concatenate([d_query, d_keys, d_values], 1).astype(jnp.bfloat16)
    g_qkv = matmul(first_normalized.T, d_packed)
    first_normalized_gradient = matmul(d_packed, w_qkv.T)
    row_norm_gradient, first_scale_gradient, first_bias_gradient = layer_norm_backward(
        first_normalized_gradient, first_standardized, first_inverse_deviation, first_norm_scale
    )
    d_rows = d_hidden + row_norm_gradient
    grads = (
        g_qkv,
        g_out,
        g_up,
        g_down,
        gb_qv,
        gb_out,
        gb_up,
        gb_down,
        first_scale_gradient,
        first_bias_gradient,
        second_scale_gradient,
        second_bias_gradient,
    )
    return (d_rows.reshape(count, length, width), grads)


def add_all(first_residual, second_residual):
    return tuple((a + b for a, b in zip(first_residual, second_residual)))


def on_device(
    images,
    cotangent,
    w_qkv,
    w_out,
    w_up,
    w_down,
    b_qv,
    b_out,
    b_up,
    b_down,
    first_norm_scale,
    first_norm_bias,
    second_norm_scale,
    second_norm_bias,
):
    per_batch = images.shape[0] // MB
    results = []
    kept = []
    for micro in range(MB):
        params = (
            lax.all_gather(w_qkv, "fsdp", axis=0, tiled=True),
            lax.all_gather(w_out, "fsdp", axis=0, tiled=True),
            lax.all_gather(w_up, "fsdp", axis=0, tiled=True),
            lax.all_gather(w_down, "fsdp", axis=0, tiled=True),
            lax.all_gather(b_qv, "fsdp", axis=0, tiled=True),
            lax.all_gather(b_out, "fsdp", axis=0, tiled=True),
            lax.all_gather(b_up, "fsdp", axis=0, tiled=True),
            lax.all_gather(b_down, "fsdp", axis=0, tiled=True),
            lax.all_gather(first_norm_scale, "fsdp", axis=0, tiled=True),
            lax.all_gather(first_norm_bias, "fsdp", axis=0, tiled=True),
            lax.all_gather(second_norm_scale, "fsdp", axis=0, tiled=True),
            lax.all_gather(second_norm_bias, "fsdp", axis=0, tiled=True),
        )
        result, saved_residuals = forward(
            images[micro * per_batch : (micro + 1) * per_batch], params
        )
        results.append(result)
        kept.append(saved_residuals)
    d_list = [None] * MB
    totals = None
    for micro in reversed(range(MB)):
        params = (
            lax.all_gather(w_qkv, "fsdp", axis=0, tiled=True),
            lax.all_gather(w_out, "fsdp", axis=0, tiled=True),
            lax.all_gather(w_up, "fsdp", axis=0, tiled=True),
            lax.all_gather(w_down, "fsdp", axis=0, tiled=True),
            lax.all_gather(b_qv, "fsdp", axis=0, tiled=True),
            lax.all_gather(b_out, "fsdp", axis=0, tiled=True),
            lax.all_gather(b_up, "fsdp", axis=0, tiled=True),
            lax.all_gather(b_down, "fsdp", axis=0, tiled=True),
            lax.all_gather(first_norm_scale, "fsdp", axis=0, tiled=True),
            lax.all_gather(first_norm_bias, "fsdp", axis=0, tiled=True),
            lax.all_gather(second_norm_scale, "fsdp", axis=0, tiled=True),
            lax.all_gather(second_norm_bias, "fsdp", axis=0, tiled=True),
        )
        d_rows, grads = backward(
            cotangent[micro * per_batch : (micro + 1) * per_batch], kept[micro], params
        )
        d_list[micro] = d_rows
        totals = grads if totals is None else add_all(totals, grads)
    totals = (
        lax.psum_scatter(totals[0], "fsdp", scatter_dimension=0, tiled=True),
        lax.psum_scatter(totals[1], "fsdp", scatter_dimension=0, tiled=True),
        lax.psum_scatter(totals[2], "fsdp", scatter_dimension=0, tiled=True),
        lax.psum_scatter(totals[3], "fsdp", scatter_dimension=0, tiled=True),
        lax.psum_scatter(totals[4], "fsdp", scatter_dimension=0, tiled=True),
        lax.psum_scatter(totals[5], "fsdp", scatter_dimension=0, tiled=True),
        lax.psum_scatter(totals[6], "fsdp", scatter_dimension=0, tiled=True),
        lax.psum_scatter(totals[7], "fsdp", scatter_dimension=0, tiled=True),
        lax.psum_scatter(totals[8], "fsdp", scatter_dimension=0, tiled=True),
        lax.psum_scatter(totals[9], "fsdp", scatter_dimension=0, tiled=True),
        lax.psum_scatter(totals[10], "fsdp", scatter_dimension=0, tiled=True),
        lax.psum_scatter(totals[11], "fsdp", scatter_dimension=0, tiled=True),
    )
    final = (
        lax.psum(totals[0].astype(jnp.bfloat16), "dp").astype(jnp.float32),
        lax.psum(totals[1].astype(jnp.bfloat16), "dp").astype(jnp.float32),
        lax.psum(totals[2].astype(jnp.bfloat16), "dp").astype(jnp.float32),
        lax.psum(totals[3].astype(jnp.bfloat16), "dp").astype(jnp.float32),
        lax.psum(totals[4].astype(jnp.bfloat16), "dp").astype(jnp.float32),
        lax.psum(totals[5].astype(jnp.bfloat16), "dp").astype(jnp.float32),
        lax.psum(totals[6].astype(jnp.bfloat16), "dp").astype(jnp.float32),
        lax.psum(totals[7].astype(jnp.bfloat16), "dp").astype(jnp.float32),
        lax.psum(totals[8].astype(jnp.bfloat16), "dp").astype(jnp.float32),
        lax.psum(totals[9].astype(jnp.bfloat16), "dp").astype(jnp.float32),
        lax.psum(totals[10].astype(jnp.bfloat16), "dp").astype(jnp.float32),
        lax.psum(totals[11].astype(jnp.bfloat16), "dp").astype(jnp.float32),
    )
    outputs = jnp.concatenate(results, 0)
    d_images = jnp.concatenate(d_list, 0)
    return (
        outputs,
        d_images,
        final[0],
        final[1],
        final[2],
        final[3],
        final[4],
        final[5],
        final[6],
        final[7],
        final[8],
        final[9],
        final[10],
        final[11],
    )


def solution(mesh):
    return jax.shard_map(
        on_device,
        mesh=mesh,
        in_specs=(
            P(("dp", "fsdp"), None, None),
            P(("dp", "fsdp"), None, None),
            P("fsdp", None),
            P("fsdp", None),
            P("fsdp", None),
            P("fsdp", None),
            P("fsdp"),
            P("fsdp"),
            P("fsdp"),
            P("fsdp"),
            P("fsdp"),
            P("fsdp"),
            P("fsdp"),
            P("fsdp"),
        ),
        out_specs=(
            P(("dp", "fsdp"), None, None),
            P(("dp", "fsdp"), None, None),
            P("fsdp", None),
            P("fsdp", None),
            P("fsdp", None),
            P("fsdp", None),
            P("fsdp"),
            P("fsdp"),
            P("fsdp"),
            P("fsdp"),
            P("fsdp"),
            P("fsdp"),
            P("fsdp"),
            P("fsdp"),
        ),
        check_vma=False,
    )
```

profile of v0, /device:TPU:0, one launch (start us, length us, event | category | flops | bytes accessed | tf_op | source)
XLA Modules:
  0.0 1918.0 jit_solution(14469423983518229722)
XLA Ops:
  42.2 66.0 %all-reduce.17 = (bf16[2560]{0:T(1024)(128)(2,1)S(1)}, bf16[1280]{0:T(1024)(128)(2,1)S(1)}, bf16[1280]{0:T(1024)(128)(2,1)S(1)}, bf16[1280]{0:T(1024)(128)(2,1)S...) all-reduce(bf16[2560]{0:T(1024)(128)(2,1)S(1)} %dynamic-update-slic, ...), channel_id=1, replica_groups=mesh['dp'=2,'fsdp'=16] {'fsdp'}, use_global_device_ids=true, to_apply=%add.2 | all-reduce | flops 15360 | bytes 61440
  149.3 17.4 fusion.30
  246.1 18.3 fusion.31
  430.9 64.1 %fusion.4 = (bf16[1028,5120]{1,0:T(8,128)(2,1)}, f32[1028,5120]{1,0:T(8,128)}) fusion(f32[5120]{0:T(1024)S(1)} %copy-done.53, bf16[1280,5120]{1,0:T(8,128)(2,1)} %all-gather.9.cloned.1.call-done, f32[1028,1280]{1,0:T(8,128)} %copy-done.4, f32[1280]{0:T(1024)S(1)} %copy-done.34, f32[1280]{0:T(1024)S(1)} %copy-done.32, f32[1028]{0:T(1024)S(1)} %add_rsqrt_fusion.3, ...), kind=kOutput, calls=%fused_computation.22 | convolution fusion | flops 13828162560 | bytes 49989664 | tf_op jit(solution)/shard_map/dot_general | solution.py:16
  495.0 24.5 %fusion.68 = (f32[5120]{0:T(1024)}, bf16[1028,5120]{1,0:T(8,128)(2,1)S(1)}) fusion(f32[1028,5120]{1,0:T(8,128)} %get-tuple-element.140, bf16[1028,1280]{1,0:T(8,128)(2,1)S(1)} %copy-done.23, bf16[5120,1280]{1,0:T(8,128)(2,1)} %all-gather.11.cloned.1.call-done), kind=kOutput, calls=%fused_computation.194 | convolution fusion | flops 13532093440 | bytes 47339520 | tf_op jit(solution)/shard_map/dot_general | solution.py:16
  519.6 23.1 %multiply_reduce_fusion.4 = (f32[1280]{0:T(1024)}, f32[1028]{0:T(1024)S(1)}, f32[1028]{0:T(1024)S(1)}, f32[1280]{0:T(1024)}, f32[1028,1280]{1,0:T(8,128)}) fusion(f32[1028,1280]{1,0:T(8,128)S(1)} %copy-done.5, f32[1028]{0:T(1024)S(1)} %add_rsqrt_fusion.3, f32[1028]{0:T(1024)S(1)} %broadcast_multiply_fusion.11, f32[1280]{0:T(1024)S(1)} %copy-done.32, ...), kind=kOutput, calls=%fused_computation.92 | convolution fusion | flops 13486040064 | bytes 34192448 | tf_op jit(solution)/shard_map/dot_general | solution.py:16
  543.9 65.7 %fusion.7 = (bf16[1028,5120]{1,0:T(8,128)(2,1)}, f32[1028,5120]{1,0:T(8,128)}) fusion(f32[5120]{0:T(1024)S(1)} %copy-done.53, bf16[1280,5120]{1,0:T(8,128)(2,1)} %all-gather.9.cloned.1.call-done, f32[1028,1280]{1,0:T(8,128)S(1)} %copy-done.9, f32[1028]{0:T(1024)S(1)} %copy-done.51, f32[1028]{0:T(1024)S(1)} %copy-done.40, f32[1280]{0:T(1024)S(1)} %copy-done.34, ...), kind=kOutput, calls=%fused_computation.25 | convolution fusion | flops 13828162560 | bytes 49989664 | tf_op jit(solution)/shard_map/dot_general | solution.py:16
  609.6 25.1 %fusion.67 = (f32[5120]{0:T(1024)}, bf16[1028,5120]{1,0:T(8,128)(2,1)}) fusion(f32[1028,5120]{1,0:T(8,128)} %get-tuple-element.134, bf16[1028,1280]{1,0:T(8,128)(2,1)S(1)} %copy-done.14, bf16[5120,1280]{1,0:T(8,128)(2,1)S(1)} %copy-done.73), kind=kOutput, calls=%fused_computation.193 | convolution fusion | flops 13532093440 | bytes 47339520 | tf_op jit(solution)/shard_map/dot_general | solution.py:16
  634.7 29.2 %fusion.59 = (f32[1280]{0:T(1024)}, f32[1028,1280]{1,0:T(8,128)}, f32[1280]{0:T(1024)}, f32[1028]{0:T(1024)S(1)}, f32[1028]{0:T(1024)S(1)}, /*index=5*/f32[1280]{0:T(1024)}, f32[1028,1280]{1,0:T(8,128)}) fusion(f32[1028]{0:T(1024)S(1)} %copy-done.68, f32[1028,1280]{1,0:T(8,128)} %copy-done.4, f32[1028]{0:T(1024)S(1)} %copy-done.18, ...), kind=kOutput, calls=%fused_computation.185 | convolution fusion | flops 13499197440 | bytes 52635776 | tf_op jit(solution)/shard_map/dot_general | solution.py:16
  712.9 20.1 %multiply_convert_fusion = bf16[4,16,257,257]{2,3,1,0:T(8,128)(2,1)} fusion(f32[4,16,257,257]{2,3,1,0:T(8,128)} %get-tuple-element.130, f32[4,16,257]{2,1,0:T(8,128)S(1)} %bitcast.106, f32[4,16,257]{2,1,0:T(8,128)S(1)} %copy-done.31, bf16[4,257,16,80]{1,3,2,0:T(8,128)(2,1)S(1)} %copy-done.2, bf16[4,257,16,80]{1,3,2,0:T(8,128)(2,1)} %copy.163), kind=kOutput, calls=%fused_computation.4 | convolution fusion | flops 701704576 | bytes 30757760 | tf_op jit(solution)/shard_map/bqhd,bkhd->bhqk/dot_general | solution.py:20
  798.3 20.1 %multiply_convert_fusion.1 = bf16[4,16,257,257]{2,3,1,0:T(8,128)(2,1)} fusion(f32[4,16,257,257]{2,3,1,0:T(8,128)} %get-tuple-element.136, f32[4,16,257]{2,1,0:T(8,128)S(1)} %bitcast.107, f32[4,16,257]{2,1,0:T(8,128)S(1)} %copy-done.29, bf16[4,257,16,80]{1,3,2,0:T(8,128)(2,1)S(1)} %copy-done.3, bf16[4,257,16,80]{1,3,2,0:T(8,128)(2,1)} %copy.154), kind=kOutput, calls=%fused_computation.5 | convolution fusion | flops 701704576 | bytes 30757760 | tf_op jit(solution)/shard_map/bqhd,bkhd->bhqk/dot_general | solution.py:20
  968.0 18.8 fusion.58
  986.7 24.4 %convolution_add_fusion.6 = f32[1280,3840]{1,0:T(8,128)} fusion(f32[1280,3840]{1,0:T(8,128)} %fusion.58, bf16[1028,3840]{1,0:T(8,128)(2,1)} %copy-done.36, f32[1028,1280]{1,0:T(8,128)} %reshape.286, f32[1280]{0:T(1024)S(1)} %copy-done.66, f32[1280]{0:T(1024)S(1)} %copy-done.50, f32[1028]{0:T(1024)S(1)} %copy-done.62, f32[1028]{0:T(1024)S(1)} %copy-done.64), kind=kOutput, calls=%fused_computation.66 | convolution fusion | flops 10117145600 | bytes 52498464 | tf_op jit(solution)/shard_map/dot_general | solution.py:16
  1011.9 26.9 %fusion.36 = f32[1280,5120]{1,0:T(8,128)} fusion(bf16[1028,5120]{1,0:T(8,128)(2,1)} %get-tuple-element.154, f32[1028,1280]{1,0:T(8,128)} %copy-done.8, f32[1028]{0:T(1024)S(1)} %copy-done.52, f32[1028]{0:T(1024)S(1)} %copy-done.41, f32[1280]{0:T(1024)S(1)} %copy-done.35, f32[1280]{0:T(1024)S(1)} %copy-done.33), kind=kOutput, calls=%fused_computation.100 | convolution fusion | flops 13480780800 | bytes 42022944 | tf_op jit(solution)/shard_map/dot_general | solution.py:16
  1038.7 33.3 %convolution_add_fusion.2 = f32[1280,5120]{1,0:T(8,128)} fusion(f32[1280,5120]{1,0:T(8,128)} %fusion.36, bf16[1028,5120]{1,0:T(8,128)(2,1)} %copy-done.6, f32[1028,1280]{1,0:T(8,128)} %copy-done.4, f32[1280]{0:T(1024)S(1)} %copy-done.35, f32[1280]{0:T(1024)S(1)} %copy-done.33, f32[1028]{0:T(1024)S(1)} %copy-done.22, f32[1028]{0:T(1024)S(1)} %copy-done.19), kind=kOutput, calls=%fused_computation.14 | convolution fusion | flops 13487334400 | bytes 68237344 | tf_op jit(solution)/shard_map/dot_general | solution.py:16
  1073.8 23.1 %fusion.69 = f32[5120,1280]{1,0:T(8,128)} fusion(bf16[1028,5120]{1,0:T(8,128)(2,1)} %get-tuple-element.133, bf16[1028,1280]{1,0:T(8,128)(2,1)S(1)} %copy-done.15), kind=kOutput, calls=%fused_computation.195 | convolution fusion | flops 13474201600 | bytes 39372800 | tf_op jit(solution)/shard_map/dot_general | solution.py:16
  1097.0 28.9 %convolution_add_fusion.3 = f32[5120,1280]{1,0:T(8,128)} fusion(f32[5120,1280]{1,0:T(8,128)} %fusion.69, bf16[1028,5120]{1,0:T(8,128)(2,1)} %get-tuple-element.139, bf16[1028,1280]{1,0:T(8,128)(2,1)S(1)} %copy-done.24), kind=kOutput, calls=%fused_computation.15 | convolution fusion | flops 13480755200 | bytes 65587200 | tf_op jit(solution)/shard_map/dot_general | solution.py:16
  1134.9 19.6 %multiply_reduce_fusion.6 = (f32[1280]{0:T(1024)S(1)}, f32[1028]{0:T(1024)S(1)}, f32[1028]{0:T(1024)S(1)}, f32[1280]{0:T(1024)S(1)}, f32[1028,1280]{1,0:T(8,128)}) fusion(f32[1028,1280]{1,0:T(8,128)} %reshape.286, f32[1028]{0:T(1024)S(1)} %copy-done.62, f32[1028]{0:T(1024)S(1)} %copy-done.64, f32[1280]{0:T(1024)S(1)} %copy-done.50, ...), kind=kOutput, calls=%fused_computation.94 | convolution fusion | flops 10117489664 | bytes 28283968 | tf_op jit(solution)/shard_map/dot_general | solution.py:16
  1154.5 26.5 %multiply_reduce_fusion.7 = (f32[1280]{0:T(1024)S(1)}, f32[1028]{0:T(1024)S(1)}, f32[1028]{0:T(1024)S(1)}, f32[1280]{0:T(1024)S(1)}, f32[1028,1280]{1,0:T(8,128)}, /*index=5*/f32[1028,1280]{1,0:T(8,128)}) fusion(f32[1028,1280]{1,0:T(8,128)} %reshape.287, f32[1028]{0:T(1024)S(1)} %copy-done.45, f32[1028]{0:T(1024)S(1)} %copy-done.48, ...), kind=kOutput, calls=%fused_computation.95 | convolution fusion | flops 10128016384 | bytes 49353856 | tf_op jit(solution)/shard_map/dot_general | solution.py:16
  1192.6 23.1 %fusion.33 = f32[1028,1280]{1,0:T(8,128)} fusion(f32[1028,1280]{1,0:T(8,128)S(1)} %bitcast.101, bf16[1028,5120]{1,0:T(8,128)(2,1)} %get-tuple-element.139, bf16[5120,1280]{1,0:T(8,128)(2,1)} %all-gather.11.cloned.1.call-done, f32[1280]{0:T(1024)S(1)} %convert_element_type.244), kind=kOutput, calls=%fused_computation.74 | convolution fusion | flops 13476833280 | bytes 34165760 | tf_op jit(solution)/shard_map/dot_general | solution.py:16
  1215.7 17.7 fusion.32
  1244.8 254.0 %reduce-scatter.9.cloned.1.call-done = f32[80,5120]{1,0:T(8,128)} async-done(((f32[1280,5120]{1,0:T(8,128)}), f32[80,5120]{1,0:T(8,128)}) %reduce-scatter.9.cloned.1.call-update) | async-done | bytes 1638416 | tf_op jit(solution)/shard_map/reduce_scatter | solution.py:271
  1501.2 253.8 %reduce-scatter.11.cloned.1.call-done = f32[320,1280]{1,0:T(8,128)} async-done(((f32[5120,1280]{1,0:T(8,128)}), f32[320,1280]{1,0:T(8,128)}) %reduce-scatter.11.cloned.1.call-update) | async-done | bytes 1638416 | tf_op jit(solution)/shard_map/reduce_scatter | solution.py:272
  1769.9 59.9 %all-reduce.16 = (bf16[2560]{0:T(1024)(128)(2,1)S(1)}, bf16[1280]{0:T(1024)(128)(2,1)S(1)}, bf16[5120]{0:T(1024)(128)(2,1)S(1)}, bf16[1280]{0:T(1024)(128)(2,1)S...) all-reduce(f32[2560]{0:T(1024)S(1)} %maximum_add_fusion, ...), channel_id=6, replica_groups=mesh['dp'=2,'fsdp'=16] {'fsdp'}, use_global_device_ids=true, to_apply=%region_34.0.clone | all-reduce | flops 15360 | bytes 92160
  (393 shorter events, 714.9 us)
Async XLA Ops:
  7.2 142.1 %all-gather.5.cloned.1.call-start = ((), (), s32[]{:S(2)}) async-start(), calls=%async_computation.4 | async-start | bytes 10444800 | tf_op jit(solution)/shard_map/all_gather | solution.py:228
  7.9 403.7 %all-gather.7.cloned.1.call-start = ((), (), s32[]{:S(2)}) async-start(), calls=%async_computation.5 | async-start | bytes 3481600 | tf_op jit(solution)/shard_map/all_gather | solution.py:229
  8.7 422.2 %all-gather.9.cloned.1.call-start = ((), (), s32[]{:S(2)}) async-start(), calls=%async_computation.6 | async-start | bytes 13926400 | tf_op jit(solution)/shard_map/all_gather | solution.py:230
  9.4 485.6 %all-gather.11.cloned.1.call-start = ((), (), s32[]{:S(2)}) async-start(), calls=%async_computation.7 | async-start | bytes 13926400 | tf_op jit(solution)/shard_map/all_gather | solution.py:231
  10.0 1223.4 %reduce-scatter.7.cloned.1.call-start = ((), (), s32[]{:S(2)}) async-start(), calls=%async_computation.9 | async-start | bytes 6963200 | tf_op jit(solution)/shard_map/reduce_scatter | solution.py:270
  108.2 137.9 %copy-start.49 = (f32[1280]{0:T(1024)}, f32[1280]{0:T(1024)S(1)}, u32[]{:S(2)}) copy-start(f32[1280]{0:T(1024)S(1)} %convert_element_type.229) | copy-start | bytes 15364
  108.2 137.8 %copy-start.65 = (f32[1280]{0:T(1024)}, f32[1280]{0:T(1024)S(1)}, u32[]{:S(2)}) copy-start(f32[1280]{0:T(1024)S(1)} %convert_element_type.230) | copy-start | bytes 15364
  108.5 40.8 %copy-start.61 = (f32[1028]{0:T(1024)}, f32[1028]{0:T(1024)S(1)}, u32[]{:S(2)}) copy-start(f32[1028]{0:T(1024)S(1)} %rsqrt.39) | copy-start | bytes 12340
  108.6 40.7 %copy-start.63 = (f32[1028]{0:T(1024)}, f32[1028]{0:T(1024)S(1)}, u32[]{:S(2)}) copy-start(f32[1028]{0:T(1024)S(1)} %div.53) | copy-start | bytes 12340
  133.3 112.8 %copy-start.43 = (f32[1028]{0:T(1024)}, f32[1028]{0:T(1024)S(1)}, u32[]{:S(2)}) copy-start(f32[1028]{0:T(1024)S(1)} %rsqrt.42) | copy-start | bytes 12340
  133.4 112.7 %copy-start.46 = (f32[1028]{0:T(1024)}, f32[1028]{0:T(1024)S(1)}, u32[]{:S(2)}) copy-start(f32[1028]{0:T(1024)S(1)} %div.58) | copy-start | bytes 12340
  230.5 33.9 %copy-start.28 = (f32[4,16,257]{2,1,0:T(8,128)}, f32[4,16,257]{2,1,0:T(8,128)S(1)}, u32[]{:S(2)}) copy-start(f32[4,16,257]{2,1,0:T(8,128)S(1)} %log_add_fusion.1) | copy-start | bytes 197380
  419.0 100.5 %copy-start.17 = (f32[1028]{0:T(1024)}, f32[1028]{0:T(1024)S(1)}, u32[]{:S(2)}) copy-start(f32[1028]{0:T(1024)S(1)} %broadcast_multiply_fusion.11) | copy-start | bytes 12340
  419.8 99.8 %copy-start.20 = (f32[1028]{0:T(1024)}, f32[1028]{0:T(1024)S(1)}, u32[]{:S(2)}) copy-start(f32[1028]{0:T(1024)S(1)} %add_rsqrt_fusion.3) | copy-start | bytes 12340
  430.9 64.1 %copy-start.23 = (bf16[1028,1280]{1,0:T(8,128)(2,1)S(1)}, bf16[1028,1280]{1,0:T(8,128)(2,1)}, u32[]{:S(2)}) copy-start(bf16[1028,1280]{1,0:T(8,128)(2,1)} %reshape.274) | copy-start | bytes 7895044
  543.9 65.7 %copy-start.14 = (bf16[1028,1280]{1,0:T(8,128)(2,1)S(1)}, bf16[1028,1280]{1,0:T(8,128)(2,1)}, u32[]{:S(2)}) copy-start(bf16[1028,1280]{1,0:T(8,128)(2,1)} %reshape.280) | copy-start | bytes 7895044
  543.9 65.7 %copy-start.73 = (bf16[5120,1280]{1,0:T(8,128)(2,1)S(1)}, bf16[5120,1280]{1,0:T(8,128)(2,1)}, u32[]{:S(2)}) copy-start(bf16[5120,1280]{1,0:T(8,128)(2,1)} %all-gather.11.cloned.1.call-done) | copy-start | bytes 39321604
  953.9 288.7 %reduce-scatter.5.cloned.1.call-start = ((), (), s32[]{:S(2)}) async-start(), calls=%async_computation.8 | async-start | bytes 20889600 | tf_op jit(solution)/shard_map/reduce_scatter | solution.py:269
  1011.2 27.6 %copy-start.19 = (f32[1028]{0:T(1024)S(1)}, f32[1028]{0:T(1024)}, u32[]{:S(2)}) copy-start(f32[1028]{0:T(1024)} %copy-done.17) | copy-start | bytes 12340
  1011.2 487.6 %reduce-scatter.9.cloned.1.call-start = ((), (), s32[]{:S(2)}) async-start(), calls=%async_computation.10 | async-start | bytes 27852800 | tf_op jit(solution)/shard_map/reduce_scatter | solution.py:271
  1072.1 682.8 %reduce-scatter.11.cloned.1.call-start = ((), (), s32[]{:S(2)}) async-start(), calls=%async_computation.11 | async-start | bytes 27852800 | tf_op jit(solution)/shard_map/reduce_scatter | solution.py:272
  1125.9 777.2 %all-reduce.22.cloned.1.call-start = ((), (), s32[]{:S(2)}) async-start(), calls=%async_computation.12 | async-start | bytes 4915200 | tf_op jit(solution)/shard_map/psum | solution.py:283
  1185.7 29.9 %slice-start.4 = ((s8[5283840]{0:T(1024)(128)(4,1)}), s8[4194304]{0:T(1024)(128)(4,1)S(1)}, s32[]{:S(2)}) async-start(s8[5283840]{0:T(1024)(128)(4,1)} %bitcast.104), calls=%async_computation.17 | async-start | bytes 8388608
  1185.7 29.9 %slice-start.6 = ((s8[10567680]{0:T(1024)(128)(4,1)}), s8[4194304]{0:T(1024)(128)(4,1)S(1)}, s32[]{:S(2)}) async-start(s8[10567680]{0:T(1024)(128)(4,1)} %bitcast.108), calls=%async_computation.19 | async-start | bytes 8388608
  (78 other events, 904.2 us)
Sparse Core Ops, SparseCore 0:
  10.3 87.5 all-gather.4
  100.2 43.9 all-gather.6
  146.5 102.8 all-gather.8
  251.5 102.1 all-gather.10
  954.0 84.1 reduce-scatter.6
  1042.8 199.7 reduce-scatter.4
  1247.3 251.3 reduce-scatter.8
  1503.5 251.3 reduce-scatter.10
  1758.2 70.4 all-reduce.21
where the time goes:
time: 1930 us; the launch traced here: 1920 us
  matrix products  740 us (38%)
  waiting for transfers between devices  518 us (27%)
  local copies, waits for them, and re-layouts  369 us (19%)
  other arithmetic  140 us (7%)
  blocking collectives  131 us (7%)
  between operations  19.4 us (1%)
    dot_general x24, matrix products, matmul(): return jnp.dot(left, right, preferred_element_type=jnp.float32)  556 us
    reduce_scatter x1, waiting for transfers between devices, on_device(): lax.psum_scatter(totals[2], 'fsdp', scatter_dimension=0, tiled=True)  254 us
    reduce_scatter x1, waiting for transfers between devices, on_device(): lax.psum_scatter(totals[3], 'fsdp', scatter_dimension=0, tiled=True)  254 us
    dot_general x12, matrix products, batched(): return jnp.einsum(form, left, right, preferred_element_type=jnp.float32)  184 us
    unnamed x2, blocking collectives  126 us
    unnamed x221, local copies, waits for them, and re-layouts  49 us
  transfers between devices with their start and end apart: 9, of which 3 were waited for; matrix products, arithmetic and copies ran while one was open for 40% of the time, Pallas kernels for 0%

commit v1 on v0

v1 whole, which is shorter than its diff:
```python
import math

import jax
import jax.numpy as jnp
from jax import lax
from jax.experimental import pallas as pl
from jax.experimental.pallas import tpu as pltpu
from jax.sharding import Mesh
from jax.sharding import PartitionSpec as P

D = 1280
H = 16
HD = 80
FF = 5120
SEQ = 257
SP = 264
GROUP = 8
GW = GROUP * HD
EPS = 1e-06
SCALE = HD ** (-0.5)
NT = (((1,), (1,)), ((), ()))
BF = jnp.bfloat16
F32 = jnp.float32


def dot_nt(left, right):
    return lax.dot_general(left, right, NT, preferred_element_type=F32)


def dot_nn(left, right):
    return jnp.dot(left, right, preferred_element_type=F32)


def pad_rows(rows):
    return jnp.concatenate([rows, jnp.zeros((SP - SEQ, rows.shape[1]), rows.dtype)], 0)


def fold_rows(rows):
    return jnp.sum(rows.reshape(rows.shape[0] // 8, 8, rows.shape[1]), 0)


def standardize(rows):
    centered = rows - jnp.mean(rows, -1, keepdims=True)
    inverse = lax.rsqrt(jnp.mean(centered * centered, -1, keepdims=True) + EPS)
    return centered * inverse, inverse


def norm_gradient(e, xhat, inverse, gain):
    scaled = e * gain
    first = jnp.mean(scaled, -1, keepdims=True)
    second = jnp.mean(scaled * xhat, -1, keepdims=True)
    return inverse * (scaled - first - xhat * second)


def cost(flops, arrays):
    moved = sum(math.prod(a.shape) * a.dtype.itemsize for a in arrays)
    return pl.CostEstimate(flops=int(flops), transcendentals=0, bytes_accessed=moved)


def call(kernel, n, ins, outs, name, flops=0, scratch=(), first=0, alias=None):
    def spec(shape, kind):
        if kind == "raw":
            return pl.BlockSpec(memory_space=pl.ANY)
        if kind == "scalars":
            return pl.BlockSpec(memory_space=pltpu.SMEM)
        if kind == "image":
            return pl.BlockSpec((1,) + tuple(shape[1:]), lambda i: (i + first,) + (0,) * (len(shape) - 1))
        if kind == "whole":
            return pl.BlockSpec(tuple(shape), lambda i: (0,) * len(shape), pipeline_mode=pl.Buffered(1))
        return pl.BlockSpec(tuple(shape), lambda i: (0,) * len(shape))

    return pl.pallas_call(
        kernel,
        grid=(n,),
        in_specs=[spec(a.shape, k) for a, k in ins],
        out_specs=[spec(a.shape, k) for a, k in outs],
        out_shape=[a for a, _ in outs],
        scratch_shapes=list(scratch),
        input_output_aliases=alias or {},
        compiler_params=pltpu.CompilerParams(vmem_limit_bytes=60 << 20),
        cost_estimate=cost(flops, [a for a, _ in ins] + [a for a, _ in outs]),
        name=name,
    )(*[a for a, _ in ins])


def accumulate(ref, value):
    @pl.when(pl.program_id(0) == 0)
    def _():
        ref[...] = jnp.zeros_like(ref)
    ref[...] += value


def prepare_kernel(x_ref, c_ref, gain_ref, shift_ref, normed_ref, cpad_ref, sum_ref):
    xhat, _ = standardize(x_ref[0].astype(F32))
    normed = xhat * gain_ref[...] + shift_ref[...]
    normed_ref[0] = pad_rows(normed).astype(BF)
    c = pad_rows(c_ref[0].astype(F32))
    cpad_ref[0] = c.astype(BF)
    accumulate(sum_ref, fold_rows(c))


def qkv_kernel(w_ref, normed_ref, bias_ref, packed_ref):
    for j in range(packed_ref.shape[2] // D):
        cols = slice(j * D, (j + 1) * D)
        packed_ref[0, :, cols] = (dot_nn(normed_ref[0], w_ref[:, cols]) + bias_ref[:, cols]).astype(BF)


def drop_tail(rows):
    tail = rows[SP - 8:]
    keep = lax.broadcasted_iota(jnp.int32, tail.shape, 0) < SEQ - (SP - 8)
    return jnp.concatenate([rows[:SP - 8], jnp.where(keep, tail, 0.0)], 0)


def attention_kernel(packed_ref, mixed_ref, lse_ref):
    def group(g, carry):
        base = g * GW
        here = pl.ds(pl.multiple_of(base, 128), GW)
        queries, keys, values = [
            packed_ref[0, :, pl.ds(pl.multiple_of(part * D + base, 128), GW)] for part in range(3)]
        values_t = values.astype(F32).T.astype(BF)
        outs, lses = [], []
        for j in range(GROUP):
            head = slice(j * HD, (j + 1) * HD)
            s = dot_nt(keys[:, head], queries[:, head])
            tail = s[SP - 8:]
            keep = lax.broadcasted_iota(jnp.int32, tail.shape, 0) < SEQ - (SP - 8)
            s = jnp.concatenate([s[:SP - 8], jnp.where(keep, tail, -1e30)], 0) * SCALE
            top = jnp.max(s, 0, keepdims=True)
            e = jnp.exp(s - top)
            total = jnp.sum(e, 0, keepdims=True)
            o = dot_nn(values_t[head], e.astype(BF)) * (1.0 / total)
            outs.append(o)
            lses.append(top + jnp.log(total))
        mixed_ref[0, :, pl.ds(pl.multiple_of(base, 128), GW)] = jnp.concatenate(outs, 0).T.astype(BF)
        lse_ref[0, pl.ds(pl.multiple_of(g * GROUP, 8), GROUP), :] = jnp.concatenate(lses, 0)
        return carry
    lax.fori_loop(0, H // GROUP, group, 0)


def out_kernel(w_ref, x_ref, mixed_ref, bias_ref, gain_ref, shift_ref, hidden_ref, normed_ref):
    hidden = pad_rows(x_ref[0].astype(F32)) + dot_nn(mixed_ref[0], w_ref[...]) + bias_ref[...]
    hidden_ref[0] = hidden
    xhat, _ = standardize(hidden)
    normed = xhat * gain_ref[...] + shift_ref[...]
    keep = lax.broadcasted_iota(jnp.int32, normed.shape, 0) < SEQ
    normed_ref[0] = jnp.where(keep, normed, 0.0).astype(BF)


CHUNK = 512


def up_kernel(w_ref, normed_ref, bias_ref, active_ref, slope_ref):
    normed = normed_ref[0]

    def step(j, carry):
        cols = pl.ds(pl.multiple_of(j * CHUNK, CHUNK), CHUNK)
        u = dot_nn(normed, w_ref[:, cols]) + bias_ref[:, cols]
        cdf = 0.5 * (1.0 + lax.erf(u * 0.7071067811865476))
        active_ref[0, :, cols] = (u * cdf).astype(BF)
        slope_ref[0, :, cols] = (cdf + u * jnp.exp(-0.5 * u * u) * 0.3989422804014327).astype(BF)
        return carry
    lax.fori_loop(0, FF // CHUNK, step, 0)


def down_kernel(w_ref, active_ref, hidden_ref, bias_ref, result_ref):
    result = hidden_ref[0] + dot_nn(active_ref[0], w_ref[...]) + bias_ref[...]
    result_ref[0] = result[:SEQ]


def down_back_kernel(w_ref, c_ref, slope_ref, dinner_ref, sum_ref):
    c = c_ref[0]

    @pl.when(pl.program_id(0) == 0)
    def _():
        sum_ref[...] = jnp.zeros_like(sum_ref)

    def step(j, carry):
        rows = pl.ds(pl.multiple_of(j * CHUNK, CHUNK), CHUNK)
        d = dot_nt(c, w_ref[rows, :]) * slope_ref[0, :, rows].astype(F32)
        dinner_ref[0, :, rows] = d.astype(BF)
        sum_ref[:, rows] += fold_rows(d)
        return carry
    lax.fori_loop(0, FF // CHUNK, step, 0)


def up_back_kernel(w_up_ref, w_out_ref, dinner_ref, hidden_ref, c_ref, gain_ref,
                   dhidden_ref, dhidden_b_ref, dmixed_ref, sum_gain_ref, sum_shift_ref, sum_out_ref):
    e = dot_nt(dinner_ref[0], w_up_ref[...])
    xhat, inverse = standardize(hidden_ref[0])
    dhidden = c_ref[0].astype(F32) + norm_gradient(e, xhat, inverse, gain_ref[...])
    dhidden_ref[0] = dhidden
    dhidden_b = dhidden.astype(BF)
    dhidden_b_ref[0] = dhidden_b
    dmixed_ref[0] = dot_nt(dhidden_b, w_out_ref[...]).astype(BF)
    accumulate(sum_gain_ref, fold_rows(e * xhat))
    accumulate(sum_shift_ref, fold_rows(e))
    accumulate(sum_out_ref, fold_rows(dhidden))


def attention_back_kernel(packed_ref, mixed_ref, dmixed_ref, lse_ref, dpacked_ref, sum_ref):
    @pl.when(pl.program_id(0) == 0)
    def _():
        sum_ref[...] = jnp.zeros_like(sum_ref)

    def group(g, carry):
        base = g * GW
        here = pl.ds(pl.multiple_of(base, 128), GW)
        queries, keys, values = [
            packed_ref[0, :, pl.ds(pl.multiple_of(part * D + base, 128), GW)] for part in range(3)]
        grads = dmixed_ref[0, :, here]
        product = (grads.astype(F32) * mixed_ref[0, :, here].astype(F32)).T
        keys_t = keys.astype(F32).T.astype(BF)
        lse = lse_ref[0, pl.ds(pl.multiple_of(g * GROUP, 8), GROUP), :]
        dq, dk, dv = [], [], []
        for j in range(GROUP):
            head = slice(j * HD, (j + 1) * HD)
            q, k, v, dm = queries[:, head], keys[:, head], values[:, head], grads[:, head]
            delta = jnp.sum(product[head], 0, keepdims=True)
            p = drop_tail(jnp.exp(dot_nt(k, q) * SCALE - lse[j:j + 1]))
            dv.append(dot_nn(p.astype(BF), dm))
            ds = (p * (dot_nt(v, dm) - delta) * SCALE).astype(BF)
            dk.append(dot_nn(ds, q))
            dq.append(dot_nn(keys_t[head], ds))
        dq = jnp.concatenate(dq, 0).T
        dk = jnp.concatenate(dk, 1)
        dv = jnp.concatenate(dv, 1)
        def out(part):
            return pl.ds(pl.multiple_of(part * D + base, 128), GW)
        keep = lax.broadcasted_iota(jnp.int32, dq.shape, 0) < SEQ
        dq = jnp.where(keep, dq, 0.0)
        dpacked_ref[0, :, out(0)] = dq.astype(BF)
        dpacked_ref[0, :, out(1)] = dk.astype(BF)
        dpacked_ref[0, :, out(2)] = dv.astype(BF)
        sum_ref[:, out(0)] += fold_rows(dq)
        sum_ref[:, out(1)] += fold_rows(dv)
        return carry
    lax.fori_loop(0, H // GROUP, group, 0)


def qkv_back_kernel(w_ref, dpacked_ref, x_ref, dhidden_ref, gain_ref, *refs):
    dimages_ref, sum_gain_ref, sum_shift_ref = refs[-3:]
    e = dot_nt(dpacked_ref[0], w_ref[...])[:SEQ]
    xhat, inverse = standardize(x_ref[0].astype(F32))
    dimages_ref[0] = dhidden_ref[0, :SEQ] + norm_gradient(e, xhat, inverse, gain_ref[...])
    accumulate(sum_gain_ref, fold_rows(pad_rows(e * xhat)))
    accumulate(sum_shift_ref, fold_rows(pad_rows(e)))


def sds(*shape, dtype=BF):
    return jax.ShapeDtypeStruct(shape, dtype)


def weighted(kernel, plans):
    total = sum(len(plan) for plan in plans)

    def run(*refs):
        pieces, rest = refs[:total], refs[total:]
        places, rest = rest[:len(plans)], rest[len(plans):]
        own, scratch = rest[:len(rest) - 2 * len(plans)], rest[len(rest) - 2 * len(plans):]
        weights, sems = scratch[0::2], scratch[1::2]

        @pl.when(pl.program_id(0) == 0)
        def _():
            copies, first = [], 0
            for plan, place, weight, sem in zip(plans, places, weights, sems):
                n = 0
                for count, there, here, width in plan:
                    rows = pieces[first].shape[1]
                    for k in range(count):
                        at = pl.ds(pl.multiple_of(place[0, n] * rows, 16), rows)
                        cols = pl.ds(pl.multiple_of(here + place[1, n] * width, 128), width)
                        copies.append(pltpu.make_async_copy(
                            pieces[first].at[k, :, there:there + width], weight.at[at, cols], sem.at[n]))
                        n += 1
                    first += 1
            for copy in copies:
                copy.start()
            for copy in copies:
                copy.wait()
        kernel(*weights, *own)
    return run


def weight_call(kernel, n, weights, ins, outs, name, flops, **more):
    plans = [[(a.shape[0], there, here, columns) for a, _, there, here, columns in w] for _, w in weights]
    operands = [(piece[0], "raw") for _, w in weights for piece in w]
    operands += [(jnp.concatenate([piece[1] for piece in w], 1), "scalars") for _, w in weights] + list(ins)
    scratch = []
    for width, w in weights:
        rows = sum(a.shape[0] * a.shape[1] * columns for a, _, _, _, columns in w) // width
        scratch.append(pltpu.VMEM((rows, width), BF))
        scratch.append(pltpu.SemaphoreType.DMA((sum(piece[0].shape[0] for piece in w),)))
    if "alias" in more:
        more["alias"] = {len(operands) - len(ins) + k: v for k, v in more["alias"].items()}
    return call(weighted(kernel, plans), n, operands, outs, name, flops * n * SP, scratch, **more)


def gradient_kernel(rows, steps, relative, spots, place_ref, l_ref, r_ref, *rest):
    outs, stage, sems = rest[:spots], rest[spots], rest[spots + 1]
    i, j = pl.program_id(0), pl.program_id(1)
    step = i * pl.num_programs(1) + j
    block, width = stage.shape[1], stage.shape[2]
    per = block // rows

    def copy(slot, t, out, at, cols):
        return pltpu.make_async_copy(stage.at[slot, t * rows:(t + 1) * rows, :], out.at[at, :, cols], sems.at[slot, t])

    def drain(slot):
        for t in range(per):
            copy(slot, t, outs[0], 0, pl.ds(0, width)).wait()

    slot = lax.rem(step, 2)

    @pl.when(step >= 2)
    def _():
        drain(slot)
    stage[slot] = lax.dot_general(l_ref[...], r_ref[...], (((0,), (0,)), ((), ())), preferred_element_type=F32).astype(BF)
    cols = pl.ds(pl.multiple_of(j * width, 128), width)
    for t in range(per):
        owner = i * per + t
        if not relative:
            copy(slot, t, outs[0], owner, cols).start()
            continue
        core = lax.rem(owner, 2) ^ place_ref[1]
        x = lax.rem(owner // 2, 2) ^ place_ref[0]
        z = owner // 4

        @pl.when(core == 1)
        def _():
            copy(slot, t, outs[0], x * (outs[0].shape[0] // 2) + z, cols).start()

        @pl.when(jnp.logical_and(core == 0, x == 0))
        def _():
            copy(slot, t, outs[1], z, cols).start()

        @pl.when(jnp.logical_and(core == 0, x == 1))
        def _():
            copy(slot, t, outs[2], z, cols).start()

    @pl.when(step == steps - 1)
    def _():
        drain(slot)
        if steps > 1:
            drain(1 - slot)


def weight_gradient(left, right, owners, place, relative, name, first=0, width=None):
    depth = left.shape[0] * left.shape[1]
    left, right = left.reshape(depth, -1), right.reshape(depth, -1)
    block, cols, width = 640, 1280, width or right.shape[1]
    if not relative:
        owners = left.shape[1] // block
    rows = left.shape[1] // owners
    steps = (left.shape[1] // block) * (width // cols)
    if relative:
        shapes = [sds(owners // 2, rows, width), sds(owners // 4, rows, width), sds(owners // 4, rows, width)]
    else:
        shapes = [sds(owners, rows, width)]

    def kernel(*refs):
        gradient_kernel(rows, steps, relative, len(shapes), *refs)

    return pl.pallas_call(
        kernel,
        grid=(left.shape[1] // block, width // cols),
        in_specs=[
            pl.BlockSpec(memory_space=pltpu.SMEM),
            pl.BlockSpec((depth, block), lambda i, j: (0, i)),
            pl.BlockSpec((depth, cols), lambda i, j: (0, j + first // cols)),
        ],
        out_specs=[pl.BlockSpec(memory_space=pl.ANY)] * len(shapes),
        out_shape=shapes,
        scratch_shapes=[pltpu.VMEM((2, block, cols), BF), pltpu.SemaphoreType.DMA((2, block // rows))],
        compiler_params=pltpu.CompilerParams(vmem_limit_bytes=60 << 20),
        cost_estimate=cost(2.5 * depth * left.shape[1] * width, [left, right] + shapes),
        name=name,
    )(place, left, right)


SWAP = [(0, 1), (1, 0)]


def row(vector):
    return vector.reshape(1, -1).astype(F32)


def after(value, *others):
    return lax.optimization_barrier((value, others))[0]


def both_groups(shard):
    if lax.axis_size("dp") != 2:
        return lax.psum(shard, "dp").astype(F32)
    return shard.astype(F32) + lax.ppermute(shard, "dp", SWAP).astype(F32)


class Whole:
    def __init__(self, owners):
        self.owners, self.mine, self.relative = owners, jnp.zeros((2,), jnp.int32), False

    def gather_small(self, vector):
        return lax.all_gather(vector.reshape(1, -1), "fsdp", axis=0, tiled=True)

    def gather(self, w):
        return [(lax.all_gather(w, "fsdp", axis=0, tiled=True)[None], jnp.zeros((2, 1), jnp.int32))]

    def first_stage(self, parts, *before):
        return parts

    def second_stage(self, parts, *before):
        return parts

    def third_stage(self, parts):
        whole = parts[0].reshape(-1, parts[0].shape[2])
        return lax.psum_scatter(whole, "fsdp", scatter_dimension=0, tiled=True)

    def scatter_small(self, shares):
        return lax.psum(lax.psum_scatter(shares, "fsdp", scatter_dimension=0, tiled=True)[0], "dp")


class Split:
    relative = True

    def __init__(self, owners):
        self.owners, self.count = owners, owners // 4
        self.mine = jnp.stack([lax.axis_index("x"), lax.axis_index("core")]).astype(jnp.int32)
        self.z = jnp.arange(self.count, dtype=jnp.int32)

    def gather(self, w):
        return [(lax.all_gather(w, ("z", "x", "core"), axis=0, tiled=True)[None], jnp.zeros((2, 1), jnp.int32))]

    def gather_small(self, vector):
        rows = vector.reshape(1, -1)

        def double(rows, axis, step, other):
            got = lax.ppermute(rows, axis, other)
            low = lax.rem(lax.axis_index(axis) // step, 2) == 0
            return jnp.concatenate([jnp.where(low, rows, got), jnp.where(low, got, rows)], 0)
        rows = double(rows, "core", 1, SWAP)
        rows = double(rows, "x", 1, SWAP)
        step = 1
        while step < self.count:
            rows = double(rows, "z", step, [(i, i ^ step) for i in range(self.count)])
            step *= 2
        return rows

    def first_stage(self, parts, *before):
        send, keep, pass_on = parts
        half = send.shape[0] // 2
        got = lax.ppermute(send, "core", SWAP)
        return after(pass_on, *before) + got[half:], keep, got

    def second_stage(self, parts, *before):
        passed, keep, got = parts
        half, keep = got.shape[0] // 2, after(keep, *before)
        got_x = lax.ppermute(passed, "x", SWAP)
        return (keep.astype(F32) + got[:half].astype(F32) + got_x.astype(F32)).astype(BF)

    def third_stage(self, total):
        return lax.psum_scatter(total, "z", scatter_dimension=0, tiled=True)[0]

    def scatter_small(self, shares):
        shares = shares.reshape(self.count, 2, 2, -1)

        def halve(rows, axis, here):
            kept = lax.dynamic_index_in_dim(rows, here, axis, keepdims=False)
            return kept, lax.dynamic_index_in_dim(rows, 1 - here, axis, keepdims=False)
        kept, sent = halve(shares, 2, self.mine[1])
        shares = kept + lax.ppermute(sent, "core", SWAP)
        kept, sent = halve(shares, 1, self.mine[0])
        shares = kept + lax.ppermute(sent, "x", SWAP)
        step = self.count // 2
        while step:
            shares = shares.reshape(2, step, -1)
            kept, sent = halve(shares, 0, lax.rem(lax.axis_index("z") // step, 2))
            shares = kept + lax.ppermute(sent, "z", [(i, i ^ step) for i in range(self.count)])
            step //= 2
        shares = shares.reshape(-1)
        if lax.axis_size("dp") != 2:
            return lax.psum(shares, "dp")
        return shares + lax.ppermute(shares, "dp", SWAP)


def row(vector):
    return vector.reshape(1, -1).astype(F32)


def columns(pieces, there, here, width):
    return [(a, places, there, here, width) for a, places in pieces]


def layer(links, images, cotangent, w_qkv, w_out, w_up, w_down, *vectors):
    n, owners = images.shape[0], links.owners

    sizes = [v.shape[0] for v in vectors]
    small = links.gather_small(jnp.concatenate(vectors))
    whole, first = [], 0
    for size in sizes:
        whole.append(row(small[:, first:first + size]))
        first += size
    b_qv, b_out, b_up, b_down, gain_one, shift_one, gain_two, shift_two = whole

    def image(a):
        return (a, "image")

    def fixed(a):
        return (a, "whole")

    def rows(*shape, dtype=BF):
        return (sds(n, *shape, dtype=dtype), "image")

    def sums(width):
        return (sds(8, width, dtype=F32), "sum")

    def gradient(left, right, name, first=0, width=None):
        return weight_gradient(left, right, owners, links.mine, links.relative, name, first, width)

    g_qkv = links.gather(w_qkv)
    full_qkv = columns(g_qkv, 0, 0, 3 * D)
    normed_one, cpad, s_down = call(
        prepare_kernel, n, [image(images), image(cotangent), fixed(gain_one), fixed(shift_one)],
        [rows(SP, D), rows(SP, D), sums(D)], "prepare", 8 * n * SP * D * 50)
    g_middle = links.gather(after(jnp.concatenate([w_out, w_up], 1), normed_one))
    full_out, full_up = columns(g_middle, 0, 0, D), columns(g_middle, D, 0, FF)
    bias = jnp.concatenate([b_qv[:, :D], jnp.zeros((1, D), F32), b_qv[:, D:]], 1)
    packed, = weight_call(
        qkv_kernel, n, [(3 * D, full_qkv)], [image(normed_one), fixed(bias)], [rows(SP, 3 * D)], "qkv", 2.5 * D * 3 * D)
    full_down = columns(links.gather(after(w_down, packed)), 0, 0, D)
    mixed, logsum = call(
        attention_kernel, n, [image(packed)], [rows(SP, D), rows(H, SP, dtype=F32)], "attention", 1e5 * n * SP * H)
    hidden, normed_two = weight_call(
        out_kernel, n, [(D, full_out)],
        [image(images), image(mixed), fixed(b_out), fixed(gain_two), fixed(shift_two)],
        [rows(SP, D, dtype=F32), rows(SP, D)], "out", 3 * D * D)
    active, slope = weight_call(
        up_kernel, n, [(FF, full_up)], [image(normed_two), fixed(b_up)], [rows(SP, FF), rows(SP, FF)], "up", 4 * D * FF)

    p_down = gradient(active, cpad, "g_down")
    result, = weight_call(
        down_kernel, n, [(D, full_down)],
        [image(after(active, p_down)), image(hidden), fixed(b_down)], [rows(SEQ, D, dtype=F32)], "down", 2.5 * D * FF)
    p_down = links.first_stage(p_down, result)
    d_inner, s_up = weight_call(
        down_back_kernel, n, [(D, full_down)], [image(after(cpad, result, p_down[0])), image(slope)],
        [rows(SP, FF), sums(FF)], "down_back", 3 * D * FF)
    p_up = gradient(normed_two, d_inner, "g_up_low", 0, FF // 2)
    p_up2 = gradient(normed_two, after(d_inner, p_up), "g_up_high", FF // 2, FF // 2)
    p_up = links.first_stage(p_up, p_up2)
    p_down = links.second_stage(p_down, p_up2)
    d_hidden, d_hidden_b, d_mixed, s_gain_two, s_shift_two, s_out = weight_call(
        up_back_kernel, n, [(FF, full_up), (D, full_out)],
        [image(after(d_inner, p_up2, p_up[0], p_down)), image(hidden), image(cpad), fixed(gain_two)],
        [rows(SP, D, dtype=F32), rows(SP, D), rows(SP, D), sums(D), sums(D), sums(D)], "up_back", 3 * D * (D + FF))
    p_down = links.third_stage(p_down)
    p_up2 = links.first_stage(p_up2, d_hidden_b)
    p_up = links.second_stage(p_up, d_hidden_b)
    p_out = gradient(mixed, after(d_hidden_b, p_up2[0], p_up, p_down), "g_out")
    p_up = links.third_stage(p_up)
    d_packed, s_qv = call(
        attention_back_kernel, n, [image(packed), image(mixed), image(after(d_mixed, p_out)), image(logsum)],
        [rows(SP, 3 * D), sums(2 * D)], "attention_back", 1.4e5 * n * SP * H)
    g_down = both_groups(after(p_down, d_packed))
    p_out = links.first_stage(p_out, d_packed)
    p_up2 = links.second_stage(p_up2, d_packed)
    p_q = gradient(normed_one, after(d_packed, p_out[0], p_up2, p_up), "g_q", 0, D)
    p_up2 = links.third_stage(p_up2)
    p_k = gradient(normed_one, after(d_packed, p_q), "g_k", D, D)
    p_q = links.first_stage(p_q, p_k)
    p_v = gradient(normed_one, after(d_packed, p_k, p_q[0]), "g_v", 2 * D, D)
    p_k = links.first_stage(p_k, p_v)
    p_out = links.second_stage(p_out, p_v)

    def qkv_back(first, d_packed, more):
        return weight_call(
            qkv_back_kernel, n // 2, [(3 * D, full_qkv)],
            [image(d_packed), image(images), image(d_hidden), fixed(gain_one)] + [(a, "raw") for a in more],
            [rows(SEQ, D, dtype=F32), sums(D), sums(D)], "qkv_back", 3 * D * 3 * D,
            first=first, alias={4: 0} if more else {})
    d_images, s_gain_one, s_shift_one = qkv_back(0, after(d_packed, p_v, p_k[0], p_out), ())
    g_up = both_groups(after(p_up, d_images))
    p_v = links.first_stage(p_v, d_images)
    p_q = links.second_stage(p_q, d_images)
    p_out = links.third_stage(after(p_out, p_up2, d_images))
    d_images, more_gain, more_shift = qkv_back(n // 2, after(d_packed, p_v[0], p_q, p_up2), (d_images,))
    p_q = links.third_stage(p_q)
    p_k = links.third_stage(links.second_stage(p_k, d_images))
    p_v = links.third_stage(links.second_stage(p_v, d_images))
    s_gain_one, s_shift_one = s_gain_one + more_gain, s_shift_one + more_shift
    g_up2, g_out, g_q, g_k, g_v = [both_groups(after(p, d_images)) for p in (p_up2, p_out, p_q, p_k, p_v)]
    g_up = jnp.concatenate([g_up, g_up2], 1)

    parts = [s_qv, s_out, s_up, s_down, s_gain_one, s_shift_one, s_gain_two, s_shift_two]
    share = links.scatter_small(jnp.concatenate([jnp.sum(s, 0).reshape(owners, -1) for s in parts], 1))
    small_grads, first = [], 0
    for size in sizes:
        small_grads.append(share[first:first + size])
        first += size
    return (result, d_images, jnp.concatenate([g_q, g_k, g_v], 1), g_out, g_up, g_down, *small_grads)


def solution(mesh):
    dp, owners = mesh.shape["dp"], mesh.shape["fsdp"]
    kind, fsdp = Whole, ("fsdp",)
    if dp == 2 and owners % 4 == 0 and (D // owners) % 16 == 0:
        kind, fsdp = Split, ("z", "x", "core")
        mesh = Mesh(mesh.devices.reshape(dp, owners // 4, 2, 2), ("dp",) + fsdp)
    images, matrix, vector = P(("dp",) + fsdp, None, None), P(fsdp, None), P(fsdp)
    specs = (images,) * 2 + (matrix,) * 4 + (vector,) * 8

    def run(*args):
        return layer(kind(owners), *args)

    return jax.shard_map(run, mesh=mesh, in_specs=specs, out_specs=specs, check_vma=False)
```

time: 1930 us -> 867 us (0.45)
  matrix products: 740 us -> 0 us
  Pallas kernels: 0 us -> 568 us
  waiting for transfers between devices: 518 us -> 137 us
  local copies, waits for them, and re-layouts: 369 us -> 46.5 us
  blocking collectives: 131 us -> 0 us
  other arithmetic: 140 us -> 63.3 us
  starting transfers between devices: 0.36 us -> 31 us
    dot_general x36 -> x0, matrix products: 740 us -> none  [the longest x24 556 us: matmul(): return jnp.dot(left, right, preferred_element_type=jnp.float32)]
    pallas_call x0 -> x18, Pallas kernels: none -> 568 us  [the longest x11 436 us: call(): pl.pallas_call(kernel, grid=(n,), in_specs=[spec(a.shape, k) for a, k in...]
    reduce_scatter x4 -> x7, waiting for transfers between devices: 515 us -> 14.6 us  [third_stage(): return lax.psum_scatter(total, 'z', scatter_dimension=0, tiled=True)[0]]
    reshape x30 -> x2, local copies, waits for them, and re-layouts: 216 us -> 0.03 us  [the longest x1 0.02 us: scatter_small(): shares = shares.reshape(2, step, -1)]
    unnamed x2 -> x0, blocking collectives: 126 us -> none
    all_gather x4 -> x3, waiting for transfers between devices: 0.05 us -> 88.6 us  [gather(): lax.all_gather(w, ('z', 'x', 'core'), axis=0, tiled=True)[None]]
    reduce_sum x14 -> x7, other arithmetic: 79.6 us -> 4.09 us  [layer(): jnp.sum(s, 0).reshape(owners, -1)]
    convert_element_type x6 -> x8, local copies, waits for them, and re-layouts: 38.6 us -> 4.83 us  [row(): return vector.reshape(1, -1).astype(F32)]
  transfers between devices with their start and end apart: 9 -> 40, of which waited for: 3 -> 13; matrix products, arithmetic and copies ran while one was open for 40% -> 12% of each run, Pallas kernels for 0% -> 64%
where the time goes in v1:
time: 867 us; the launch traced here: 861 us
  Pallas kernels  568 us (66%)
  waiting for transfers between devices  137 us (16%)
  other arithmetic  63.3 us (7%)
  local copies, waits for them, and re-layouts  46.5 us (5%)
  starting transfers between devices  31 us (4%)
  between operations  15.3 us (2%)
    pallas_call x11, Pallas kernels, call(): pl.pallas_call(kernel, grid=(n,), in_specs=[spec(a.shape, k) for a, k in...  436 us
    pallas_call x7, Pallas kernels, weight_gradient(): pl.pallas_call(kernel, grid=(left.shape[1] // block, width // cols), in_s...  132 us
    all_gather x3, waiting for transfers between devices, gather(): lax.all_gather(w, ('z', 'x', 'core'), axis=0, tiled=True)[None]  88.6 us
    unnamed x30, local copies, waits for them, and re-layouts  32.8 us
    convert_element_type x7, other arithmetic, second_stage(): (keep.astype(F32) + got[:half].astype(F32) + got_x.astype(F32)).astype(BF)  24.8 us
    add x7, other arithmetic, first_stage(): return (after(pass_on, *before) + got[half:], keep, got)  19.4 us
  transfers between devices with their start and end apart: 40, of which 13 were waited for; matrix products, arithmetic and copies ran while one was open for 12% of the time, Pallas kernels for 64%

profile of v1, /device:TPU:0, one launch (start us, length us, event | category | flops | bytes accessed | tf_op | source)
XLA Modules:
  0.0 860.8 jit_solution(8819031366723737128)
XLA Ops:
  39.5 12.5 %prepare.1 = (bf16[8,264,1280]{2,1,0:T(8,128)(2,1)}, bf16[8,264,1280]{2,1,0:T(8,128)(2,1)}, f32[8,1280]{1,0:T(8,128)}) custom-call(bf16[8,257,1280]{2,1,0:T(8,128)(2,1)} %copy.29.x_ref.refs_2_.refs_3_, bf16[8,257,1280]{2,1,0:T(8,128)(2,1)} %copy.30.c_ref, f32[1,1280]{1,0:T(1,128)} %reshape.237.gain_ref.refs_5_, f32[1,1280]{1,0:T(1,128)} %reshape.238.shift_ref), custom_call_target="tpu_custom_call" | custom-call | flops 1081344000 | bytes 21391360 | tf_op jit(solution)/shard_map/prepare/pallas_call | solution.py:72
  52.9 44.6 %all-gather.4.cloned.1.call-done = bf16[1280,3840]{1,0:T(8,128)(2,1)} async-done(((bf16[80,3840]{1,0:T(8,128)(2,1)}), bf16[1280,3840]{1,0:T(8,128)(2,1)}) %all-gather.4.cloned.1.call-update) | async-done | bytes 9830416 | tf_op jit(solution)/shard_map/all_gather | solution.py:430
  98.1 29.6 %qkv.1.packed_ref = bf16[8,264,3840]{2,1,0:T(8,128)(2,1)} custom-call(bf16[1,1280,3840]{2,1,0:T(8,128)(2,1)} %bitcast.66, s32[2,1]{1,0:T(2,128)} %broadcast_1_refs_1__refs_2__refs_3_.2.refs_1_.refs_2_.refs_3_, bf16[8,264,1280]{2,1,0:T(8,128)(2,1)} %get-tuple-element.95.refs_2_, f32[1,3840]{1,0:T(1,128)} %fusion.refs_3_), custom_call_target="tpu_custom_call" | custom-call | flops 25952256000 | bytes 31472648 | tf_op jit(solution)/shard_map/qkv/pallas_call | solution.py:72
  131.4 48.0 %attention.1 = (bf16[8,264,1280]{2,1,0:T(8,128)(2,1)}, f32[8,16,264]{2,1,0:T(8,128)}) custom-call(bf16[8,264,3840]{2,1,0:T(8,128)(2,1)} %qkv.1.packed_ref), custom_call_target="tpu_custom_call" | custom-call | flops 3379200000 | bytes 21762048 | tf_op jit(solution)/shard_map/attention/pallas_call | solution.py:72
  179.4 44.0 %all-gather.8.cloned.1.call-done = bf16[1280,6400]{1,0:T(8,128)(2,1)} async-done(((bf16[80,6400]{1,0:T(8,128)(2,1)}), bf16[1280,6400]{1,0:T(8,128)(2,1)}) %all-gather.8.cloned.1.call-update) | async-done | bytes 16384016 | tf_op jit(solution)/shard_map/all_gather | solution.py:430
  223.4 16.9 %out.1 = (f32[8,264,1280]{2,1,0:T(8,128)}, bf16[8,264,1280]{2,1,0:T(8,128)(2,1)}) custom-call(bf16[1,1280,6400]{2,1,0:T(8,128)(2,1)} %bitcast.57, s32[2,1]{1,0:T(2,128)} %broadcast_1_refs_1__refs_2__refs_3_.2.refs_1_.refs_2_.refs_3_, bf16[8,257,1280]{2,1,0:T(8,128)(2,1)} %copy.29.x_ref.refs_2_.refs_3_, ...), custom_call_target="tpu_custom_call" | custom-call | flops 10380902400 | bytes 43289608 | tf_op jit(solution)/shard_map/out/pallas_call | solution.py:72
  240.3 66.7 %up.1 = (bf16[8,264,5120]{2,1,0:T(8,128)(2,1)}, bf16[8,264,5120]{2,1,0:T(8,128)(2,1)}) custom-call(bf16[1,1280,6400]{2,1,0:T(8,128)(2,1)} %bitcast.58, s32[2,1]{1,0:T(2,128)} %broadcast_1_refs_1__refs_2__refs_3_.2.refs_1_.refs_2_.refs_3_, bf16[8,264,1280]{2,1,0:T(8,128)(2,1)} %get-tuple-element.99.refs_2_, f32[1,5120]{1,0:T(1,128)} %reshape.243.refs_3_), custom_call_target="tpu_custom_call" | custom-call | flops 55364812800 | bytes 65064968 | tf_op jit(solution)/shard_map/up/pallas_call | solution.py:72
  307.0 37.0 %g_down.1 = (bf16[8,320,1280]{2,1,0:T(8,128)(2,1)}, bf16[4,320,1280]{2,1,0:T(8,128)(2,1)}, bf16[4,320,1280]{2,1,0:T(8,128)(2,1)}) custom-call(s32[2]{0:T(128)} %pad_add_fusion.refs_0_, bf16[2112,5120]{1,0:T(8,128)(2,1)} %bitcast.75, bf16[2112,1280]{1,0:T(8,128)(2,1)} %bitcast.72), custom_call_target="tpu_custom_call" | custom-call | flops 34603008000 | bytes 40140800 | tf_op jit(solution)/shard_map/g_down/pallas_call | solution.py:363
  345.0 39.2 %down.1 = f32[8,257,1280]{2,1,0:T(8,128)} custom-call(bf16[1,5120,1280]{2,1,0:T(8,128)(2,1)} %bitcast.64, s32[2,1]{1,0:T(2,128)} %broadcast_1_refs_1__refs_2__refs_3_.2.refs_1_.refs_2_.refs_3_, bf16[8,264,5120]{2,1,0:T(8,128)(2,1)} %get-tuple-element.105.refs_2_, f32[8,264,1280]{2,1,0:T(8,128)} %get-tuple-element.106.refs_3_.refs_5_, f32[1,1280]{1,0:T(1,128)} %reshape.244.refs_4_), custom_call_target="tpu_custom_call" | custom-call | flops 34603008000 | bytes 56079368 | tf_op jit(solution)/shard_map/down/pallas_call | solution.py:72
  388.9 54.4 %down_back.1 = (bf16[8,264,5120]{2,1,0:T(8,128)(2,1)}, f32[8,5120]{1,0:T(8,128)}) custom-call(bf16[1,5120,1280]{2,1,0:T(8,128)(2,1)} %bitcast.65, s32[2,1]{1,0:T(2,128)} %broadcast_1_refs_1__refs_2__refs_3_.2.refs_1_.refs_2_.refs_3_, bf16[8,264,1280]{2,1,0:T(8,128)(2,1)} %get-tuple-element.108.refs_2_.refs_6_, bf16[8,264,5120]{2,1,0:T(8,128)(2,1)} %get-tuple-element.109.refs_3_), custom_call_target="tpu_custom_call" | custom-call | flops 41523609600 | bytes 61931528 | tf_op jit(solution)/shard_map/down_back/pallas_call | solution.py:72
  443.3 21.7 %g_up_low.1 = (bf16[8,80,2560]{2,1,0:T(8,128)(2,1)}, bf16[4,80,2560]{2,1,0:T(8,128)(2,1)}, bf16[4,80,2560]{2,1,0:T(8,128)(2,1)}) custom-call(s32[2]{0:T(128)} %pad_add_fusion.refs_0_, bf16[2112,1280]{1,0:T(8,128)(2,1)} %bitcast.76, bf16[2112,5120]{1,0:T(8,128)(2,1)} %bitcast.73), custom_call_target="tpu_custom_call" | custom-call | flops 17301504000 | bytes 33587200 | tf_op jit(solution)/shard_map/g_up_low/pallas_call | solution.py:363
  465.0 21.3 %g_up_high.1 = (bf16[8,80,2560]{2,1,0:T(8,128)(2,1)}, bf16[4,80,2560]{2,1,0:T(8,128)(2,1)}, bf16[4,80,2560]{2,1,0:T(8,128)(2,1)}) custom-call(s32[2]{0:T(128)} %pad_add_fusion.refs_0_, bf16[2112,1280]{1,0:T(8,128)(2,1)} %bitcast.77, bf16[2112,5120]{1,0:T(8,128)(2,1)} %bitcast.74), custom_call_target="tpu_custom_call" | custom-call | flops 17301504000 | bytes 33587200 | tf_op jit(solution)/shard_map/g_up_high/pallas_call | solution.py:363
  498.3 63.0 %up_back.1 = (f32[8,264,1280]{2,1,0:T(8,128)}, bf16[8,264,1280]{2,1,0:T(8,128)(2,1)}, bf16[8,264,1280]{2,1,0:T(8,128)(2,1)}, f32[8,1280]{1,0:T(8,128)}, f32[8,1280]{1,0:T(8,128)}, /*index=5*/f32[8,1280]{1,0:T(8,128)}) custom-call(bf16[1,1280,6400]{2,1,0:T(8,128)(2,1)} %bitcast.59, bf16[1,1280,6400]{2,1,0:T(8,128)(2,1)} %bitcast.60, ...), custom_call_target="tpu_custom_call" | custom-call | flops 51904512000 | bytes 92369936 | tf_op jit(solution)/shard_map/up_back/pallas_call | solution.py:72
  569.2 13.2 %g_out.1 = (bf16[8,80,1280]{2,1,0:T(8,128)(2,1)}, bf16[4,80,1280]{2,1,0:T(8,128)(2,1)}, bf16[4,80,1280]{2,1,0:T(8,128)(2,1)}) custom-call(s32[2]{0:T(128)} %pad_add_fusion.refs_0_, bf16[2112,1280]{1,0:T(8,128)(2,1)} %bitcast.38, bf16[2112,1280]{1,0:T(8,128)(2,1)} %bitcast.78), custom_call_target="tpu_custom_call" | custom-call | flops 8650752000 | bytes 14090240 | tf_op jit(solution)/shard_map/g_out/pallas_call | solution.py:363
  582.5 62.6 %attention_back.1 = (bf16[8,264,3840]{2,1,0:T(8,128)(2,1)}, f32[8,2560]{1,0:T(8,128)}) custom-call(bf16[8,264,3840]{2,1,0:T(8,128)(2,1)} %qkv.1.packed_ref, bf16[8,264,1280]{2,1,0:T(8,128)(2,1)} %get-tuple-element.98.refs_3_.mixed_ref, bf16[8,264,1280]{2,1,0:T(8,128)(2,1)} %get-tuple-element.129.dmixed_ref, f32[8,16,264]{2,1,0:T(8,128)} %get-tuple-element.130.lse_ref), custom_call_target="tpu_custom_call" | custom-call | flops 4730880000 | bytes 43470848 | tf_op jit(solution)/shard_map/attention_back/pallas_call | solution.py:72
  651.2 12.9 %g_q.1 = (bf16[8,80,1280]{2,1,0:T(8,128)(2,1)}, bf16[4,80,1280]{2,1,0:T(8,128)(2,1)}, bf16[4,80,1280]{2,1,0:T(8,128)(2,1)}) custom-call(s32[2]{0:T(128)} %pad_add_fusion.refs_0_, bf16[2112,1280]{1,0:T(8,128)(2,1)} %bitcast.69, bf16[2112,3840]{1,0:T(8,128)(2,1)} %bitcast.61), custom_call_target="tpu_custom_call" | custom-call | flops 8650752000 | bytes 24903680 | tf_op jit(solution)/shard_map/g_q/pallas_call | solution.py:363
  664.6 13.1 %g_k.1 = (bf16[8,80,1280]{2,1,0:T(8,128)(2,1)}, bf16[4,80,1280]{2,1,0:T(8,128)(2,1)}, bf16[4,80,1280]{2,1,0:T(8,128)(2,1)}) custom-call(s32[2]{0:T(128)} %pad_add_fusion.refs_0_, bf16[2112,1280]{1,0:T(8,128)(2,1)} %bitcast.70, bf16[2112,3840]{1,0:T(8,128)(2,1)} %bitcast.62), custom_call_target="tpu_custom_call" | custom-call | flops 8650752000 | bytes 24903680 | tf_op jit(solution)/shard_map/g_k/pallas_call | solution.py:363
  687.5 12.9 %g_v.1 = (bf16[8,80,1280]{2,1,0:T(8,128)(2,1)}, bf16[4,80,1280]{2,1,0:T(8,128)(2,1)}, bf16[4,80,1280]{2,1,0:T(8,128)(2,1)}) custom-call(s32[2]{0:T(128)} %pad_add_fusion.refs_0_, bf16[2112,1280]{1,0:T(8,128)(2,1)} %bitcast.71, bf16[2112,3840]{1,0:T(8,128)(2,1)} %bitcast.63), custom_call_target="tpu_custom_call" | custom-call | flops 8650752000 | bytes 24903680 | tf_op jit(solution)/shard_map/g_v/pallas_call | solution.py:363
  706.7 21.4 %qkv_back.2 = (f32[8,257,1280]{2,1,0:T(8,128)}, f32[8,1280]{1,0:T(8,128)}, f32[8,1280]{1,0:T(8,128)}) custom-call(bf16[1,1280,3840]{2,1,0:T(8,128)(2,1)} %bitcast.67, s32[2,1]{1,0:T(2,128)} %broadcast_1_refs_1__refs_2__refs_3_.2.refs_1_.refs_2_.refs_3_, bf16[8,264,3840]{2,1,0:T(8,128)(2,1)} %get-tuple-element.154.refs_2_, ...), custom_call_target="tpu_custom_call" | custom-call | flops 15571353600 | bytes 52741128 | tf_op jit(solution)/shard_map/qkv_back/pallas_call | solution.py:72
  733.1 21.6 %qkv_back.3 = (f32[8,257,1280]{2,1,0:T(8,128)}, f32[8,1280]{1,0:T(8,128)}, f32[8,1280]{1,0:T(8,128)}) custom-call(bf16[1,1280,3840]{2,1,0:T(8,128)(2,1)} %bitcast.68, s32[2,1]{1,0:T(2,128)} %broadcast_1_refs_1__refs_2__refs_3_.2.refs_1_.refs_2_.refs_3_, bf16[8,264,3840]{2,1,0:T(8,128)(2,1)} %get-tuple-element.154.refs_2_, ...), custom_call_target="tpu_custom_call", output_to_operand_aliasing={{0}: (6, {})} | custom-call | flops 15571353600 | bytes 63267848 | tf_op jit(solution)/shard_map/qkv_back/pallas_call | solution.py:72
  759.5 11.6 %copy.34 = f32[8,257,1280]{2,0,1:T(8,128)} copy(f32[8,257,1280]{2,1,0:T(8,128)} %down.1) | data formatting | bytes 21053440
  779.0 13.6 %collective-permute-done.17 = bf16[4,80,1280]{2,1,0:T(8,128)(2,1)} collective-permute-done((bf16[4,80,1280]{2,1,0:T(8,128)(2,1)}, bf16[4,80,1280]{2,1,0:T(8,128)(2,1)}, u32[]{:S(2)}, u32[]{:S(2)}) %collective-permute-start.17) | collective-permute-done | bytes 819232 | tf_op jit(solution)/shard_map/ppermute | solution.py:456
  797.0 11.6 %copy.35 = f32[8,257,1280]{2,0,1:T(8,128)} copy(f32[8,257,1280]{2,1,0:T(8,128)} %get-tuple-element.177) | data formatting | bytes 21053440
  830.3 14.6 %reduce-scatter.18.cloned.1.call-done = bf16[1,80,1280]{2,1,0:T(8,128)(2,1)} async-done(((bf16[4,80,1280]{2,1,0:T(8,128)(2,1)}), bf16[1,80,1280]{2,1,0:T(8,128)(2,1)}) %reduce-scatter.18.cloned.1.call-update) | async-done | bytes 204816 | tf_op jit(solution)/shard_map/reduce_scatter | solution.py:460
  (194 shorter events, 137.4 us)
Async XLA Ops:
  7.2 90.3 %all-gather.4.cloned.1.call-start = ((), (), s32[]{:S(2)}) async-start(), calls=%async_computation.7 | async-start | bytes 10444800 | tf_op jit(solution)/shard_map/all_gather | solution.py:430
  7.9 215.5 %all-gather.8.cloned.1.call-start = ((), (), s32[]{:S(2)}) async-start(), calls=%async_computation.9 | async-start | bytes 17408000 | tf_op jit(solution)/shard_map/all_gather | solution.py:430
  52.1 292.9 %all-gather.6.cloned.1.call-start = ((), (), s32[]{:S(2)}) async-start(), calls=%async_computation.8 | async-start | bytes 13926400 | tf_op jit(solution)/shard_map/all_gather | solution.py:430
  127.7 441.5 %reduce-scatter.8.cloned.1.call-start = ((), (), s32[]{:S(2)}) async-start(), calls=%async_computation.10 | async-start | bytes 4096000 | tf_op jit(solution)/shard_map/reduce_scatter | solution.py:460
  344.1 40.2 %collective-permute-start.4 = (bf16[8,320,1280]{2,1,0:T(8,128)(2,1)}, bf16[8,320,1280]{2,1,0:T(8,128)(2,1)}, u32[]{:S(2)}, u32[]{:S(2)}) collective-permute-start(bf16[8,320,1280]{2,1,0:T(8,128)(2,1)} %get-tuple-element.102), channel_id=1, source_target_pairs={{0,1},{1,0},{2,3},{3,2},{4,5},{5,4},{6,7},{7,6},{8,9},{9,8},{10,11... | collective-permute-start | bytes 19660808 | tf_op jit(solution)/shard_map/ppermute | solution.py:450
  388.2 98.6 %collective-permute-start.6 = (bf16[4,320,1280]{2,1,0:T(8,128)(2,1)}, bf16[4,320,1280]{2,1,0:T(8,128)(2,1)}, u32[]{:S(2)}, u32[]{:S(2)}) collective-permute-start(bf16[4,320,1280]{2,1,0:T(8,128)(2,1)} %slice_add_fusion), channel_id=1, source_target_pairs={{0,2},{2,0},{1,3},{3,1},{4,6},{6,4},{5,7},{7,5},{8,10},{10,8},{9,1... | collective-permute-start | bytes 9830408 | tf_op jit(solution)/shard_map/ppermute | solution.py:456
  465.0 28.7 %collective-permute-start.5 = (bf16[8,80,2560]{2,1,0:T(8,128)(2,1)}, bf16[8,80,2560]{2,1,0:T(8,128)(2,1)}, u32[]{:S(2)}, u32[]{:S(2)}) collective-permute-start(bf16[8,80,2560]{2,1,0:T(8,128)(2,1)} %get-tuple-element.111), channel_id=1, source_target_pairs={{0,1},{1,0},{2,3},{3,2},{4,5},{5,4},{6,7},{7,6},{8,9},{9,8},{10,11... | collective-permute-start | bytes 9830408 | tf_op jit(solution)/shard_map/ppermute | solution.py:450
  486.3 79.3 %collective-permute-start.7 = (bf16[8,80,2560]{2,1,0:T(8,128)(2,1)}, bf16[8,80,2560]{2,1,0:T(8,128)(2,1)S(1)}, u32[]{:S(2)}, u32[]{:S(2)}) collective-permute-start(bf16[8,80,2560]{2,1,0:T(8,128)(2,1)} %get-tuple-element.115), channel_id=1, source_target_pairs={{0,1},{1,0},{2,3},{3,2},{4,5},{5,4},{6,7},{7,6},{8,9},{9,8},{10,11... | collective-permute-start | bytes 9830408 | tf_op jit(solution)/shard_map/ppermute | solution.py:450
  493.6 157.6 %reduce-scatter.10.cloned.1.call-start = ((), (), s32[]{:S(2)}) async-start(), calls=%async_computation.11 | async-start | bytes 2048000 | tf_op jit(solution)/shard_map/reduce_scatter | solution.py:460
  496.9 64.4 %collective-permute-start.8 = (bf16[4,80,2560]{2,1,0:T(8,128)(2,1)}, bf16[4,80,2560]{2,1,0:T(8,128)(2,1)}, u32[]{:S(2)}, u32[]{:S(2)}) collective-permute-start(bf16[4,80,2560]{2,1,0:T(8,128)(2,1)} %slice_add_fusion.2), channel_id=1, source_target_pairs={{0,2},{2,0},{1,3},{3,1},{4,6},{6,4},{5,7},{7,5},{8,10},{10,8},{9,1... | collective-permute-start | bytes 4915208 | tf_op jit(solution)/shard_map/ppermute | solution.py:456
  565.5 162.6 %reduce-scatter.12.cloned.1.call-start = ((), (), s32[]{:S(2)}) async-start(), calls=%async_computation.12 | async-start | bytes 2048000 | tf_op jit(solution)/shard_map/reduce_scatter | solution.py:460
  568.4 76.7 %collective-permute-start.10 = (bf16[4,80,2560]{2,1,0:T(8,128)(2,1)}, bf16[4,80,2560]{2,1,0:T(8,128)(2,1)}, u32[]{:S(2)}, u32[]{:S(2)}) collective-permute-start(bf16[4,80,2560]{2,1,0:T(8,128)(2,1)} %slice_add_fusion.1), channel_id=1, source_target_pairs={{0,2},{2,0},{1,3},{3,1},{4,6},{6,4},{5,7},{7,5},{8,10},{10,8},{9,1... | collective-permute-start | bytes 4915208 | tf_op jit(solution)/shard_map/ppermute | solution.py:456
  582.5 66.3 %collective-permute-start.9 = (bf16[8,80,1280]{2,1,0:T(8,128)(2,1)}, bf16[8,80,1280]{2,1,0:T(8,128)(2,1)}, u32[]{:S(2)}, u32[]{:S(2)}) collective-permute-start(bf16[8,80,1280]{2,1,0:T(8,128)(2,1)} %get-tuple-element.126), channel_id=1, source_target_pairs={{0,1},{1,0},{2,3},{3,2},{4,5},{5,4},{6,7},{7,6},{8,9},{9,8},{10,11... | collective-permute-start | bytes 4915208 | tf_op jit(solution)/shard_map/ppermute | solution.py:450
  677.7 23.6 %collective-permute-start.12 = (bf16[8,80,1280]{2,1,0:T(8,128)(2,1)}, bf16[8,80,1280]{2,1,0:T(8,128)(2,1)S(1)}, u32[]{:S(2)}, u32[]{:S(2)}) collective-permute-start(bf16[8,80,1280]{2,1,0:T(8,128)(2,1)} %get-tuple-element.139), channel_id=1, source_target_pairs={{0,1},{1,0},{2,3},{3,2},{4,5},{5,4},{6,7},{7,6},{8,9},{9,8},{10,11... | collective-permute-start | bytes 4915208 | tf_op jit(solution)/shard_map/ppermute | solution.py:450
  681.6 127.0 %reduce-scatter.20.cloned.1.call-start = ((), (), s32[]{:S(2)}) async-start(), calls=%async_computation.16 | async-start | bytes 1024000 | tf_op jit(solution)/shard_map/reduce_scatter | solution.py:460
  681.6 91.4 %collective-permute-start.24 = (bf16[320,1280]{1,0:T(8,128)(2,1)}, bf16[320,1280]{1,0:T(8,128)(2,1)}, u32[]{:S(2)}, u32[]{:S(2)}) collective-permute-start(bf16[320,1280]{1,0:T(8,128)(2,1)} %bitcast.41), channel_id=1, source_target_pairs={{0,16},{16,0},{1,17},{17,1},{2,18},{18,2},{3,19},{19,3},{4,20},{20... | collective-permute-start | bytes 2457608 | tf_op jit(solution)/shard_map/ppermute | solution.py:394
  683.3 20.7 %collective-permute-start.13 = (bf16[4,80,1280]{2,1,0:T(8,128)(2,1)}, bf16[4,80,1280]{2,1,0:T(8,128)(2,1)}, u32[]{:S(2)}, u32[]{:S(2)}) collective-permute-start(bf16[4,80,1280]{2,1,0:T(8,128)(2,1)} %slice_add_fusion.6), channel_id=1, source_target_pairs={{0,2},{2,0},{1,3},{3,1},{4,6},{6,4},{5,7},{7,5},{8,10},{10,8},{9,1... | collective-permute-start | bytes 2457608 | tf_op jit(solution)/shard_map/ppermute | solution.py:456
  700.5 30.5 %collective-permute-start.14 = (bf16[8,80,1280]{2,1,0:T(8,128)(2,1)}, bf16[8,80,1280]{2,1,0:T(8,128)(2,1)S(1)}, u32[]{:S(2)}, u32[]{:S(2)}) collective-permute-start(bf16[8,80,1280]{2,1,0:T(8,128)(2,1)} %get-tuple-element.145), channel_id=1, source_target_pairs={{0,1},{1,0},{2,3},{3,2},{4,5},{5,4},{6,7},{7,6},{8,9},{9,8},{10,11... | collective-permute-start | bytes 4915208 | tf_op jit(solution)/shard_map/ppermute | solution.py:450
  700.6 27.6 %collective-permute-start.15 = (bf16[4,80,1280]{2,1,0:T(8,128)(2,1)}, bf16[4,80,1280]{2,1,0:T(8,128)(2,1)}, u32[]{:S(2)}, u32[]{:S(2)}) collective-permute-start(bf16[4,80,1280]{2,1,0:T(8,128)(2,1)} %slice_add_fusion.5), channel_id=1, source_target_pairs={{0,2},{2,0},{1,3},{3,1},{4,6},{6,4},{5,7},{7,5},{8,10},{10,8},{9,1... | collective-permute-start | bytes 2457608 | tf_op jit(solution)/shard_map/ppermute | solution.py:456
  728.1 95.4 %reduce-scatter.14.cloned.1.call-start = ((), (), s32[]{:S(2)}) async-start(), calls=%async_computation.13 | async-start | bytes 1024000 | tf_op jit(solution)/shard_map/reduce_scatter | solution.py:460
  771.1 21.4 %collective-permute-start.17 = (bf16[4,80,1280]{2,1,0:T(8,128)(2,1)}, bf16[4,80,1280]{2,1,0:T(8,128)(2,1)}, u32[]{:S(2)}, u32[]{:S(2)}) collective-permute-start(bf16[4,80,1280]{2,1,0:T(8,128)(2,1)} %slice_add_fusion.4), channel_id=1, source_target_pairs={{0,2},{2,0},{1,3},{3,1},{4,6},{6,4},{5,7},{7,5},{8,10},{10,8},{9,1... | collective-permute-start | bytes 2457608 | tf_op jit(solution)/shard_map/ppermute | solution.py:456
  771.1 55.5 %reduce-scatter.16.cloned.1.call-start = ((), (), s32[]{:S(2)}) async-start(), calls=%async_computation.14 | async-start | bytes 1024000 | tf_op jit(solution)/shard_map/reduce_scatter | solution.py:460
  776.4 42.2 %collective-permute-start.19 = (bf16[4,80,1280]{2,1,0:T(8,128)(2,1)}, bf16[4,80,1280]{2,1,0:T(8,128)(2,1)}, u32[]{:S(2)}, u32[]{:S(2)}) collective-permute-start(bf16[4,80,1280]{2,1,0:T(8,128)(2,1)} %slice_add_fusion.3), channel_id=1, source_target_pairs={{0,2},{2,0},{1,3},{3,1},{4,6},{6,4},{5,7},{7,5},{8,10},{10,8},{9,1... | collective-permute-start | bytes 2457608 | tf_op jit(solution)/shard_map/ppermute | solution.py:456
  794.9 49.9 %reduce-scatter.18.cloned.1.call-start = ((), (), s32[]{:S(2)}) async-start(), calls=%async_computation.15 | async-start | bytes 1024000 | tf_op jit(solution)/shard_map/reduce_scatter | solution.py:460
  (28 other events, 358.2 us)
Sparse Core Ops, SparseCore 0:
  10.3 87.1 all-gather.3
  100.4 122.9 all-gather.7
  225.7 102.2 all-gather.5
  493.7 61.4 reduce-scatter.7
  565.7 34.7 reduce-scatter.9
  681.7 35.5 reduce-scatter.11
  728.2 22.4 reduce-scatter.19
  771.3 22.6 reduce-scatter.13
  796.3 22.8 reduce-scatter.15
  821.9 22.9 reduce-scatter.17

commit v2 on v1

--- a/solution.py
+++ b/solution.py
@@ -57,32 +57,41 @@
     return pl.CostEstimate(flops=int(flops), transcendentals=0, bytes_accessed=moved)
 
 
-def call(kernel, n, ins, outs, name, flops=0, scratch=(), first=0, alias=None):
-    def spec(shape, kind):
-        if kind == "raw":
-            return pl.BlockSpec(memory_space=pl.ANY)
-        if kind == "scalars":
-            return pl.BlockSpec(memory_space=pltpu.SMEM)
-        if kind == "image":
-            return pl.BlockSpec((1,) + tuple(shape[1:]), lambda i: (i + first,) + (0,) * (len(shape) - 1))
-        if kind == "whole":
-            return pl.BlockSpec(tuple(shape), lambda i: (0,) * len(shape), pipeline_mode=pl.Buffered(1))
-        return pl.BlockSpec(tuple(shape), lambda i: (0,) * len(shape))
-
+def grid_call(kernel, grid, ins, outs, name, flops=0, scratch=()):
     return pl.pallas_call(
         kernel,
-        grid=(n,),
-        in_specs=[spec(a.shape, k) for a, k in ins],
-        out_specs=[spec(a.shape, k) for a, k in outs],
+        grid=grid,
+        in_specs=[spec for _, spec in ins],
+        out_specs=[spec for _, spec in outs],
         out_shape=[a for a, _ in outs],
         scratch_shapes=list(scratch),
-        input_output_aliases=alias or {},
-        compiler_params=pltpu.CompilerParams(vmem_limit_bytes=60 << 20),
+        compiler_params=pltpu.CompilerParams(vmem_limit_bytes=62 << 20),
         cost_estimate=cost(flops, [a for a, _ in ins] + [a for a, _ in outs]),
         name=name,
     )(*[a for a, _ in ins])
 
 
+def whole(a):
+    return a, pl.BlockSpec(tuple(a.shape), lambda *at: (0,) * len(a.shape), pipeline_mode=pl.Buffered(1))
+
+
+def total(a):
+    return a, pl.BlockSpec(tuple(a.shape), lambda *at: (0,) * len(a.shape))
+
+
+def untouched(a):
+    return a, pl.BlockSpec(memory_space=pl.ANY)
+
+
+def call(kernel, n, ins, outs, name, flops=0, scratch=()):
+    def specs(pairs):
+        for a, kind in pairs:
+            if kind == "image":
+                kind = pl.BlockSpec((1,) + tuple(a.shape[1:]), lambda i, last=len(a.shape) - 1: (i,) + (0,) * last)
+            yield a, kind
+    return grid_call(kernel, (n,), list(specs(ins)), list(specs(outs)), name, flops, scratch)
+
+
 def accumulate(ref, value):
     @pl.when(pl.program_id(0) == 0)
     def _():
@@ -90,19 +99,24 @@
     ref[...] += value
 
 
-def prepare_kernel(x_ref, c_ref, gain_ref, shift_ref, normed_ref, cpad_ref, sum_ref):
-    xhat, _ = standardize(x_ref[0].astype(F32))
+def prepare_kernel(x_ref, c_ref, gain_ref, shift_ref, normed_ref, xpad_ref, cpad_ref, sum_ref):
+    x = x_ref[0].astype(F32)
+    xhat, _ = standardize(x)
     normed = xhat * gain_ref[...] + shift_ref[...]
     normed_ref[0] = pad_rows(normed).astype(BF)
+    xpad_ref[0] = pad_rows(x).astype(BF)
     c = pad_rows(c_ref[0].astype(F32))
     cpad_ref[0] = c.astype(BF)
     accumulate(sum_ref, fold_rows(c))
 
 
+def flat(ref):
+    return ref[...].reshape(ref.shape[0] * ref.shape[1], ref.shape[2])
+
+
 def qkv_kernel(w_ref, normed_ref, bias_ref, packed_ref):
-    for j in range(packed_ref.shape[2] // D):
-        cols = slice(j * D, (j + 1) * D)
-        packed_ref[0, :, cols] = (dot_nn(normed_ref[0], w_ref[:, cols]) + bias_ref[:, cols]).astype(BF)
+    out = dot_nn(flat(normed_ref), w_ref[...]) + bias_ref[...]
+    packed_ref[...] = out.astype(BF).reshape(packed_ref.shape)
 
 
 def drop_tail(rows):
@@ -138,63 +152,82 @@
 
 
 def out_kernel(w_ref, x_ref, mixed_ref, bias_ref, gain_ref, shift_ref, hidden_ref, normed_ref):
-    hidden = pad_rows(x_ref[0].astype(F32)) + dot_nn(mixed_ref[0], w_ref[...]) + bias_ref[...]
-    hidden_ref[0] = hidden
+    hidden = flat(x_ref).astype(F32) + dot_nn(flat(mixed_ref), w_ref[...]) + bias_ref[...]
+    hidden_ref[...] = hidden.reshape(hidden_ref.shape)
     xhat, _ = standardize(hidden)
     normed = xhat * gain_ref[...] + shift_ref[...]
-    keep = lax.broadcasted_iota(jnp.int32, normed.shape, 0) < SEQ
-    normed_ref[0] = jnp.where(keep, normed, 0.0).astype(BF)
-
-
-CHUNK = 512
+    keep = lax.rem(lax.broadcasted_iota(jnp.int32, normed.shape, 0), SP) < SEQ
+    normed_ref[...] = jnp.where(keep, normed, 0.0).astype(BF).reshape(normed_ref.shape)
 
 
 def up_kernel(w_ref, normed_ref, bias_ref, active_ref, slope_ref):
-    normed = normed_ref[0]
-
-    def step(j, carry):
-        cols = pl.ds(pl.multiple_of(j * CHUNK, CHUNK), CHUNK)
-        u = dot_nn(normed, w_ref[:, cols]) + bias_ref[:, cols]
-        cdf = 0.5 * (1.0 + lax.erf(u * 0.7071067811865476))
-        active_ref[0, :, cols] = (u * cdf).astype(BF)
-        slope_ref[0, :, cols] = (cdf + u * jnp.exp(-0.5 * u * u) * 0.3989422804014327).astype(BF)
-        return carry
-    lax.fori_loop(0, FF // CHUNK, step, 0)
-
-
-def down_kernel(w_ref, active_ref, hidden_ref, bias_ref, result_ref):
+    u = dot_nn(flat(normed_ref), w_ref[...]) + bias_ref[...]
+    cdf = 0.5 * (1.0 + lax.erf(u * 0.7071067811865476))
+    active_ref[...] = (u * cdf).astype(BF).reshape(active_ref.shape)
+    slope_ref[...] = (cdf + u * jnp.exp(-0.5 * u * u) * 0.3989422804014327).astype(BF).reshape(slope_ref.shape)
+
+
+def interleave(rows, out_ref, stage_ref, sems):
+    image, last = pl.program_id(0), pl.num_programs(0) - 1
+    tiles = stage_ref.shape[0]
+    step = stage_ref.shape[1] // SEQ
+    for k in range(tiles):
+        stage_ref[k, pl.ds(image, SEQ, stride=step), :] = rows[:SEQ, k * 128:(k + 1) * 128]
+
+    @pl.when(image == last)
+    def _():
+        copies = [pltpu.make_async_copy(stage_ref.at[k], out_ref.at[:, k * 128:(k + 1) * 128], sems.at[k]) for k in range(tiles)]
+        for copy in copies:
+            copy.start()
+        for copy in copies:
+            copy.wait()
+
+
+def down_kernel(w_ref, active_ref, hidden_ref, bias_ref, result_ref, stage_ref, sems):
     result = hidden_ref[0] + dot_nn(active_ref[0], w_ref[...]) + bias_ref[...]
-    result_ref[0] = result[:SEQ]
+    interleave(result, result_ref, stage_ref, sems)
 
 
 def down_back_kernel(w_ref, c_ref, slope_ref, dinner_ref, sum_ref):
-    c = c_ref[0]
-
-    @pl.when(pl.program_id(0) == 0)
+    d = dot_nt(flat(c_ref), w_ref[...]) * flat(slope_ref).astype(F32)
+    dinner_ref[...] = d.astype(BF).reshape(dinner_ref.shape)
+
+    @pl.when(pl.program_id(1) == 0)
     def _():
         sum_ref[...] = jnp.zeros_like(sum_ref)
-
-    def step(j, carry):
-        rows = pl.ds(pl.multiple_of(j * CHUNK, CHUNK), CHUNK)
-        d = dot_nt(c, w_ref[rows, :]) * slope_ref[0, :, rows].astype(F32)
-        dinner_ref[0, :, rows] = d.astype(BF)
-        sum_ref[:, rows] += fold_rows(d)
-        return carry
-    lax.fori_loop(0, FF // CHUNK, step, 0)
-
-
-def up_back_kernel(w_up_ref, w_out_ref, dinner_ref, hidden_ref, c_ref, gain_ref,
-                   dhidden_ref, dhidden_b_ref, dmixed_ref, sum_gain_ref, sum_shift_ref, sum_out_ref):
-    e = dot_nt(dinner_ref[0], w_up_ref[...])
-    xhat, inverse = standardize(hidden_ref[0])
-    dhidden = c_ref[0].astype(F32) + norm_gradient(e, xhat, inverse, gain_ref[...])
-    dhidden_ref[0] = dhidden
-    dhidden_b = dhidden.astype(BF)
-    dhidden_b_ref[0] = dhidden_b
-    dmixed_ref[0] = dot_nt(dhidden_b, w_out_ref[...]).astype(BF)
-    accumulate(sum_gain_ref, fold_rows(e * xhat))
-    accumulate(sum_shift_ref, fold_rows(e))
-    accumulate(sum_out_ref, fold_rows(dhidden))
+    sum_ref[...] += fold_rows(d)
+
+
+def up_back_kernel(w_up_ref, dinner_ref, w_out_ref, hidden_ref, c_ref, gain_ref,
+                   dhidden_ref, dhidden_b_ref, dmixed_ref, sum_gain_ref, sum_shift_ref, sum_out_ref, acc_ref):
+    i, k = pl.program_id(0), pl.program_id(1)
+
+    @pl.when(k == 0)
+    def _():
+        acc_ref[...] = dot_nt(flat(dinner_ref), w_up_ref[...])
+
+    @pl.when(k > 0)
+    def _():
+        acc_ref[...] += dot_nt(flat(dinner_ref), w_up_ref[...])
+
+    @pl.when(jnp.logical_and(i == 0, k == 0))
+    def _():
+        for ref in (sum_gain_ref, sum_shift_ref, sum_out_ref):
+            ref[...] = jnp.zeros_like(ref)
+
+    @pl.when(k == pl.num_programs(1) - 1)
+    def _():
+        for image in range(dhidden_ref.shape[0]):
+            e = acc_ref[image * SP:(image + 1) * SP]
+            xhat, inverse = standardize(hidden_ref[image])
+            dhidden = c_ref[image].astype(F32) + norm_gradient(e, xhat, inverse, gain_ref[...])
+            dhidden_ref[image] = dhidden
+            dhidden_b = dhidden.astype(BF)
+            dhidden_b_ref[image] = dhidden_b
+            dmixed_ref[image] = dot_nt(dhidden_b, w_out_ref[...]).astype(BF)
+            sum_gain_ref[...] += fold_rows(e * xhat)
+            sum_shift_ref[...] += fold_rows(e)
+            sum_out_ref[...] += fold_rows(dhidden)
 
 
 def attention_back_kernel(packed_ref, mixed_ref, dmixed_ref, lse_ref, dpacked_ref, sum_ref):
@@ -237,62 +270,18 @@
     lax.fori_loop(0, H // GROUP, group, 0)
 
 
-def qkv_back_kernel(w_ref, dpacked_ref, x_ref, dhidden_ref, gain_ref, *refs):
-    dimages_ref, sum_gain_ref, sum_shift_ref = refs[-3:]
-    e = dot_nt(dpacked_ref[0], w_ref[...])[:SEQ]
+def qkv_back_kernel(w_ref, dpacked_ref, x_ref, dhidden_ref, gain_ref,
+                    dimages_ref, sum_gain_ref, sum_shift_ref, stage_ref, sems):
+    e = dot_nt(dpacked_ref[0], w_ref[...])
     xhat, inverse = standardize(x_ref[0].astype(F32))
-    dimages_ref[0] = dhidden_ref[0, :SEQ] + norm_gradient(e, xhat, inverse, gain_ref[...])
-    accumulate(sum_gain_ref, fold_rows(pad_rows(e * xhat)))
-    accumulate(sum_shift_ref, fold_rows(pad_rows(e)))
+    dimages = dhidden_ref[0] + norm_gradient(e, xhat, inverse, gain_ref[...])
+    interleave(dimages, dimages_ref, stage_ref, sems)
+    accumulate(sum_gain_ref, fold_rows(e * xhat))
+    accumulate(sum_shift_ref, fold_rows(e))
 
 
 def sds(*shape, dtype=BF):
     return jax.ShapeDtypeStruct(shape, dtype)
-
-
-def weighted(kernel, plans):
-    total = sum(len(plan) for plan in plans)
-
-    def run(*refs):
-        pieces, rest = refs[:total], refs[total:]
-        places, rest = rest[:len(plans)], rest[len(plans):]
-        own, scratch = rest[:len(rest) - 2 * len(plans)], rest[len(rest) - 2 * len(plans):]
-        weights, sems = scratch[0::2], scratch[1::2]
-
-        @pl.when(pl.program_id(0) == 0)
-        def _():
-            copies, first = [], 0
-            for plan, place, weight, sem in zip(plans, places, weights, sems):
-                n = 0
-                for count, there, here, width in plan:
-                    rows = pieces[first].shape[1]
-                    for k in range(count):
-                        at = pl.ds(pl.multiple_of(place[0, n] * rows, 16), rows)
-                        cols = pl.ds(pl.multiple_of(here + place[1, n] * width, 128), width)
-                        copies.append(pltpu.make_async_copy(
-                            pieces[first].at[k, :, there:there + width], weight.at[at, cols], sem.at[n]))
-                        n += 1
-                    first += 1
-            for copy in copies:
-                copy.start()
-            for copy in copies:
-                copy.wait()
-        kernel(*weights, *own)
-    return run
-
-
-def weight_call(kernel, n, weights, ins, outs, name, flops, **more):
-    plans = [[(a.shape[0], there, here, columns) for a, _, there, here, columns in w] for _, w in weights]
-    operands = [(piece[0], "raw") for _, w in weights for piece in w]
-    operands += [(jnp.concatenate([piece[1] for piece in w], 1), "scalars") for _, w in weights] + list(ins)
-    scratch = []
-    for width, w in weights:
-        rows = sum(a.shape[0] * a.shape[1] * columns for a, _, _, _, columns in w) // width
-        scratch.append(pltpu.VMEM((rows, width), BF))
-        scratch.append(pltpu.SemaphoreType.DMA((sum(piece[0].shape[0] for piece in w),)))
-    if "alias" in more:
-        more["alias"] = {len(operands) - len(ins) + k: v for k, v in more["alias"].items()}
-    return call(weighted(kernel, plans), n, operands, outs, name, flops * n * SP, scratch, **more)
 
 
 def gradient_kernel(rows, steps, relative, spots, place_ref, l_ref, r_ref, *rest):
@@ -402,13 +391,16 @@
         return lax.all_gather(vector.reshape(1, -1), "fsdp", axis=0, tiled=True)
 
     def gather(self, w):
-        return [(lax.all_gather(w, "fsdp", axis=0, tiled=True)[None], jnp.zeros((2, 1), jnp.int32))]
+        return lax.all_gather(w, "fsdp", axis=0, tiled=True)
 
     def first_stage(self, parts, *before):
         return parts
 
     def second_stage(self, parts, *before):
         return parts
+
+    def joined(self, parts):
+        return (jnp.concatenate([p[0] for p in parts], 2),)
 
     def third_stage(self, parts):
         whole = parts[0].reshape(-1, parts[0].shape[2])
@@ -427,7 +419,7 @@
         self.z = jnp.arange(self.count, dtype=jnp.int32)
 
     def gather(self, w):
-        return [(lax.all_gather(w, ("z", "x", "core"), axis=0, tiled=True)[None], jnp.zeros((2, 1), jnp.int32))]
+        return lax.all_gather(w, ("z", "x", "core"), axis=0, tiled=True)
 
     def gather_small(self, vector):
         rows = vector.reshape(1, -1)
@@ -455,6 +447,9 @@
         half, keep = got.shape[0] // 2, after(keep, *before)
         got_x = lax.ppermute(passed, "x", SWAP)
         return (keep.astype(F32) + got[:half].astype(F32) + got_x.astype(F32)).astype(BF)
+
+    def joined(self, parts):
+        return tuple(jnp.concatenate(a, 2) for a in zip(*parts))
 
     def third_stage(self, total):
         return lax.psum_scatter(total, "z", scatter_dimension=0, tiled=True)[0]
@@ -485,108 +480,115 @@
     return vector.reshape(1, -1).astype(F32)
 
 
-def columns(pieces, there, here, width):
-    return [(a, places, there, here, width) for a, places in pieces]
-
-
 def layer(links, images, cotangent, w_qkv, w_out, w_up, w_down, *vectors):
     n, owners = images.shape[0], links.owners
 
     sizes = [v.shape[0] for v in vectors]
     small = links.gather_small(jnp.concatenate(vectors))
-    whole, first = [], 0
+    full, first = [], 0
     for size in sizes:
-        whole.append(row(small[:, first:first + size]))
+        full.append(row(small[:, first:first + size]))
         first += size
-    b_qv, b_out, b_up, b_down, gain_one, shift_one, gain_two, shift_two = whole
+    b_qv, b_out, b_up, b_down, gain_one, shift_one, gain_two, shift_two = full
 
     def image(a):
         return (a, "image")
 
-    def fixed(a):
-        return (a, "whole")
-
     def rows(*shape, dtype=BF):
         return (sds(n, *shape, dtype=dtype), "image")
 
     def sums(width):
-        return (sds(8, width, dtype=F32), "sum")
+        return total(sds(8, width, dtype=F32))
 
     def gradient(left, right, name, first=0, width=None):
         return weight_gradient(left, right, owners, links.mine, links.relative, name, first, width)
 
-    g_qkv = links.gather(w_qkv)
-    full_qkv = columns(g_qkv, 0, 0, 3 * D)
-    normed_one, cpad, s_down = call(
-        prepare_kernel, n, [image(images), image(cotangent), fixed(gain_one), fixed(shift_one)],
-        [rows(SP, D), rows(SP, D), sums(D)], "prepare", 8 * n * SP * D * 50)
-    g_middle = links.gather(after(jnp.concatenate([w_out, w_up], 1), normed_one))
-    full_out, full_up = columns(g_middle, 0, 0, D), columns(g_middle, D, 0, FF)
+    def by_columns(kernel, weight, rows_in, others, outs, name, flops, sum_width=0):
+        def cut(a):
+            if len(a.shape) == 2:
+                return a, pl.BlockSpec((a.shape[0], D), lambda j, i: (0, j))
+            return a, pl.BlockSpec((4, SP, D), lambda j, i: (i, 0, j))
+        results = [cut(a) for a in outs]
+        return grid_call(
+            kernel, (outs[0].shape[2] // D, n // 4),
+            [weight, (rows_in, pl.BlockSpec((4, SP, D), lambda j, i: (i, 0, 0)))] + [cut(a) for a in others],
+            results, name, flops * n * SP)
+
+    full_qkv = links.gather(w_qkv)
+    normed_one, xpad, cpad, s_down = call(
+        prepare_kernel, n, [image(images), image(cotangent), whole(gain_one), whole(shift_one)],
+        [rows(SP, D), rows(SP, D), rows(SP, D), sums(D)], "prepare", 8 * n * SP * D * 50)
+    middle = links.gather(after(jnp.concatenate([w_up, w_out], 1), normed_one))
+    full_out = middle, pl.BlockSpec((D, D), lambda *at: (0, FF // D), pipeline_mode=pl.Buffered(1))
     bias = jnp.concatenate([b_qv[:, :D], jnp.zeros((1, D), F32), b_qv[:, D:]], 1)
-    packed, = weight_call(
-        qkv_kernel, n, [(3 * D, full_qkv)], [image(normed_one), fixed(bias)], [rows(SP, 3 * D)], "qkv", 2.5 * D * 3 * D)
-    full_down = columns(links.gather(after(w_down, packed)), 0, 0, D)
+    packed, = by_columns(
+        qkv_kernel, (full_qkv, pl.BlockSpec((D, D), lambda j, i: (0, j))), normed_one, [bias], [sds(n, SP, 3 * D)],
+        "qkv", 2.5 * D * 3 * D)
+    full_down = links.gather(after(w_down, packed))
     mixed, logsum = call(
         attention_kernel, n, [image(packed)], [rows(SP, D), rows(H, SP, dtype=F32)], "attention", 1e5 * n * SP * H)
-    hidden, normed_two = weight_call(
-        out_kernel, n, [(D, full_out)],
-        [image(images), image(mixed), fixed(b_out), fixed(gain_two), fixed(shift_two)],
-        [rows(SP, D, dtype=F32), rows(SP, D)], "out", 3 * D * D)
-    active, slope = weight_call(
-        up_kernel, n, [(FF, full_up)], [image(normed_two), fixed(b_up)], [rows(SP, FF), rows(SP, FF)], "up", 4 * D * FF)
+    hidden, normed_two = call(
+        out_kernel, n,
+        [full_out, image(xpad), image(mixed), whole(b_out), whole(gain_two), whole(shift_two)],
+        [rows(SP, D, dtype=F32), rows(SP, D)], "out", 3 * D * D * n * SP)
+    active, slope = by_columns(
+        up_kernel, (middle, pl.BlockSpec((D, D), lambda j, i: (0, j))), normed_two, [b_up], [sds(n, SP, FF)] * 2,
+        "up", 4 * D * FF)
 
     p_down = gradient(active, cpad, "g_down")
-    result, = weight_call(
-        down_kernel, n, [(D, full_down)],
-        [image(after(active, p_down)), image(hidden), fixed(b_down)], [rows(SEQ, D, dtype=F32)], "down", 2.5 * D * FF)
+    staging = [pltpu.VMEM((D // 128, SEQ * n, 128), F32), pltpu.SemaphoreType.DMA((D // 128,))]
+    result, = call(
+        down_kernel, n, [whole(full_down), image(after(active, p_down)), image(hidden), whole(b_down)],
+        [untouched(sds(SEQ * n, D, dtype=F32))], "down", 2.5 * D * FF * n * SP, staging)
     p_down = links.first_stage(p_down, result)
-    d_inner, s_up = weight_call(
-        down_back_kernel, n, [(D, full_down)], [image(after(cpad, result, p_down[0])), image(slope)],
-        [rows(SP, FF), sums(FF)], "down_back", 3 * D * FF)
+    d_inner, s_up = by_columns(
+        down_back_kernel, (full_down, pl.BlockSpec((D, D), lambda j, i: (j, 0))), after(cpad, result, p_down[0]), [slope],
+        [sds(n, SP, FF), sds(8, FF, dtype=F32)], "down_back", 3 * D * FF)
     p_up = gradient(normed_two, d_inner, "g_up_low", 0, FF // 2)
     p_up2 = gradient(normed_two, after(d_inner, p_up), "g_up_high", FF // 2, FF // 2)
     p_up = links.first_stage(p_up, p_up2)
     p_down = links.second_stage(p_down, p_up2)
-    d_hidden, d_hidden_b, d_mixed, s_gain_two, s_shift_two, s_out = weight_call(
-        up_back_kernel, n, [(FF, full_up), (D, full_out)],
-        [image(after(d_inner, p_up2, p_up[0], p_down)), image(hidden), image(cpad), fixed(gain_two)],
-        [rows(SP, D, dtype=F32), rows(SP, D), rows(SP, D), sums(D), sums(D), sums(D)], "up_back", 3 * D * (D + FF))
+
+    def pair(a):
+        return a, pl.BlockSpec((2,) + tuple(a.shape[1:]), lambda i, k: (i, 0, 0))
+    d_hidden, d_hidden_b, d_mixed, s_gain_two, s_shift_two, s_out = grid_call(
+        up_back_kernel, (n // 2, 2),
+        [(middle, pl.BlockSpec((D, FF // 2), lambda i, k: (0, k))),
+         (after(d_inner, p_up2, p_up[0], p_down), pl.BlockSpec((2, SP, FF // 2), lambda i, k: (i, 0, k))),
+         full_out, pair(hidden), pair(cpad), whole(gain_two)],
+        [pair(sds(n, SP, D, dtype=F32)), pair(sds(n, SP, D)), pair(sds(n, SP, D)), sums(D), sums(D), sums(D)],
+        "up_back", 3 * D * (D + FF) * n * SP, [pltpu.VMEM((2 * SP, D), F32)])
     p_down = links.third_stage(p_down)
-    p_up2 = links.first_stage(p_up2, d_hidden_b)
     p_up = links.second_stage(p_up, d_hidden_b)
-    p_out = gradient(mixed, after(d_hidden_b, p_up2[0], p_up, p_down), "g_out")
+    p_out = gradient(mixed, after(d_hidden_b, p_up, p_down), "g_out")
     p_up = links.third_stage(p_up)
+    p_up2 = links.first_stage(p_up2, p_out)
+    p_out = links.first_stage(p_out)
+    rest = links.joined([p_up2, p_out])
     d_packed, s_qv = call(
-        attention_back_kernel, n, [image(packed), image(mixed), image(after(d_mixed, p_out)), image(logsum)],
+        attention_back_kernel, n, [image(packed), image(mixed), image(after(d_mixed, rest[0])), image(logsum)],
         [rows(SP, 3 * D), sums(2 * D)], "attention_back", 1.4e5 * n * SP * H)
     g_down = both_groups(after(p_down, d_packed))
-    p_out = links.first_stage(p_out, d_packed)
-    p_up2 = links.second_stage(p_up2, d_packed)
-    p_q = gradient(normed_one, after(d_packed, p_out[0], p_up2, p_up), "g_q", 0, D)
-    p_up2 = links.third_stage(p_up2)
-    p_k = gradient(normed_one, after(d_packed, p_q), "g_k", D, D)
-    p_q = links.first_stage(p_q, p_k)
-    p_v = gradient(normed_one, after(d_packed, p_k, p_q[0]), "g_v", 2 * D, D)
-    p_k = links.first_stage(p_k, p_v)
-    p_out = links.second_stage(p_out, p_v)
-
-    def qkv_back(first, d_packed, more):
-        return weight_call(
-            qkv_back_kernel, n // 2, [(3 * D, full_qkv)],
-            [image(d_packed), image(images), image(d_hidden), fixed(gain_one)] + [(a, "raw") for a in more],
-            [rows(SEQ, D, dtype=F32), sums(D), sums(D)], "qkv_back", 3 * D * 3 * D,
-            first=first, alias={4: 0} if more else {})
-    d_images, s_gain_one, s_shift_one = qkv_back(0, after(d_packed, p_v, p_k[0], p_out), ())
-    g_up = both_groups(after(p_up, d_images))
+    rest = links.second_stage(rest, d_packed)
+    p_qk = gradient(normed_one, after(d_packed, rest, p_up), "g_qk", 0, 2 * D)
+    rest = links.third_stage(rest)
+    p_v = gradient(normed_one, after(d_packed, p_qk), "g_v", 2 * D, D)
+    p_qk = links.first_stage(p_qk, p_v)
+    d_images, s_gain_one, s_shift_one = call(
+        qkv_back_kernel, n,
+        [whole(full_qkv), image(after(d_packed, p_v, p_qk[0], rest)), image(xpad), image(d_hidden), whole(gain_one)],
+        [untouched(sds(SEQ * n, D, dtype=F32)), sums(D), sums(D)], "qkv_back", 3 * D * 3 * D * n * SP, staging)
+    g_up = both_groups(after(p_up, p_qk[0]))
     p_v = links.first_stage(p_v, d_images)
-    p_q = links.second_stage(p_q, d_images)
-    p_out = links.third_stage(after(p_out, p_up2, d_images))
-    d_images, more_gain, more_shift = qkv_back(n // 2, after(d_packed, p_v[0], p_q, p_up2), (d_images,))
-    p_q = links.third_stage(p_q)
-    p_k = links.third_stage(links.second_stage(p_k, d_images))
-    p_v = links.third_stage(links.second_stage(p_v, d_images))
-    s_gain_one, s_shift_one = s_gain_one + more_gain, s_shift_one + more_shift
-    g_up2, g_out, g_q, g_k, g_v = [both_groups(after(p, d_images)) for p in (p_up2, p_out, p_q, p_k, p_v)]
+    p_qk = links.second_stage(p_qk, d_images)
+    p_v = links.second_stage(p_v, d_images, p_qk)
+    p_qk = links.third_stage(p_qk)
+    s_gain_one = after(s_gain_one, p_v)
+    rest = both_groups(after(rest, p_qk))
+    g_up2, g_out = rest[:, :FF // 2], rest[:, FF // 2:]
+    p_v = links.third_stage(after(p_v, p_qk))
+    g_qk, g_v = both_groups(p_qk), both_groups(p_v)
+    result, d_images = [jnp.transpose(a.reshape(SEQ, n, D), (1, 0, 2)) for a in (result, d_images)]
     g_up = jnp.concatenate([g_up, g_up2], 1)
 
     parts = [s_qv, s_out, s_up, s_down, s_gain_one, s_shift_one, s_gain_two, s_shift_two]
@@ -595,7 +597,7 @@
     for size in sizes:
         small_grads.append(share[first:first + size])
         first += size
-    return (result, d_images, jnp.concatenate([g_q, g_k, g_v], 1), g_out, g_up, g_down, *small_grads)
+    return (result, d_images, jnp.concatenate([g_qk, g_v], 1), g_out, g_up, g_down, *small_grads)
 
 
 def solution(mesh):

time: 867 us -> 821 us (0.947)
  Pallas kernels: 568 us -> 520 us
  waiting for transfers between devices: 137 us -> 173 us
  local copies, waits for them, and re-layouts: 46.5 us -> 27.9 us
  other arithmetic: 63.3 us -> 51.4 us
    pallas_call x11 -> x10, Pallas kernels: 436 us -> 393 us  [grid_call(): pl.pallas_call(kernel, grid=grid, in_specs=[spec for _, spec in ins], out...]
    ppermute x7 -> x5, waiting for transfers between devices: 13.1 us -> 33.8 us  [both_groups(): return shard.astype(F32) + lax.ppermute(shard, 'dp', SWAP).astype(F32)]
    unnamed x30 -> x46, local copies, waits for them, and re-layouts: 32.8 us -> 13 us
    all_gather x3, waiting for transfers between devices: 88.6 us -> 101 us  [gather(): return lax.all_gather(w, ('z', 'x', 'core'), axis=0, tiled=True)]
    pallas_call x7 -> x6, Pallas kernels: 132 us -> 127 us  [weight_gradient(): pl.pallas_call(kernel, grid=(left.shape[1] // block, width // cols), in_s...]
    add x7 -> x6, other arithmetic: 19.4 us -> 14.8 us  [first_stage(): return (after(pass_on, *before) + got[half:], keep, got)]
    convert_element_type x7 -> x5, other arithmetic: 24.8 us -> 21.8 us  [second_stage(): (keep.astype(F32) + got[:half].astype(F32) + got_x.astype(F32)).astype(BF)]
  transfers between devices with their start and end apart: 40 -> 33, of which waited for: 13 -> 17; matrix products, arithmetic and copies ran while one was open for 12% -> 8% of each run, Pallas kernels for 64% -> 64%
where the time goes in v2:
time: 821 us; the launch traced here: 815 us
  Pallas kernels  520 us (63%)
  waiting for transfers between devices  173 us (21%)
  other arithmetic  51.4 us (6%)
  starting transfers between devices  28.7 us (3%)
  local copies, waits for them, and re-layouts  27.9 us (3%)
  between operations  15 us (2%)
    pallas_call x10, Pallas kernels, grid_call(): pl.pallas_call(kernel, grid=grid, in_specs=[spec for _, spec in ins], out...  393 us
    pallas_call x6, Pallas kernels, weight_gradient(): pl.pallas_call(kernel, grid=(left.shape[1] // block, width // cols), in_s...  127 us
    all_gather x3, waiting for transfers between devices, gather(): return lax.all_gather(w, ('z', 'x', 'core'), axis=0, tiled=True)  101 us
    ppermute x5, waiting for transfers between devices, both_groups(): return shard.astype(F32) + lax.ppermute(shard, 'dp', SWAP).astype(F32)  33.8 us
    convert_element_type x5, other arithmetic, second_stage(): (keep.astype(F32) + got[:half].astype(F32) + got_x.astype(F32)).astype(BF)  21.8 us
  transfers between devices with their start and end apart: 33, of which 17 were waited for; matrix products, arithmetic and copies ran while one was open for 8% of the time, Pallas kernels for 64%

profile of v2, /device:TPU:0, one launch (start us, length us, event | category | flops | bytes accessed | tf_op | source)
XLA Modules:
  0.0 815.4 jit_solution(15558587858547595309)
XLA Ops:
  39.5 13.5 %prepare.1 = (bf16[8,264,1280]{2,1,0:T(8,128)(2,1)}, bf16[8,264,1280]{2,1,0:T(8,128)(2,1)}, bf16[8,264,1280]{2,1,0:T(8,128)(2,1)}, f32[8,1280]{1,0:T(8,128)}) custom-call(bf16[8,257,1280]{2,1,0:T(8,128)(2,1)} %copy.28.x_ref, bf16[8,257,1280]{2,1,0:T(8,128)(2,1)} %copy.29.c_ref, f32[1,1280]{1,0:T(1,128)} %reshape.240.gain_ref, f32[1,1280]{1,0:T(1,128)} %reshape.241.shift_ref), custom_call_target="tpu_custom_call" | custom-call | flops 1081344000 | bytes 26798080 | tf_op jit(solution)/shard_map/prepare/pallas_call | solution.py:61
  53.9 43.6 %all-gather.4.cloned.1.call-done.w_ref = bf16[1280,3840]{1,0:T(8,128)(2,1)} async-done(((bf16[80,3840]{1,0:T(8,128)(2,1)}), bf16[1280,3840]{1,0:T(8,128)(2,1)}) %all-gather.4.cloned.1.call-update) | async-done | bytes 9830416 | tf_op jit(solution)/shard_map/all_gather | solution.py:422
  97.5 27.1 %qkv.1.packed_ref = bf16[8,264,3840]{2,1,0:T(8,128)(2,1)} custom-call(bf16[1280,3840]{1,0:T(8,128)(2,1)} %all-gather.4.cloned.1.call-done.w_ref, bf16[8,264,1280]{2,1,0:T(8,128)(2,1)} %get-tuple-element.81.normed_ref, f32[1,3840]{1,0:T(1,128)} %fusion.bias_ref), custom_call_target="tpu_custom_call" | custom-call | flops 25952256000 | bytes 31472640 | tf_op jit(solution)/shard_map/qkv/pallas_call | solution.py:61
  128.6 48.0 %attention.1 = (bf16[8,264,1280]{2,1,0:T(8,128)(2,1)}, f32[8,16,264]{2,1,0:T(8,128)}) custom-call(bf16[8,264,3840]{2,1,0:T(8,128)(2,1)} %qkv.1.packed_ref), custom_call_target="tpu_custom_call" | custom-call | flops 3379200000 | bytes 21762048 | tf_op jit(solution)/shard_map/attention/pallas_call | solution.py:61
  176.6 46.3 %all-gather.8.cloned.1.call-done.w_ref.w_up_ref.w_out_ref = bf16[1280,6400]{1,0:T(8,128)(2,1)} async-done(((bf16[80,6400]{1,0:T(8,128)(2,1)}), bf16[1280,6400]{1,0:T(8,128)(2,1)}) %all-gather.8.cloned.1.call-update) | async-done | bytes 16384016 | tf_op jit(solution)/shard_map/all_gather | solution.py:422
  222.9 15.9 %out.1 = (f32[8,264,1280]{2,1,0:T(8,128)}, bf16[8,264,1280]{2,1,0:T(8,128)(2,1)}) custom-call(bf16[1280,6400]{1,0:T(8,128)(2,1)} %all-gather.8.cloned.1.call-done.w_ref.w_up_ref.w_out_ref, bf16[8,264,1280]{2,1,0:T(8,128)(2,1)} %get-tuple-element.84.x_ref, bf16[8,264,1280]{2,1,0:T(8,128)(2,1)} %get-tuple-element.85.mixed_ref, f32[1,1280]{1,0:T(1,128)} %reshape.243.bias_ref, ...), custom_call_target="tpu_custom_call" | custom-call | flops 10380902400 | bytes 43432960 | tf_op jit(solution)/shard_map/out/pallas_call | solution.py:61
  238.8 45.8 %up.1 = (bf16[8,264,5120]{2,1,0:T(8,128)(2,1)}, bf16[8,264,5120]{2,1,0:T(8,128)(2,1)}) custom-call(bf16[1280,6400]{1,0:T(8,128)(2,1)} %all-gather.8.cloned.1.call-done.w_ref.w_up_ref.w_out_ref, bf16[8,264,1280]{2,1,0:T(8,128)(2,1)} %get-tuple-element.86.normed_ref, f32[1,5120]{1,0:T(1,128)} %reshape.246.bias_ref), custom_call_target="tpu_custom_call" | custom-call | flops 55364812800 | bytes 65064960 | tf_op jit(solution)/shard_map/up/pallas_call | solution.py:61
  284.6 37.0 %g_down.1 = (bf16[8,320,1280]{2,1,0:T(8,128)(2,1)}, bf16[4,320,1280]{2,1,0:T(8,128)(2,1)}, bf16[4,320,1280]{2,1,0:T(8,128)(2,1)}) custom-call(s32[2]{0:T(128)} %pad_add_fusion.refs_0_, bf16[2112,5120]{1,0:T(8,128)(2,1)} %bitcast.62, bf16[2112,1280]{1,0:T(8,128)(2,1)} %bitcast.59), custom_call_target="tpu_custom_call" | custom-call | flops 34603008000 | bytes 40140800 | tf_op jit(solution)/shard_map/g_down/pallas_call | solution.py:352
  322.7 11.4 %all-gather.6.cloned.1.call-done.w_ref = bf16[5120,1280]{1,0:T(8,128)(2,1)} async-done(((bf16[320,1280]{1,0:T(8,128)(2,1)}), bf16[5120,1280]{1,0:T(8,128)(2,1)}) %all-gather.6.cloned.1.call-update) | async-done | bytes 13107216 | tf_op jit(solution)/shard_map/all_gather | solution.py:422
  334.1 42.3 %down.1 = f32[2056,1280]{1,0:T(8,128)} custom-call(bf16[5120,1280]{1,0:T(8,128)(2,1)} %all-gather.6.cloned.1.call-done.w_ref, bf16[8,264,5120]{2,1,0:T(8,128)(2,1)} %get-tuple-element.92.active_ref, f32[8,264,1280]{2,1,0:T(8,128)} %get-tuple-element.93.hidden_ref, f32[1,1280]{1,0:T(1,128)} %reshape.247.bias_ref), custom_call_target="tpu_custom_call" | custom-call | flops 34603008000 | bytes 56079360 | tf_op jit(solution)/shard_map/down/pallas_call | solution.py:61
  382.1 37.6 %down_back.1 = (bf16[8,264,5120]{2,1,0:T(8,128)(2,1)}, f32[8,5120]{1,0:T(8,128)}) custom-call(bf16[5120,1280]{1,0:T(8,128)(2,1)} %all-gather.6.cloned.1.call-done.w_ref, bf16[8,264,1280]{2,1,0:T(8,128)(2,1)} %get-tuple-element.95.c_ref, bf16[8,264,5120]{2,1,0:T(8,128)(2,1)} %get-tuple-element.96.slope_ref), custom_call_target="tpu_custom_call" | custom-call | flops 41523609600 | bytes 61931520 | tf_op jit(solution)/shard_map/down_back/pallas_call | solution.py:61
  419.7 21.2 %g_up_low.1 = (bf16[8,80,2560]{2,1,0:T(8,128)(2,1)}, bf16[4,80,2560]{2,1,0:T(8,128)(2,1)}, bf16[4,80,2560]{2,1,0:T(8,128)(2,1)}) custom-call(s32[2]{0:T(128)} %pad_add_fusion.refs_0_, bf16[2112,1280]{1,0:T(8,128)(2,1)} %bitcast.65, bf16[2112,5120]{1,0:T(8,128)(2,1)} %bitcast.60), custom_call_target="tpu_custom_call" | custom-call | flops 17301504000 | bytes 33587200 | tf_op jit(solution)/shard_map/g_up_low/pallas_call | solution.py:352
  441.0 21.4 %g_up_high.1 = (bf16[8,80,2560]{2,1,0:T(8,128)(2,1)}, bf16[4,80,2560]{2,1,0:T(8,128)(2,1)}, bf16[4,80,2560]{2,1,0:T(8,128)(2,1)}) custom-call(s32[2]{0:T(128)} %pad_add_fusion.refs_0_, bf16[2112,1280]{1,0:T(8,128)(2,1)} %bitcast.66, bf16[2112,5120]{1,0:T(8,128)(2,1)} %bitcast.61), custom_call_target="tpu_custom_call" | custom-call | flops 17301504000 | bytes 33587200 | tf_op jit(solution)/shard_map/g_up_high/pallas_call | solution.py:352
  462.9 6.8 add_convert_fusion
  475.6 58.6 %up_back.1 = (f32[8,264,1280]{2,1,0:T(8,128)}, bf16[8,264,1280]{2,1,0:T(8,128)(2,1)}, bf16[8,264,1280]{2,1,0:T(8,128)(2,1)}, f32[8,1280]{1,0:T(8,128)}, f32[8,1280]{1,0:T(8,128)}, /*index=5*/f32[8,1280]{1,0:T(8,128)}) custom-call(bf16[1280,6400]{1,0:T(8,128)(2,1)} %all-gather.8.cloned.1.call-done.w_ref.w_up_ref.w_out_ref, ...), custom_call_target="tpu_custom_call" | custom-call | flops 51904512000 | bytes 92369920 | tf_op jit(solution)/shard_map/up_back/pallas_call | solution.py:61
  537.9 13.0 %g_out.1 = (bf16[8,80,1280]{2,1,0:T(8,128)(2,1)}, bf16[4,80,1280]{2,1,0:T(8,128)(2,1)}, bf16[4,80,1280]{2,1,0:T(8,128)(2,1)}) custom-call(s32[2]{0:T(128)} %pad_add_fusion.refs_0_, bf16[2112,1280]{1,0:T(8,128)(2,1)} %bitcast.40, bf16[2112,1280]{1,0:T(8,128)(2,1)} %bitcast.67), custom_call_target="tpu_custom_call" | custom-call | flops 8650752000 | bytes 14090240 | tf_op jit(solution)/shard_map/g_out/pallas_call | solution.py:352
  560.4 62.7 %attention_back.1 = (bf16[8,264,3840]{2,1,0:T(8,128)(2,1)}, f32[8,2560]{1,0:T(8,128)}) custom-call(bf16[8,264,3840]{2,1,0:T(8,128)(2,1)} %qkv.1.packed_ref, bf16[8,264,1280]{2,1,0:T(8,128)(2,1)} %get-tuple-element.85.mixed_ref, bf16[8,264,1280]{2,1,0:T(8,128)(2,1)} %get-tuple-element.116.dmixed_ref, f32[8,16,264]{2,1,0:T(8,128)} %get-tuple-element.117.lse_ref), custom_call_target="tpu_custom_call" | custom-call | flops 4730880000 | bytes 43470848 | tf_op jit(solution)/shard_map/attention_back/pallas_call | solution.py:61
  628.5 21.3 %g_qk.1 = (bf16[8,80,2560]{2,1,0:T(8,128)(2,1)}, bf16[4,80,2560]{2,1,0:T(8,128)(2,1)}, bf16[4,80,2560]{2,1,0:T(8,128)(2,1)}) custom-call(s32[2]{0:T(128)} %pad_add_fusion.refs_0_, bf16[2112,1280]{1,0:T(8,128)(2,1)} %bitcast.57, bf16[2112,3840]{1,0:T(8,128)(2,1)} %bitcast.55), custom_call_target="tpu_custom_call" | custom-call | flops 17301504000 | bytes 28180480 | tf_op jit(solution)/shard_map/g_qk/pallas_call | solution.py:352
  649.8 12.9 %g_v.1 = (bf16[8,80,1280]{2,1,0:T(8,128)(2,1)}, bf16[4,80,1280]{2,1,0:T(8,128)(2,1)}, bf16[4,80,1280]{2,1,0:T(8,128)(2,1)}) custom-call(s32[2]{0:T(128)} %pad_add_fusion.refs_0_, bf16[2112,1280]{1,0:T(8,128)(2,1)} %bitcast.58, bf16[2112,3840]{1,0:T(8,128)(2,1)} %bitcast.56), custom_call_target="tpu_custom_call" | custom-call | flops 8650752000 | bytes 24903680 | tf_op jit(solution)/shard_map/g_v/pallas_call | solution.py:352
  668.9 8.9 %reduce-scatter.10.cloned.1.call-done = bf16[1,80,3840]{2,1,0:T(8,128)(2,1)} async-done(((bf16[4,80,3840]{2,1,0:T(8,128)(2,1)}), bf16[1,80,3840]{2,1,0:T(8,128)(2,1)}) %reduce-scatter.10.cloned.1.call-update) | async-done | bytes 614416 | tf_op jit(solution)/shard_map/reduce_scatter | solution.py:455
  677.8 41.4 %qkv_back.1 = (f32[2056,1280]{1,0:T(8,128)}, f32[8,1280]{1,0:T(8,128)}, f32[8,1280]{1,0:T(8,128)}) custom-call(bf16[1280,3840]{1,0:T(8,128)(2,1)} %all-gather.4.cloned.1.call-done.w_ref, bf16[8,264,3840]{2,1,0:T(8,128)(2,1)} %get-tuple-element.129.dpacked_ref, bf16[8,264,1280]{2,1,0:T(8,128)(2,1)} %get-tuple-element.84.x_ref, ...), custom_call_target="tpu_custom_call" | custom-call | flops 31142707200 | bytes 52884480 | tf_op jit(solution)/shard_map/qkv_back/pallas_call | solution.py:61
  727.6 14.3 %collective-permute-done.15 = bf16[4,80,1280]{2,1,0:T(8,128)(2,1)} collective-permute-done((bf16[4,80,1280]{2,1,0:T(8,128)(2,1)}, bf16[4,80,1280]{2,1,0:T(8,128)(2,1)}, u32[]{:S(2)}, u32[]{:S(2)}) %collective-permute-start.15) | collective-permute-done | bytes 819232 | tf_op jit(solution)/shard_map/ppermute | solution.py:448
  756.6 9.7 %collective-permute-done.19 = bf16[320,1280]{1,0:T(8,128)(2,1)S(1)} collective-permute-done((bf16[320,1280]{1,0:T(8,128)(2,1)S(1)}, bf16[320,1280]{1,0:T(8,128)(2,1)S(1)}, u32[]{:S(2)}, u32[]{:S(2)}) %collective-permute-start.19) | collective-permute-done | bytes 819232 | tf_op jit(solution)/shard_map/ppermute | solution.py:383
  785.1 11.6 %collective-permute-done.17 = bf16[80,3840]{1,0:T(8,128)(2,1)S(1)} collective-permute-done((bf16[80,3840]{1,0:T(8,128)(2,1)S(1)}, bf16[80,3840]{1,0:T(8,128)(2,1)S(1)}, u32[]{:S(2)}, u32[]{:S(2)}) %collective-permute-start.17) | collective-permute-done | bytes 614432 | tf_op jit(solution)/shard_map/ppermute | solution.py:383
  (191 shorter events, 128.2 us)
Async XLA Ops:
  7.2 90.3 %all-gather.4.cloned.1.call-start = ((), (), s32[]{:S(2)}) async-start(), calls=%async_computation.5 | async-start | bytes 10444800 | tf_op jit(solution)/shard_map/all_gather | solution.py:422
  7.9 215.0 %all-gather.8.cloned.1.call-start = ((), (), s32[]{:S(2)}) async-start(), calls=%async_computation.7 | async-start | bytes 17408000 | tf_op jit(solution)/shard_map/all_gather | solution.py:422
  23.2 14.9 %collective-permute-start.3 = (bf16[8,960]{1,0:T(8,128)(2,1)S(1)}, bf16[8,960]{1,0:T(8,128)(2,1)S(1)}, u32[]{:S(2)}, u32[]{:S(2)}) collective-permute-start(bf16[8,960]{1,0:T(8,128)(2,1)S(1)} %pad_maximum_fusion.6), channel_id=1, source_target_pairs={{0,8},{4,12},{8,0},{12,4},{1,9},{5,13},{9,1},{13,5},{2,10},{6,14},... | collective-permute-start | bytes 46088 | tf_op jit(solution)/shard_map/ppermute | solution.py:428
  53.1 281.0 %all-gather.6.cloned.1.call-start = ((), (), s32[]{:S(2)}) async-start(), calls=%async_computation.6 | async-start | bytes 13926400 | tf_op jit(solution)/shard_map/all_gather | solution.py:422
  124.7 413.2 %reduce-scatter.6.cloned.1.call-start = ((), (), s32[]{:S(2)}) async-start(), calls=%async_computation.8 | async-start | bytes 4096000 | tf_op jit(solution)/shard_map/reduce_scatter | solution.py:455
  321.7 54.7 %collective-permute-start.4 = (bf16[8,320,1280]{2,1,0:T(8,128)(2,1)}, bf16[8,320,1280]{2,1,0:T(8,128)(2,1)}, u32[]{:S(2)}, u32[]{:S(2)}) collective-permute-start(bf16[8,320,1280]{2,1,0:T(8,128)(2,1)} %get-tuple-element.89), channel_id=1, source_target_pairs={{0,1},{1,0},{2,3},{3,2},{4,5},{5,4},{6,7},{7,6},{8,9},{9,8},{10,11... | collective-permute-start | bytes 19660808 | tf_op jit(solution)/shard_map/ppermute | solution.py:442
  381.4 81.5 %collective-permute-start.6 = (bf16[4,320,1280]{2,1,0:T(8,128)(2,1)}, bf16[4,320,1280]{2,1,0:T(8,128)(2,1)}, u32[]{:S(2)}, u32[]{:S(2)}) collective-permute-start(bf16[4,320,1280]{2,1,0:T(8,128)(2,1)} %slice_add_fusion), channel_id=1, source_target_pairs={{0,2},{2,0},{1,3},{3,1},{4,6},{6,4},{5,7},{7,5},{8,10},{10,8},{9,1... | collective-permute-start | bytes 9830408 | tf_op jit(solution)/shard_map/ppermute | solution.py:448
  440.9 28.8 %collective-permute-start.5 = (bf16[8,80,2560]{2,1,0:T(8,128)(2,1)}, bf16[8,80,2560]{2,1,0:T(8,128)(2,1)S(1)}, u32[]{:S(2)}, u32[]{:S(2)}) collective-permute-start(bf16[8,80,2560]{2,1,0:T(8,128)(2,1)} %get-tuple-element.98), channel_id=1, source_target_pairs={{0,1},{1,0},{2,3},{3,2},{4,5},{5,4},{6,7},{7,6},{8,9},{9,8},{10,11... | collective-permute-start | bytes 9830408 | tf_op jit(solution)/shard_map/ppermute | solution.py:442
  462.4 88.6 %collective-permute-start.8 = (bf16[8,80,2560]{2,1,0:T(8,128)(2,1)}, bf16[8,80,2560]{2,1,0:T(8,128)(2,1)}, u32[]{:S(2)}, u32[]{:S(2)}) collective-permute-start(bf16[8,80,2560]{2,1,0:T(8,128)(2,1)} %get-tuple-element.102), channel_id=1, source_target_pairs={{0,1},{1,0},{2,3},{3,2},{4,5},{5,4},{6,7},{7,6},{8,9},{9,8},{10,11... | collective-permute-start | bytes 9830408 | tf_op jit(solution)/shard_map/ppermute | solution.py:442
  469.7 158.8 %reduce-scatter.8.cloned.1.call-start = ((), (), s32[]{:S(2)}) async-start(), calls=%async_computation.9 | async-start | bytes 2048000 | tf_op jit(solution)/shard_map/reduce_scatter | solution.py:455
  474.3 59.9 %collective-permute-start.7 = (bf16[4,80,2560]{2,1,0:T(8,128)(2,1)}, bf16[4,80,2560]{2,1,0:T(8,128)(2,1)}, u32[]{:S(2)}, u32[]{:S(2)}) collective-permute-start(bf16[4,80,2560]{2,1,0:T(8,128)(2,1)} %slice_add_fusion.3), channel_id=1, source_target_pairs={{0,2},{2,0},{1,3},{3,1},{4,6},{6,4},{5,7},{7,5},{8,10},{10,8},{9,1... | collective-permute-start | bytes 4915208 | tf_op jit(solution)/shard_map/ppermute | solution.py:448
  556.4 66.7 %collective-permute-start.10 = (bf16[4,80,3840]{2,1,0:T(8,128)(2,1)}, bf16[4,80,3840]{2,1,0:T(8,128)(2,1)}, u32[]{:S(2)}, u32[]{:S(2)}) collective-permute-start(bf16[4,80,3840]{2,1,0:T(8,128)(2,1)} %pad_maximum_fusion.1), channel_id=1, source_target_pairs={{0,2},{2,0},{1,3},{3,1},{4,6},{6,4},{5,7},{7,5},{8,10},{10,8},{9,1... | collective-permute-start | bytes 7372808 | tf_op jit(solution)/shard_map/ppermute | solution.py:448
  557.3 120.5 %reduce-scatter.10.cloned.1.call-start = ((), (), s32[]{:S(2)}) async-start(), calls=%async_computation.10 | async-start | bytes 3072000 | tf_op jit(solution)/shard_map/reduce_scatter | solution.py:455
  628.4 140.8 %reduce-scatter.12.cloned.1.call-start = ((), (), s32[]{:S(2)}) async-start(), calls=%async_computation.11 | async-start | bytes 2048000 | tf_op jit(solution)/shard_map/reduce_scatter | solution.py:455
  649.8 13.5 %collective-permute-start.11 = (bf16[8,80,2560]{2,1,0:T(8,128)(2,1)}, bf16[8,80,2560]{2,1,0:T(8,128)(2,1)S(1)}, u32[]{:S(2)}, u32[]{:S(2)}) collective-permute-start(bf16[8,80,2560]{2,1,0:T(8,128)(2,1)} %get-tuple-element.121), channel_id=1, source_target_pairs={{0,1},{1,0},{2,3},{3,2},{4,5},{5,4},{6,7},{7,6},{8,9},{9,8},{10,11... | collective-permute-start | bytes 9830408 | tf_op jit(solution)/shard_map/ppermute | solution.py:442
  662.8 56.4 %collective-permute-start.14 = (bf16[8,80,1280]{2,1,0:T(8,128)(2,1)}, bf16[8,80,1280]{2,1,0:T(8,128)(2,1)}, u32[]{:S(2)}, u32[]{:S(2)}) collective-permute-start(bf16[8,80,1280]{2,1,0:T(8,128)(2,1)} %get-tuple-element.125), channel_id=1, source_target_pairs={{0,1},{1,0},{2,3},{3,2},{4,5},{5,4},{6,7},{7,6},{8,9},{9,8},{10,11... | collective-permute-start | bytes 4915208 | tf_op jit(solution)/shard_map/ppermute | solution.py:442
  667.8 55.5 %collective-permute-start.12 = (bf16[4,80,2560]{2,1,0:T(8,128)(2,1)}, bf16[4,80,2560]{2,1,0:T(8,128)(2,1)S(1)}, u32[]{:S(2)}, u32[]{:S(2)}) collective-permute-start(bf16[4,80,2560]{2,1,0:T(8,128)(2,1)} %slice_add_fusion.1), channel_id=1, source_target_pairs={{0,2},{2,0},{1,3},{3,1},{4,6},{6,4},{5,7},{7,5},{8,10},{10,8},{9,1... | collective-permute-start | bytes 4915208 | tf_op jit(solution)/shard_map/ppermute | solution.py:448
  721.7 20.2 %collective-permute-start.15 = (bf16[4,80,1280]{2,1,0:T(8,128)(2,1)}, bf16[4,80,1280]{2,1,0:T(8,128)(2,1)}, u32[]{:S(2)}, u32[]{:S(2)}) collective-permute-start(bf16[4,80,1280]{2,1,0:T(8,128)(2,1)} %slice_add_fusion.4), channel_id=1, source_target_pairs={{0,2},{2,0},{1,3},{3,1},{4,6},{6,4},{5,7},{7,5},{8,10},{10,8},{9,1... | collective-permute-start | bytes 2457608 | tf_op jit(solution)/shard_map/ppermute | solution.py:448
  726.5 74.2 %reduce-scatter.14.cloned.1.call-start = ((), (), s32[]{:S(2)}) async-start(), calls=%async_computation.12 | async-start | bytes 1024000 | tf_op jit(solution)/shard_map/reduce_scatter | solution.py:455
  745.2 21.1 %collective-permute-start.19 = (bf16[320,1280]{1,0:T(8,128)(2,1)S(1)}, bf16[320,1280]{1,0:T(8,128)(2,1)S(1)}, u32[]{:S(2)}, u32[]{:S(2)}) collective-permute-start(bf16[320,1280]{1,0:T(8,128)(2,1)S(1)} %bitcast.43), channel_id=1, source_target_pairs={{0,16},{16,0},{1,17},{17,1},{2,18},{18,2},{3,19},{19,3},{4,20},{20... | collective-permute-start | bytes 2457608 | tf_op jit(solution)/shard_map/ppermute | solution.py:383
  753.0 22.1 %collective-permute-start.18 = (bf16[80,2560]{1,0:T(8,128)(2,1)S(1)}, bf16[80,2560]{1,0:T(8,128)(2,1)S(1)}, u32[]{:S(2)}, u32[]{:S(2)}) collective-permute-start(bf16[80,2560]{1,0:T(8,128)(2,1)S(1)} %bitcast.47), channel_id=1, source_target_pairs={{0,16},{16,0},{1,17},{17,1},{2,18},{18,2},{3,19},{19,3},{4,20},{20... | collective-permute-start | bytes 1228808 | tf_op jit(solution)/shard_map/ppermute | solution.py:383
  756.6 11.1 %collective-permute-start.23 = (f32[1,960]{1,0:T(1,128)S(1)}, f32[1,960]{1,0:T(1,128)S(1)}, u32[]{:S(2)}, u32[]{:S(2)}) collective-permute-start(f32[1,960]{1,0:T(1,128)S(1)} %constant_dynamic-slice_fusion), channel_id=1, source_target_pairs={{0,4},{4,0},{8,12},{12,8},{1,5},{5,1},{9,13},{13,9},{2,6},{6,2},{1... | collective-permute-start | bytes 11528 | tf_op jit(solution)/shard_map/ppermute | solution.py:471
  769.2 14.8 %collective-permute-start.13 = (bf16[80,2560]{1,0:T(8,128)(2,1)}, bf16[80,2560]{1,0:T(8,128)(2,1)S(1)}, u32[]{:S(2)}, u32[]{:S(2)}) collective-permute-start(bf16[80,2560]{1,0:T(8,128)(2,1)} %bitcast.49), channel_id=1, source_target_pairs={{0,16},{16,0},{1,17},{17,1},{2,18},{18,2},{3,19},{19,3},{4,20},{20... | collective-permute-start | bytes 1228808 | tf_op jit(solution)/shard_map/ppermute | solution.py:383
  777.1 19.6 %collective-permute-start.17 = (bf16[80,3840]{1,0:T(8,128)(2,1)S(1)}, bf16[80,3840]{1,0:T(8,128)(2,1)S(1)}, u32[]{:S(2)}, u32[]{:S(2)}) collective-permute-start(bf16[80,3840]{1,0:T(8,128)(2,1)S(1)} %bitcast.45), channel_id=1, source_target_pairs={{0,16},{16,0},{1,17},{17,1},{2,18},{18,2},{3,19},{19,3},{4,20},{20... | collective-permute-start | bytes 1843208 | tf_op jit(solution)/shard_map/ppermute | solution.py:383
  (30 other events, 278.2 us)
Sparse Core Ops, SparseCore 0:
  10.3 87.1 all-gather.3
  100.4 122.5 all-gather.7
  225.2 108.8 all-gather.5
  469.8 61.6 reduce-scatter.5
  557.4 35.9 reduce-scatter.7
  628.5 49.1 reduce-scatter.9
  726.6 35.1 reduce-scatter.11
  777.2 23.4 reduce-scatter.13

commit v3 on v2

--- a/solution.py
+++ b/solution.py
@@ -231,40 +231,66 @@
 
 
 def attention_back_kernel(packed_ref, mixed_ref, dmixed_ref, lse_ref, dpacked_ref, sum_ref):
+    full = SEQ - 1
+
     @pl.when(pl.program_id(0) == 0)
     def _():
         sum_ref[...] = jnp.zeros_like(sum_ref)
 
     def group(g, carry):
         base = g * GW
-        here = pl.ds(pl.multiple_of(base, 128), GW)
         queries, keys, values = [
             packed_ref[0, :, pl.ds(pl.multiple_of(part * D + base, 128), GW)] for part in range(3)]
+        here = pl.ds(pl.multiple_of(base, 128), GW)
         grads = dmixed_ref[0, :, here]
-        product = (grads.astype(F32) * mixed_ref[0, :, here].astype(F32)).T
-        keys_t = keys.astype(F32).T.astype(BF)
+        product = grads.astype(F32) * mixed_ref[0, :, here].astype(F32)
+        product_t = product[:full].T
+        keys_t = keys.astype(F32).T
+        keys_tb = keys_t[:, :full].astype(BF)
         lse = lse_ref[0, pl.ds(pl.multiple_of(g * GROUP, 8), GROUP), :]
         dq, dk, dv = [], [], []
         for j in range(GROUP):
             head = slice(j * HD, (j + 1) * HD)
-            q, k, v, dm = queries[:, head], keys[:, head], values[:, head], grads[:, head]
-            delta = jnp.sum(product[head], 0, keepdims=True)
-            p = drop_tail(jnp.exp(dot_nt(k, q) * SCALE - lse[j:j + 1]))
+            q, k, v, dm = queries[:full, head], keys[:, head], values[:, head], grads[:full, head]
+            delta = jnp.sum(product_t[head], 0, keepdims=True)
+            p = drop_tail(jnp.exp(dot_nt(k, q) * SCALE - lse[j:j + 1, :full]))
             dv.append(dot_nn(p.astype(BF), dm))
             ds = (p * (dot_nt(v, dm) - delta) * SCALE).astype(BF)
             dk.append(dot_nn(ds, q))
-            dq.append(dot_nn(keys_t[head], ds))
+            dq.append(dot_nn(keys_tb[head], ds[:full])
+                      + keys_t[head, full:full + 1] * ds[full:].astype(F32)[:1])
         dq = jnp.concatenate(dq, 0).T
         dk = jnp.concatenate(dk, 1)
         dv = jnp.concatenate(dv, 1)
+
+        head_row = lax.broadcasted_iota(jnp.int32, (GROUP, GW), 0)
+        lane = lax.broadcasted_iota(jnp.int32, (GROUP, GW), 1)
+        mine = jnp.logical_and(lane >= head_row * HD, lane < (head_row + 1) * HD)
+        diagonal = lax.broadcasted_iota(jnp.int32, (GROUP, GROUP), 0) == lax.broadcasted_iota(jnp.int32, (GROUP, GROUP), 1)
+
+        def spread(rows):
+            return jnp.where(mine, rows[full:].astype(F32)[:1], 0.0)
+
+        def as_row(column):
+            return jnp.sum(jnp.where(diagonal, column, 0.0), 0, keepdims=True)
+        q, dm = spread(queries).astype(BF), spread(grads).astype(BF)
+        delta = as_row(jnp.sum(spread(product), 1, keepdims=True))
+        p = drop_tail(jnp.exp(dot_nt(keys, q) * SCALE - as_row(lse[:, full:full + 1])))
+        ds = p * (dot_nt(values, dm) - delta) * SCALE
+        dv = dv + dot_nn(p.astype(BF), dm)
+        dk = dk + dot_nn(ds.astype(BF), q)
+        ds_t = jnp.concatenate([ds, jnp.zeros((SP, 128 - GROUP), F32)], 1).T[:GROUP].astype(BF)
+        dq_last = jnp.sum(jnp.where(mine, dot_nn(ds_t, keys), 0.0), 0, keepdims=True)
+        tail = lax.broadcasted_iota(jnp.int32, (SP - full, GW), 0) == 0
+        dq_last = jnp.where(tail, dq_last, 0.0)
+
         def out(part):
             return pl.ds(pl.multiple_of(part * D + base, 128), GW)
-        keep = lax.broadcasted_iota(jnp.int32, dq.shape, 0) < SEQ
-        dq = jnp.where(keep, dq, 0.0)
-        dpacked_ref[0, :, out(0)] = dq.astype(BF)
+        dpacked_ref[0, :full, out(0)] = dq.astype(BF)
+        dpacked_ref[0, full:, out(0)] = dq_last.astype(BF)
         dpacked_ref[0, :, out(1)] = dk.astype(BF)
         dpacked_ref[0, :, out(2)] = dv.astype(BF)
-        sum_ref[:, out(0)] += fold_rows(dq)
+        sum_ref[:, out(0)] += fold_rows(dq) + dq_last
         sum_ref[:, out(1)] += fold_rows(dv)
         return carry
     lax.fori_loop(0, H // GROUP, group, 0)
@@ -570,24 +596,18 @@
         [rows(SP, 3 * D), sums(2 * D)], "attention_back", 1.4e5 * n * SP * H)
     g_down = both_groups(after(p_down, d_packed))
     rest = links.second_stage(rest, d_packed)
-    p_qk = gradient(normed_one, after(d_packed, rest, p_up), "g_qk", 0, 2 * D)
+    last = gradient(normed_one, after(d_packed, rest, p_up), "g_qkv")
     rest = links.third_stage(rest)
-    p_v = gradient(normed_one, after(d_packed, p_qk), "g_v", 2 * D, D)
-    p_qk = links.first_stage(p_qk, p_v)
+    last = links.first_stage(last)
     d_images, s_gain_one, s_shift_one = call(
         qkv_back_kernel, n,
-        [whole(full_qkv), image(after(d_packed, p_v, p_qk[0], rest)), image(xpad), image(d_hidden), whole(gain_one)],
+        [whole(full_qkv), image(after(d_packed, last[0])), image(xpad), image(d_hidden), whole(gain_one)],
         [untouched(sds(SEQ * n, D, dtype=F32)), sums(D), sums(D)], "qkv_back", 3 * D * 3 * D * n * SP, staging)
-    g_up = both_groups(after(p_up, p_qk[0]))
-    p_v = links.first_stage(p_v, d_images)
-    p_qk = links.second_stage(p_qk, d_images)
-    p_v = links.second_stage(p_v, d_images, p_qk)
-    p_qk = links.third_stage(p_qk)
-    s_gain_one = after(s_gain_one, p_v)
-    rest = both_groups(after(rest, p_qk))
+    g_up = both_groups(after(p_up, last[0]))
+    last = links.second_stage(last, d_images, rest)
+    rest, s_gain_one = after((rest, s_gain_one), last)
+    rest, g_qkv = both_groups(rest), both_groups(links.third_stage(last))
     g_up2, g_out = rest[:, :FF // 2], rest[:, FF // 2:]
-    p_v = links.third_stage(after(p_v, p_qk))
-    g_qk, g_v = both_groups(p_qk), both_groups(p_v)
     result, d_images = [jnp.transpose(a.reshape(SEQ, n, D), (1, 0, 2)) for a in (result, d_images)]
     g_up = jnp.concatenate([g_up, g_up2], 1)
 
@@ -597,7 +617,7 @@
     for size in sizes:
         small_grads.append(share[first:first + size])
         first += size
-    return (result, d_images, jnp.concatenate([g_qk, g_v], 1), g_out, g_up, g_down, *small_grads)
+    return (result, d_images, g_qkv, g_out, g_up, g_down, *small_grads)
 
 
 def solution(mesh):

time: 821 us -> 801 us (0.976)
  Pallas kernels: 520 us -> 506 us
    ppermute x1, waiting for transfers between devices: 0.01 us -> 12.7 us  [scatter_small(): return shares + lax.ppermute(shares, 'dp', SWAP)]
    pallas_call x10, Pallas kernels: 393 us -> 384 us  [grid_call(): pl.pallas_call(kernel, grid=grid, in_specs=[spec for _, spec in ins], out...]
    ppermute x6 -> x5, waiting for transfers between devices: 2.04 us -> 10.5 us  [first_stage(): got = lax.ppermute(send, 'core', SWAP)]
    ppermute x5 -> x4, waiting for transfers between devices: 33.8 us -> 27.8 us  [both_groups(): return shard.astype(F32) + lax.ppermute(shard, 'dp', SWAP).astype(F32)]
    pallas_call x6 -> x5, Pallas kernels: 127 us -> 122 us  [weight_gradient(): pl.pallas_call(kernel, grid=(left.shape[1] // block, width // cols), in_s...]
    convert_element_type x5 -> x4, other arithmetic: 21.8 us -> 21.2 us  [second_stage(): (keep.astype(F32) + got[:half].astype(F32) + got_x.astype(F32)).astype(BF)]
  transfers between devices with their start and end apart: 33 -> 29, of which waited for: 17 -> 16; matrix products, arithmetic and copies ran while one was open for 8% -> 7% of each run, Pallas kernels for 64% -> 60%
where the time goes in v3:
time: 801 us; the launch traced here: 795 us
  Pallas kernels  506 us (63%)
  waiting for transfers between devices  179 us (22%)
  other arithmetic  46.8 us (6%)
  local copies, waits for them, and re-layouts  25.3 us (3%)
  starting transfers between devices  23.5 us (3%)
  between operations  14.9 us (2%)
    pallas_call x10, Pallas kernels, grid_call(): pl.pallas_call(kernel, grid=grid, in_specs=[spec for _, spec in ins], out...  384 us
    pallas_call x5, Pallas kernels, weight_gradient(): pl.pallas_call(kernel, grid=(left.shape[1] // block, width // cols), in_s...  122 us
    all_gather x3, waiting for transfers between devices, gather(): return lax.all_gather(w, ('z', 'x', 'core'), axis=0, tiled=True)  101 us
    ppermute x4, waiting for transfers between devices, both_groups(): return shard.astype(F32) + lax.ppermute(shard, 'dp', SWAP).astype(F32)  27.8 us
    convert_element_type x4, other arithmetic, second_stage(): (keep.astype(F32) + got[:half].astype(F32) + got_x.astype(F32)).astype(BF)  21.2 us
  transfers between devices with their start and end apart: 29, of which 16 were waited for; matrix products, arithmetic and copies ran while one was open for 7% of the time, Pallas kernels for 60%

profile of v3, /device:TPU:0, one launch (start us, length us, event | category | flops | bytes accessed | tf_op | source)
XLA Modules:
  0.0 795.2 jit_solution(7619318760138423282)
XLA Ops:
  39.5 13.5 %prepare.1 = (bf16[8,264,1280]{2,1,0:T(8,128)(2,1)}, bf16[8,264,1280]{2,1,0:T(8,128)(2,1)}, bf16[8,264,1280]{2,1,0:T(8,128)(2,1)}, f32[8,1280]{1,0:T(8,128)}) custom-call(bf16[8,257,1280]{2,1,0:T(8,128)(2,1)} %copy.28.x_ref, bf16[8,257,1280]{2,1,0:T(8,128)(2,1)} %copy.29.c_ref, f32[1,1280]{1,0:T(1,128)} %reshape.235.gain_ref, f32[1,1280]{1,0:T(1,128)} %reshape.236.shift_ref), custom_call_target="tpu_custom_call" | custom-call | flops 1081344000 | bytes 26798080 | tf_op jit(solution)/shard_map/prepare/pallas_call | solution.py:61
  53.9 43.6 %all-gather.4.cloned.1.call-done.w_ref = bf16[1280,3840]{1,0:T(8,128)(2,1)} async-done(((bf16[80,3840]{1,0:T(8,128)(2,1)}), bf16[1280,3840]{1,0:T(8,128)(2,1)}) %all-gather.4.cloned.1.call-update) | async-done | bytes 9830416 | tf_op jit(solution)/shard_map/all_gather | solution.py:448
  97.5 27.2 %qkv.1.packed_ref = bf16[8,264,3840]{2,1,0:T(8,128)(2,1)} custom-call(bf16[1280,3840]{1,0:T(8,128)(2,1)} %all-gather.4.cloned.1.call-done.w_ref, bf16[8,264,1280]{2,1,0:T(8,128)(2,1)} %get-tuple-element.73.normed_ref, f32[1,3840]{1,0:T(1,128)} %fusion.bias_ref), custom_call_target="tpu_custom_call" | custom-call | flops 25952256000 | bytes 31472640 | tf_op jit(solution)/shard_map/qkv/pallas_call | solution.py:61
  128.7 48.0 %attention.1 = (bf16[8,264,1280]{2,1,0:T(8,128)(2,1)}, f32[8,16,264]{2,1,0:T(8,128)}) custom-call(bf16[8,264,3840]{2,1,0:T(8,128)(2,1)} %qkv.1.packed_ref), custom_call_target="tpu_custom_call" | custom-call | flops 3379200000 | bytes 21762048 | tf_op jit(solution)/shard_map/attention/pallas_call | solution.py:61
  176.7 46.2 %all-gather.8.cloned.1.call-done.w_ref.w_up_ref.w_out_ref = bf16[1280,6400]{1,0:T(8,128)(2,1)} async-done(((bf16[80,6400]{1,0:T(8,128)(2,1)}), bf16[1280,6400]{1,0:T(8,128)(2,1)}) %all-gather.8.cloned.1.call-update) | async-done | bytes 16384016 | tf_op jit(solution)/shard_map/all_gather | solution.py:448
  222.9 15.9 %out.1 = (f32[8,264,1280]{2,1,0:T(8,128)}, bf16[8,264,1280]{2,1,0:T(8,128)(2,1)}) custom-call(bf16[1280,6400]{1,0:T(8,128)(2,1)} %all-gather.8.cloned.1.call-done.w_ref.w_up_ref.w_out_ref, bf16[8,264,1280]{2,1,0:T(8,128)(2,1)} %get-tuple-element.76.x_ref, bf16[8,264,1280]{2,1,0:T(8,128)(2,1)} %get-tuple-element.77.mixed_ref, f32[1,1280]{1,0:T(1,128)} %reshape.238.bias_ref, ...), custom_call_target="tpu_custom_call" | custom-call | flops 10380902400 | bytes 43432960 | tf_op jit(solution)/shard_map/out/pallas_call | solution.py:61
  238.8 45.8 %up.1 = (bf16[8,264,5120]{2,1,0:T(8,128)(2,1)}, bf16[8,264,5120]{2,1,0:T(8,128)(2,1)}) custom-call(bf16[1280,6400]{1,0:T(8,128)(2,1)} %all-gather.8.cloned.1.call-done.w_ref.w_up_ref.w_out_ref, bf16[8,264,1280]{2,1,0:T(8,128)(2,1)} %get-tuple-element.78.normed_ref, f32[1,5120]{1,0:T(1,128)} %reshape.241.bias_ref), custom_call_target="tpu_custom_call" | custom-call | flops 55364812800 | bytes 65064960 | tf_op jit(solution)/shard_map/up/pallas_call | solution.py:61
  284.7 37.0 %g_down.1 = (bf16[8,320,1280]{2,1,0:T(8,128)(2,1)}, bf16[4,320,1280]{2,1,0:T(8,128)(2,1)}, bf16[4,320,1280]{2,1,0:T(8,128)(2,1)}) custom-call(s32[2]{0:T(128)} %pad_add_fusion.refs_0_, bf16[2112,5120]{1,0:T(8,128)(2,1)} %bitcast.56, bf16[2112,1280]{1,0:T(8,128)(2,1)} %bitcast.53), custom_call_target="tpu_custom_call" | custom-call | flops 34603008000 | bytes 40140800 | tf_op jit(solution)/shard_map/g_down/pallas_call | solution.py:378
  322.8 11.4 %all-gather.6.cloned.1.call-done.w_ref = bf16[5120,1280]{1,0:T(8,128)(2,1)} async-done(((bf16[320,1280]{1,0:T(8,128)(2,1)}), bf16[5120,1280]{1,0:T(8,128)(2,1)}) %all-gather.6.cloned.1.call-update) | async-done | bytes 13107216 | tf_op jit(solution)/shard_map/all_gather | solution.py:448
  334.1 42.3 %down.1 = f32[2056,1280]{1,0:T(8,128)} custom-call(bf16[5120,1280]{1,0:T(8,128)(2,1)} %all-gather.6.cloned.1.call-done.w_ref, bf16[8,264,5120]{2,1,0:T(8,128)(2,1)} %get-tuple-element.84.active_ref, f32[8,264,1280]{2,1,0:T(8,128)} %get-tuple-element.85.hidden_ref, f32[1,1280]{1,0:T(1,128)} %reshape.242.bias_ref), custom_call_target="tpu_custom_call" | custom-call | flops 34603008000 | bytes 56079360 | tf_op jit(solution)/shard_map/down/pallas_call | solution.py:61
  382.1 37.6 %down_back.1 = (bf16[8,264,5120]{2,1,0:T(8,128)(2,1)}, f32[8,5120]{1,0:T(8,128)}) custom-call(bf16[5120,1280]{1,0:T(8,128)(2,1)} %all-gather.6.cloned.1.call-done.w_ref, bf16[8,264,1280]{2,1,0:T(8,128)(2,1)} %get-tuple-element.87.c_ref, bf16[8,264,5120]{2,1,0:T(8,128)(2,1)} %get-tuple-element.88.slope_ref), custom_call_target="tpu_custom_call" | custom-call | flops 41523609600 | bytes 61931520 | tf_op jit(solution)/shard_map/down_back/pallas_call | solution.py:61
  419.6 21.2 %g_up_low.1 = (bf16[8,80,2560]{2,1,0:T(8,128)(2,1)}, bf16[4,80,2560]{2,1,0:T(8,128)(2,1)}, bf16[4,80,2560]{2,1,0:T(8,128)(2,1)}) custom-call(s32[2]{0:T(128)} %pad_add_fusion.refs_0_, bf16[2112,1280]{1,0:T(8,128)(2,1)} %bitcast.59, bf16[2112,5120]{1,0:T(8,128)(2,1)} %bitcast.54), custom_call_target="tpu_custom_call" | custom-call | flops 17301504000 | bytes 33587200 | tf_op jit(solution)/shard_map/g_up_low/pallas_call | solution.py:378
  441.0 21.3 %g_up_high.1 = (bf16[8,80,2560]{2,1,0:T(8,128)(2,1)}, bf16[4,80,2560]{2,1,0:T(8,128)(2,1)}, bf16[4,80,2560]{2,1,0:T(8,128)(2,1)}) custom-call(s32[2]{0:T(128)} %pad_add_fusion.refs_0_, bf16[2112,1280]{1,0:T(8,128)(2,1)} %bitcast.60, bf16[2112,5120]{1,0:T(8,128)(2,1)} %bitcast.55), custom_call_target="tpu_custom_call" | custom-call | flops 17301504000 | bytes 33587200 | tf_op jit(solution)/shard_map/g_up_high/pallas_call | solution.py:378
  462.8 6.8 add_convert_fusion
  475.5 58.4 %up_back.1 = (f32[8,264,1280]{2,1,0:T(8,128)}, bf16[8,264,1280]{2,1,0:T(8,128)(2,1)}, bf16[8,264,1280]{2,1,0:T(8,128)(2,1)}, f32[8,1280]{1,0:T(8,128)}, f32[8,1280]{1,0:T(8,128)}, /*index=5*/f32[8,1280]{1,0:T(8,128)}) custom-call(bf16[1280,6400]{1,0:T(8,128)(2,1)} %all-gather.8.cloned.1.call-done.w_ref.w_up_ref.w_out_ref, ...), custom_call_target="tpu_custom_call" | custom-call | flops 51904512000 | bytes 92369920 | tf_op jit(solution)/shard_map/up_back/pallas_call | solution.py:61
  537.6 13.0 %g_out.1 = (bf16[8,80,1280]{2,1,0:T(8,128)(2,1)}, bf16[4,80,1280]{2,1,0:T(8,128)(2,1)}, bf16[4,80,1280]{2,1,0:T(8,128)(2,1)}) custom-call(s32[2]{0:T(128)} %pad_add_fusion.refs_0_, bf16[2112,1280]{1,0:T(8,128)(2,1)} %bitcast.37, bf16[2112,1280]{1,0:T(8,128)(2,1)} %bitcast.61), custom_call_target="tpu_custom_call" | custom-call | flops 8650752000 | bytes 14090240 | tf_op jit(solution)/shard_map/g_out/pallas_call | solution.py:378
  560.3 53.6 %attention_back.1 = (bf16[8,264,3840]{2,1,0:T(8,128)(2,1)}, f32[8,2560]{1,0:T(8,128)}) custom-call(bf16[8,264,3840]{2,1,0:T(8,128)(2,1)} %qkv.1.packed_ref, bf16[8,264,1280]{2,1,0:T(8,128)(2,1)} %get-tuple-element.77.mixed_ref, bf16[8,264,1280]{2,1,0:T(8,128)(2,1)} %get-tuple-element.108.dmixed_ref, f32[8,16,264]{2,1,0:T(8,128)} %get-tuple-element.109.lse_ref), custom_call_target="tpu_custom_call" | custom-call | flops 4730880000 | bytes 43470848 | tf_op jit(solution)/shard_map/attention_back/pallas_call | solution.py:61
  619.1 29.6 %g_qkv.1 = (bf16[8,80,3840]{2,1,0:T(8,128)(2,1)}, bf16[4,80,3840]{2,1,0:T(8,128)(2,1)}, bf16[4,80,3840]{2,1,0:T(8,128)(2,1)}) custom-call(s32[2]{0:T(128)} %pad_add_fusion.refs_0_, bf16[2112,1280]{1,0:T(8,128)(2,1)} %bitcast.52, bf16[2112,3840]{1,0:T(8,128)(2,1)} %bitcast.51), custom_call_target="tpu_custom_call" | custom-call | flops 25952256000 | bytes 31457280 | tf_op jit(solution)/shard_map/g_qkv/pallas_call | solution.py:378
  648.9 8.4 %collective-permute-done.11 = bf16[8,80,3840]{2,1,0:T(8,128)(2,1)} collective-permute-done((bf16[8,80,3840]{2,1,0:T(8,128)(2,1)}, bf16[8,80,3840]{2,1,0:T(8,128)(2,1)}, u32[]{:S(2)}, u32[]{:S(2)}) %collective-permute-start.11) | collective-permute-done | bytes 4915232 | tf_op jit(solution)/shard_map/ppermute | solution.py:468
  661.7 41.6 %qkv_back.1 = (f32[2056,1280]{1,0:T(8,128)}, f32[8,1280]{1,0:T(8,128)}, f32[8,1280]{1,0:T(8,128)}) custom-call(bf16[1280,3840]{1,0:T(8,128)(2,1)} %all-gather.4.cloned.1.call-done.w_ref, bf16[8,264,3840]{2,1,0:T(8,128)(2,1)} %get-tuple-element.115.dpacked_ref, bf16[8,264,1280]{2,1,0:T(8,128)(2,1)} %get-tuple-element.76.x_ref, ...), custom_call_target="tpu_custom_call" | custom-call | flops 31142707200 | bytes 52884480 | tf_op jit(solution)/shard_map/qkv_back/pallas_call | solution.py:61
  703.4 13.0 %collective-permute-done.12 = bf16[4,80,3840]{2,1,0:T(8,128)(2,1)} collective-permute-done((bf16[4,80,3840]{2,1,0:T(8,128)(2,1)}, bf16[4,80,3840]{2,1,0:T(8,128)(2,1)}, u32[]{:S(2)}, u32[]{:S(2)}) %collective-permute-start.12) | collective-permute-done | bytes 2457632 | tf_op jit(solution)/shard_map/ppermute | solution.py:474
  733.8 10.7 %collective-permute-done.16 = bf16[320,1280]{1,0:T(8,128)(2,1)S(1)} collective-permute-done((bf16[320,1280]{1,0:T(8,128)(2,1)S(1)}, bf16[320,1280]{1,0:T(8,128)(2,1)S(1)}, u32[]{:S(2)}, u32[]{:S(2)}) %collective-permute-start.16) | collective-permute-done | bytes 819232 | tf_op jit(solution)/shard_map/ppermute | solution.py:409
  753.3 12.7 %collective-permute-done.21 = f32[960]{0:T(1024)S(1)} collective-permute-done((f32[960]{0:T(1024)S(1)}, f32[960]{0:T(1024)S(1)}, u32[]{:S(2)}, u32[]{:S(2)}) %collective-permute-start.21) | collective-permute-done | bytes 3872 | tf_op jit(solution)/shard_map/ppermute | solution.py:502
  775.2 11.8 %collective-permute-done.13 = bf16[80,3840]{1,0:T(8,128)(2,1)S(1)} collective-permute-done((bf16[80,3840]{1,0:T(8,128)(2,1)}, bf16[80,3840]{1,0:T(8,128)(2,1)S(1)}, u32[]{:S(2)}, u32[]{:S(2)}) %collective-permute-start.13) | collective-permute-done | bytes 614432 | tf_op jit(solution)/shard_map/ppermute | solution.py:409
  (175 shorter events, 109.7 us)
Async XLA Ops:
  7.2 90.3 %all-gather.4.cloned.1.call-start = ((), (), s32[]{:S(2)}) async-start(), calls=%async_computation.4 | async-start | bytes 10444800 | tf_op jit(solution)/shard_map/all_gather | solution.py:448
  7.9 215.0 %all-gather.8.cloned.1.call-start = ((), (), s32[]{:S(2)}) async-start(), calls=%async_computation.6 | async-start | bytes 17408000 | tf_op jit(solution)/shard_map/all_gather | solution.py:448
  14.8 4.5 collective-permute-start.1
  23.2 14.9 %collective-permute-start.3 = (bf16[8,960]{1,0:T(8,128)(2,1)S(1)}, bf16[8,960]{1,0:T(8,128)(2,1)S(1)}, u32[]{:S(2)}, u32[]{:S(2)}) collective-permute-start(bf16[8,960]{1,0:T(8,128)(2,1)S(1)} %pad_maximum_fusion.5), channel_id=1, source_target_pairs={{0,8},{4,12},{8,0},{12,4},{1,9},{5,13},{9,1},{13,5},{2,10},{6,14},... | collective-permute-start | bytes 46088 | tf_op jit(solution)/shard_map/ppermute | solution.py:454
  53.1 281.1 %all-gather.6.cloned.1.call-start = ((), (), s32[]{:S(2)}) async-start(), calls=%async_computation.5 | async-start | bytes 13926400 | tf_op jit(solution)/shard_map/all_gather | solution.py:448
  124.8 412.9 %reduce-scatter.5.cloned.1.call-start = ((), (), s32[]{:S(2)}) async-start(), calls=%async_computation.7 | async-start | bytes 4096000 | tf_op jit(solution)/shard_map/reduce_scatter | solution.py:481
  321.7 54.7 %collective-permute-start.4 = (bf16[8,320,1280]{2,1,0:T(8,128)(2,1)}, bf16[8,320,1280]{2,1,0:T(8,128)(2,1)}, u32[]{:S(2)}, u32[]{:S(2)}) collective-permute-start(bf16[8,320,1280]{2,1,0:T(8,128)(2,1)} %get-tuple-element.81), channel_id=1, source_target_pairs={{0,1},{1,0},{2,3},{3,2},{4,5},{5,4},{6,7},{7,6},{8,9},{9,8},{10,11... | collective-permute-start | bytes 19660808 | tf_op jit(solution)/shard_map/ppermute | solution.py:468
  381.4 81.4 %collective-permute-start.6 = (bf16[4,320,1280]{2,1,0:T(8,128)(2,1)}, bf16[4,320,1280]{2,1,0:T(8,128)(2,1)}, u32[]{:S(2)}, u32[]{:S(2)}) collective-permute-start(bf16[4,320,1280]{2,1,0:T(8,128)(2,1)} %slice_add_fusion), channel_id=1, source_target_pairs={{0,2},{2,0},{1,3},{3,1},{4,6},{6,4},{5,7},{7,5},{8,10},{10,8},{9,1... | collective-permute-start | bytes 9830408 | tf_op jit(solution)/shard_map/ppermute | solution.py:474
  440.9 28.8 %collective-permute-start.5 = (bf16[8,80,2560]{2,1,0:T(8,128)(2,1)}, bf16[8,80,2560]{2,1,0:T(8,128)(2,1)S(1)}, u32[]{:S(2)}, u32[]{:S(2)}) collective-permute-start(bf16[8,80,2560]{2,1,0:T(8,128)(2,1)} %get-tuple-element.90), channel_id=1, source_target_pairs={{0,1},{1,0},{2,3},{3,2},{4,5},{5,4},{6,7},{7,6},{8,9},{9,8},{10,11... | collective-permute-start | bytes 9830408 | tf_op jit(solution)/shard_map/ppermute | solution.py:468
  462.3 88.4 %collective-permute-start.8 = (bf16[8,80,2560]{2,1,0:T(8,128)(2,1)}, bf16[8,80,2560]{2,1,0:T(8,128)(2,1)}, u32[]{:S(2)}, u32[]{:S(2)}) collective-permute-start(bf16[8,80,2560]{2,1,0:T(8,128)(2,1)} %get-tuple-element.94), channel_id=1, source_target_pairs={{0,1},{1,0},{2,3},{3,2},{4,5},{5,4},{6,7},{7,6},{8,9},{9,8},{10,11... | collective-permute-start | bytes 9830408 | tf_op jit(solution)/shard_map/ppermute | solution.py:468
  469.6 149.5 %reduce-scatter.7.cloned.1.call-start = ((), (), s32[]{:S(2)}) async-start(), calls=%async_computation.8 | async-start | bytes 2048000 | tf_op jit(solution)/shard_map/reduce_scatter | solution.py:481
  474.2 59.7 %collective-permute-start.7 = (bf16[4,80,2560]{2,1,0:T(8,128)(2,1)}, bf16[4,80,2560]{2,1,0:T(8,128)(2,1)}, u32[]{:S(2)}, u32[]{:S(2)}) collective-permute-start(bf16[4,80,2560]{2,1,0:T(8,128)(2,1)} %slice_add_fusion.3), channel_id=1, source_target_pairs={{0,2},{2,0},{1,3},{3,1},{4,6},{6,4},{5,7},{7,5},{8,10},{10,8},{9,1... | collective-permute-start | bytes 4915208 | tf_op jit(solution)/shard_map/ppermute | solution.py:474
  556.1 57.7 %collective-permute-start.10 = (bf16[4,80,3840]{2,1,0:T(8,128)(2,1)}, bf16[4,80,3840]{2,1,0:T(8,128)(2,1)}, u32[]{:S(2)}, u32[]{:S(2)}) collective-permute-start(bf16[4,80,3840]{2,1,0:T(8,128)(2,1)} %pad_maximum_fusion.1), channel_id=1, source_target_pairs={{0,2},{2,0},{1,3},{3,1},{4,6},{6,4},{5,7},{7,5},{8,10},{10,8},{9,1... | collective-permute-start | bytes 7372808 | tf_op jit(solution)/shard_map/ppermute | solution.py:474
  557.2 146.2 %reduce-scatter.9.cloned.1.call-start = ((), (), s32[]{:S(2)}) async-start(), calls=%async_computation.9 | async-start | bytes 3072000 | tf_op jit(solution)/shard_map/reduce_scatter | solution.py:481
  648.7 8.6 %collective-permute-start.11 = (bf16[8,80,3840]{2,1,0:T(8,128)(2,1)}, bf16[8,80,3840]{2,1,0:T(8,128)(2,1)}, u32[]{:S(2)}, u32[]{:S(2)}) collective-permute-start(bf16[8,80,3840]{2,1,0:T(8,128)(2,1)} %get-tuple-element.114), channel_id=1, source_target_pairs={{0,1},{1,0},{2,3},{3,2},{4,5},{5,4},{6,7},{7,6},{8,9},{9,8},{10,11... | collective-permute-start | bytes 14745608 | tf_op jit(solution)/shard_map/ppermute | solution.py:468
  648.8 122.5 %reduce-scatter.11.cloned.1.call-start = ((), (), s32[]{:S(2)}) async-start(), calls=%async_computation.10 | async-start | bytes 3072000 | tf_op jit(solution)/shard_map/reduce_scatter | solution.py:481
  660.7 55.7 %collective-permute-start.12 = (bf16[4,80,3840]{2,1,0:T(8,128)(2,1)}, bf16[4,80,3840]{2,1,0:T(8,128)(2,1)}, u32[]{:S(2)}, u32[]{:S(2)}) collective-permute-start(bf16[4,80,3840]{2,1,0:T(8,128)(2,1)} %slice_add_fusion.1), channel_id=1, source_target_pairs={{0,2},{2,0},{1,3},{3,1},{4,6},{6,4},{5,7},{7,5},{8,10},{10,8},{9,1... | collective-permute-start | bytes 7372808 | tf_op jit(solution)/shard_map/ppermute | solution.py:474
  723.3 21.1 %collective-permute-start.16 = (bf16[320,1280]{1,0:T(8,128)(2,1)S(1)}, bf16[320,1280]{1,0:T(8,128)(2,1)S(1)}, u32[]{:S(2)}, u32[]{:S(2)}) collective-permute-start(bf16[320,1280]{1,0:T(8,128)(2,1)S(1)} %bitcast.40), channel_id=1, source_target_pairs={{0,16},{16,0},{1,17},{17,1},{2,18},{18,2},{3,19},{19,3},{4,20},{20... | collective-permute-start | bytes 2457608 | tf_op jit(solution)/shard_map/ppermute | solution.py:409
  728.9 4.8 collective-permute-start.19
  730.1 23.1 %collective-permute-start.15 = (bf16[80,2560]{1,0:T(8,128)(2,1)S(1)}, bf16[80,2560]{1,0:T(8,128)(2,1)S(1)}, u32[]{:S(2)}, u32[]{:S(2)}) collective-permute-start(bf16[80,2560]{1,0:T(8,128)(2,1)S(1)} %bitcast.45), channel_id=1, source_target_pairs={{0,16},{16,0},{1,17},{17,1},{2,18},{18,2},{3,19},{19,3},{4,20},{20... | collective-permute-start | bytes 1228808 | tf_op jit(solution)/shard_map/ppermute | solution.py:409
  733.7 13.6 %collective-permute-start.20 = (f32[1,960]{1,0:T(1,128)S(1)}, f32[1,960]{1,0:T(1,128)S(1)}, u32[]{:S(2)}, u32[]{:S(2)}) collective-permute-start(f32[1,960]{1,0:T(1,128)S(1)} %constant_dynamic-slice_fusion), channel_id=1, source_target_pairs={{0,4},{4,0},{8,12},{12,8},{1,5},{5,1},{9,13},{13,9},{2,6},{6,2},{1... | collective-permute-start | bytes 11528 | tf_op jit(solution)/shard_map/ppermute | solution.py:497
  745.8 27.2 %collective-permute-start.14 = (bf16[80,3840]{1,0:T(8,128)(2,1)S(1)}, bf16[80,3840]{1,0:T(8,128)(2,1)S(1)}, u32[]{:S(2)}, u32[]{:S(2)}) collective-permute-start(bf16[80,3840]{1,0:T(8,128)(2,1)S(1)} %bitcast.42), channel_id=1, source_target_pairs={{0,16},{16,0},{1,17},{17,1},{2,18},{18,2},{3,19},{19,3},{4,20},{20... | collective-permute-start | bytes 1843208 | tf_op jit(solution)/shard_map/ppermute | solution.py:409
  747.3 18.7 %collective-permute-start.21 = (f32[960]{0:T(1024)S(1)}, f32[960]{0:T(1024)S(1)}, u32[]{:S(2)}, u32[]{:S(2)}) collective-permute-start(f32[960]{0:T(1024)S(1)} %bitcast.48), channel_id=1, source_target_pairs={{0,16},{16,0},{1,17},{17,1},{2,18},{18,2},{3,19},{19,3},{4,20},{20... | collective-permute-start | bytes 11528 | tf_op jit(solution)/shard_map/ppermute | solution.py:502
  771.4 15.6 %collective-permute-start.13 = (bf16[80,3840]{1,0:T(8,128)(2,1)}, bf16[80,3840]{1,0:T(8,128)(2,1)S(1)}, u32[]{:S(2)}, u32[]{:S(2)}) collective-permute-start(bf16[80,3840]{1,0:T(8,128)(2,1)} %bitcast.44), channel_id=1, source_target_pairs={{0,16},{16,0},{1,17},{17,1},{2,18},{18,2},{3,19},{19,3},{4,20},{20... | collective-permute-start | bytes 1843208 | tf_op jit(solution)/shard_map/ppermute | solution.py:409
  (25 other events, 315.5 us)
Sparse Core Ops, SparseCore 0:
  10.3 87.1 all-gather.3
  100.4 122.5 all-gather.7
  225.2 108.8 all-gather.5
  469.7 61.6 reduce-scatter.4
  557.3 35.9 reduce-scatter.6
  648.9 49.2 reduce-scatter.8
  722.0 49.2 reduce-scatter.10

commit v4 on v3

--- a/solution.py
+++ b/solution.py
@@ -562,51 +562,51 @@
         "up", 4 * D * FF)
 
     p_down = gradient(active, cpad, "g_down")
-    staging = [pltpu.VMEM((D // 128, SEQ * n, 128), F32), pltpu.SemaphoreType.DMA((D // 128,))]
-    result, = call(
-        down_kernel, n, [whole(full_down), image(after(active, p_down)), image(hidden), whole(b_down)],
-        [untouched(sds(SEQ * n, D, dtype=F32))], "down", 2.5 * D * FF * n * SP, staging)
-    p_down = links.first_stage(p_down, result)
     d_inner, s_up = by_columns(
-        down_back_kernel, (full_down, pl.BlockSpec((D, D), lambda j, i: (j, 0))), after(cpad, result, p_down[0]), [slope],
+        down_back_kernel, (full_down, pl.BlockSpec((D, D), lambda j, i: (j, 0))), after(cpad, p_down), [slope],
         [sds(n, SP, FF), sds(8, FF, dtype=F32)], "down_back", 3 * D * FF)
-    p_up = gradient(normed_two, d_inner, "g_up_low", 0, FF // 2)
+    p_down = links.first_stage(p_down, d_inner)
+    p_up = gradient(normed_two, after(d_inner, p_down[0]), "g_up_low", 0, FF // 2)
     p_up2 = gradient(normed_two, after(d_inner, p_up), "g_up_high", FF // 2, FF // 2)
     p_up = links.first_stage(p_up, p_up2)
-    p_down = links.second_stage(p_down, p_up2)
 
     def pair(a):
         return a, pl.BlockSpec((2,) + tuple(a.shape[1:]), lambda i, k: (i, 0, 0))
     d_hidden, d_hidden_b, d_mixed, s_gain_two, s_shift_two, s_out = grid_call(
         up_back_kernel, (n // 2, 2),
         [(middle, pl.BlockSpec((D, FF // 2), lambda i, k: (0, k))),
-         (after(d_inner, p_up2, p_up[0], p_down), pl.BlockSpec((2, SP, FF // 2), lambda i, k: (i, 0, k))),
+         (after(d_inner, p_up2, p_up[0]), pl.BlockSpec((2, SP, FF // 2), lambda i, k: (i, 0, k))),
          full_out, pair(hidden), pair(cpad), whole(gain_two)],
         [pair(sds(n, SP, D, dtype=F32)), pair(sds(n, SP, D)), pair(sds(n, SP, D)), sums(D), sums(D), sums(D)],
         "up_back", 3 * D * (D + FF) * n * SP, [pltpu.VMEM((2 * SP, D), F32)])
+    p_down = links.second_stage(p_down, d_hidden_b)
+    p_up = links.second_stage(p_up, d_hidden_b)
+    p_out = gradient(mixed, after(d_hidden_b, p_down, p_up), "g_out")
     p_down = links.third_stage(p_down)
-    p_up = links.second_stage(p_up, d_hidden_b)
-    p_out = gradient(mixed, after(d_hidden_b, p_up, p_down), "g_out")
-    p_up = links.third_stage(p_up)
     p_up2 = links.first_stage(p_up2, p_out)
     p_out = links.first_stage(p_out)
     rest = links.joined([p_up2, p_out])
     d_packed, s_qv = call(
         attention_back_kernel, n, [image(packed), image(mixed), image(after(d_mixed, rest[0])), image(logsum)],
         [rows(SP, 3 * D), sums(2 * D)], "attention_back", 1.4e5 * n * SP * H)
-    g_down = both_groups(after(p_down, d_packed))
     rest = links.second_stage(rest, d_packed)
-    last = gradient(normed_one, after(d_packed, rest, p_up), "g_qkv")
-    rest = links.third_stage(rest)
-    last = links.first_stage(last)
+    p_up = links.third_stage(after(p_up, p_down, d_packed))
+    last = gradient(normed_one, after(d_packed, rest, p_down), "g_qkv")
+    last = links.first_stage(after(last, p_up))
+    rest = links.third_stage(after(rest, p_up))
+    staging = [pltpu.VMEM((D // 128, SEQ * n, 128), F32), pltpu.SemaphoreType.DMA((D // 128,))]
     d_images, s_gain_one, s_shift_one = call(
         qkv_back_kernel, n,
         [whole(full_qkv), image(after(d_packed, last[0])), image(xpad), image(d_hidden), whole(gain_one)],
         [untouched(sds(SEQ * n, D, dtype=F32)), sums(D), sums(D)], "qkv_back", 3 * D * 3 * D * n * SP, staging)
-    g_up = both_groups(after(p_up, last[0]))
+    g_down, g_up = both_groups(after(p_down, last[0])), both_groups(after(p_up, last[0]))
     last = links.second_stage(last, d_images, rest)
-    rest, s_gain_one = after((rest, s_gain_one), last)
-    rest, g_qkv = both_groups(rest), both_groups(links.third_stage(last))
+    result, = call(
+        down_kernel, n, [whole(full_down), image(after(active, last)), image(hidden), whole(b_down)],
+        [untouched(sds(SEQ * n, D, dtype=F32))], "down", 2.5 * D * FF * n * SP, staging)
+    rest = both_groups(after(rest, last))
+    last, rest, g_down, g_up, s_gain_one = after((links.third_stage(last), rest, g_down, g_up, s_gain_one), result)
+    g_qkv = both_groups(last)
     g_up2, g_out = rest[:, :FF // 2], rest[:, FF // 2:]
     result, d_images = [jnp.transpose(a.reshape(SEQ, n, D), (1, 0, 2)) for a in (result, d_images)]
     g_up = jnp.concatenate([g_up, g_up2], 1)

time: 801 us -> 792 us (0.989)
  waiting for transfers between devices: 179 us -> 169 us
    ppermute x4, waiting for transfers between devices: 27.8 us -> 10.7 us  [both_groups(): return shard.astype(F32) + lax.ppermute(shard, 'dp', SWAP).astype(F32)]
    ppermute x4, waiting for transfers between devices: 13 us -> 25 us  [second_stage(): got_x = lax.ppermute(passed, 'x', SWAP)]
  transfers between devices with their start and end apart: 29 -> 29, of which waited for: 16 -> 18; matrix products, arithmetic and copies ran while one was open for 7% -> 8% of each run, Pallas kernels for 60% -> 62%
where the time goes in v4:
time: 792 us; the launch traced here: 786 us
  Pallas kernels  507 us (64%)
  waiting for transfers between devices  169 us (21%)
  other arithmetic  48.7 us (6%)
  local copies, waits for them, and re-layouts  25.3 us (3%)
  starting transfers between devices  21.6 us (3%)
  between operations  14.9 us (2%)
    pallas_call x10, Pallas kernels, grid_call(): pl.pallas_call(kernel, grid=grid, in_specs=[spec for _, spec in ins], out...  384 us
    pallas_call x5, Pallas kernels, weight_gradient(): pl.pallas_call(kernel, grid=(left.shape[1] // block, width // cols), in_s...  123 us
    all_gather x3, waiting for transfers between devices, gather(): return lax.all_gather(w, ('z', 'x', 'core'), axis=0, tiled=True)  99.2 us
    ppermute x4, waiting for transfers between devices, second_stage(): got_x = lax.ppermute(passed, 'x', SWAP)  25 us
    convert_element_type x4, other arithmetic, second_stage(): (keep.astype(F32) + got[:half].astype(F32) + got_x.astype(F32)).astype(BF)  21.1 us
  transfers between devices with their start and end apart: 29, of which 18 were waited for; matrix products, arithmetic and copies ran while one was open for 8% of the time, Pallas kernels for 62%

profile of v4, /device:TPU:0, one launch (start us, length us, event | category | flops | bytes accessed | tf_op | source)
XLA Modules:
  0.0 786.2 jit_solution(2646263341125740061)
XLA Ops:
  40.1 13.6 %prepare.1 = (bf16[8,264,1280]{2,1,0:T(8,128)(2,1)}, bf16[8,264,1280]{2,1,0:T(8,128)(2,1)}, bf16[8,264,1280]{2,1,0:T(8,128)(2,1)}, f32[8,1280]{1,0:T(8,128)}) custom-call(bf16[8,257,1280]{2,1,0:T(8,128)(2,1)} %copy.28.x_ref, bf16[8,257,1280]{2,1,0:T(8,128)(2,1)} %copy.29.c_ref, f32[1,1280]{1,0:T(1,128)} %reshape.235.gain_ref, f32[1,1280]{1,0:T(1,128)} %reshape.236.shift_ref), custom_call_target="tpu_custom_call" | custom-call | flops 1081344000 | bytes 26798080 | tf_op jit(solution)/shard_map/prepare/pallas_call | solution.py:61
  54.5 43.0 %all-gather.4.cloned.1.call-done.w_ref = bf16[1280,3840]{1,0:T(8,128)(2,1)} async-done(((bf16[80,3840]{1,0:T(8,128)(2,1)}), bf16[1280,3840]{1,0:T(8,128)(2,1)}) %all-gather.4.cloned.1.call-update) | async-done | bytes 9830416 | tf_op jit(solution)/shard_map/all_gather | solution.py:448
  97.5 27.1 %qkv.1.packed_ref = bf16[8,264,3840]{2,1,0:T(8,128)(2,1)} custom-call(bf16[1280,3840]{1,0:T(8,128)(2,1)} %all-gather.4.cloned.1.call-done.w_ref, bf16[8,264,1280]{2,1,0:T(8,128)(2,1)} %get-tuple-element.83.normed_ref, f32[1,3840]{1,0:T(1,128)} %fusion.bias_ref), custom_call_target="tpu_custom_call" | custom-call | flops 25952256000 | bytes 31472640 | tf_op jit(solution)/shard_map/qkv/pallas_call | solution.py:61
  128.3 48.0 %attention.1 = (bf16[8,264,1280]{2,1,0:T(8,128)(2,1)}, f32[8,16,264]{2,1,0:T(8,128)}) custom-call(bf16[8,264,3840]{2,1,0:T(8,128)(2,1)} %qkv.1.packed_ref), custom_call_target="tpu_custom_call" | custom-call | flops 3379200000 | bytes 21762048 | tf_op jit(solution)/shard_map/attention/pallas_call | solution.py:61
  176.2 46.7 %all-gather.8.cloned.1.call-done.w_ref.w_up_ref.w_out_ref = bf16[1280,6400]{1,0:T(8,128)(2,1)} async-done(((bf16[80,6400]{1,0:T(8,128)(2,1)}), bf16[1280,6400]{1,0:T(8,128)(2,1)}) %all-gather.8.cloned.1.call-update) | async-done | bytes 16384016 | tf_op jit(solution)/shard_map/all_gather | solution.py:448
  222.9 15.9 %out.1 = (f32[8,264,1280]{2,1,0:T(8,128)}, bf16[8,264,1280]{2,1,0:T(8,128)(2,1)}) custom-call(bf16[1280,6400]{1,0:T(8,128)(2,1)} %all-gather.8.cloned.1.call-done.w_ref.w_up_ref.w_out_ref, bf16[8,264,1280]{2,1,0:T(8,128)(2,1)} %get-tuple-element.86.x_ref, bf16[8,264,1280]{2,1,0:T(8,128)(2,1)} %get-tuple-element.87.mixed_ref, f32[1,1280]{1,0:T(1,128)} %reshape.238.bias_ref, ...), custom_call_target="tpu_custom_call" | custom-call | flops 10380902400 | bytes 43432960 | tf_op jit(solution)/shard_map/out/pallas_call | solution.py:61
  238.9 45.7 %up.1 = (bf16[8,264,5120]{2,1,0:T(8,128)(2,1)}, bf16[8,264,5120]{2,1,0:T(8,128)(2,1)}) custom-call(bf16[1280,6400]{1,0:T(8,128)(2,1)} %all-gather.8.cloned.1.call-done.w_ref.w_up_ref.w_out_ref, bf16[8,264,1280]{2,1,0:T(8,128)(2,1)} %get-tuple-element.88.normed_ref, f32[1,5120]{1,0:T(1,128)} %reshape.241.bias_ref), custom_call_target="tpu_custom_call" | custom-call | flops 55364812800 | bytes 65064960 | tf_op jit(solution)/shard_map/up/pallas_call | solution.py:61
  284.6 37.0 %g_down.1 = (bf16[8,320,1280]{2,1,0:T(8,128)(2,1)}, bf16[4,320,1280]{2,1,0:T(8,128)(2,1)}, bf16[4,320,1280]{2,1,0:T(8,128)(2,1)}) custom-call(s32[2]{0:T(128)} %pad_add_fusion.refs_0_, bf16[2112,5120]{1,0:T(8,128)(2,1)} %bitcast.52, bf16[2112,1280]{1,0:T(8,128)(2,1)} %bitcast.51), custom_call_target="tpu_custom_call" | custom-call | flops 34603008000 | bytes 40140800 | tf_op jit(solution)/shard_map/g_down/pallas_call | solution.py:378
  322.0 9.5 %all-gather.6.cloned.1.call-done.w_ref = bf16[5120,1280]{1,0:T(8,128)(2,1)} async-done(((bf16[320,1280]{1,0:T(8,128)(2,1)}), bf16[5120,1280]{1,0:T(8,128)(2,1)}) %all-gather.6.cloned.1.call-update) | async-done | bytes 13107216 | tf_op jit(solution)/shard_map/all_gather | solution.py:448
  331.5 37.8 %down_back.1 = (bf16[8,264,5120]{2,1,0:T(8,128)(2,1)}, f32[8,5120]{1,0:T(8,128)}) custom-call(bf16[5120,1280]{1,0:T(8,128)(2,1)} %all-gather.6.cloned.1.call-done.w_ref, bf16[8,264,1280]{2,1,0:T(8,128)(2,1)} %get-tuple-element.94.c_ref, bf16[8,264,5120]{2,1,0:T(8,128)(2,1)} %get-tuple-element.95.slope_ref), custom_call_target="tpu_custom_call" | custom-call | flops 41523609600 | bytes 61931520 | tf_op jit(solution)/shard_map/down_back/pallas_call | solution.py:61
  374.3 21.2 %g_up_low.1 = (bf16[8,80,2560]{2,1,0:T(8,128)(2,1)}, bf16[4,80,2560]{2,1,0:T(8,128)(2,1)}, bf16[4,80,2560]{2,1,0:T(8,128)(2,1)}) custom-call(s32[2]{0:T(128)} %pad_add_fusion.refs_0_, bf16[2112,1280]{1,0:T(8,128)(2,1)} %bitcast.57, bf16[2112,5120]{1,0:T(8,128)(2,1)} %bitcast.53), custom_call_target="tpu_custom_call" | custom-call | flops 17301504000 | bytes 33587200 | tf_op jit(solution)/shard_map/g_up_low/pallas_call | solution.py:378
  395.8 21.3 %g_up_high.1 = (bf16[8,80,2560]{2,1,0:T(8,128)(2,1)}, bf16[4,80,2560]{2,1,0:T(8,128)(2,1)}, bf16[4,80,2560]{2,1,0:T(8,128)(2,1)}) custom-call(s32[2]{0:T(128)} %pad_add_fusion.refs_0_, bf16[2112,1280]{1,0:T(8,128)(2,1)} %bitcast.58, bf16[2112,5120]{1,0:T(8,128)(2,1)} %bitcast.54), custom_call_target="tpu_custom_call" | custom-call | flops 17301504000 | bytes 33587200 | tf_op jit(solution)/shard_map/g_up_high/pallas_call | solution.py:378
  423.8 58.5 %up_back.1 = (f32[8,264,1280]{2,1,0:T(8,128)}, bf16[8,264,1280]{2,1,0:T(8,128)(2,1)}, bf16[8,264,1280]{2,1,0:T(8,128)(2,1)}, f32[8,1280]{1,0:T(8,128)}, f32[8,1280]{1,0:T(8,128)}, /*index=5*/f32[8,1280]{1,0:T(8,128)}) custom-call(bf16[1280,6400]{1,0:T(8,128)(2,1)} %all-gather.8.cloned.1.call-done.w_ref.w_up_ref.w_out_ref, ...), custom_call_target="tpu_custom_call" | custom-call | flops 51904512000 | bytes 92369920 | tf_op jit(solution)/shard_map/up_back/pallas_call | solution.py:61
  482.3 6.8 add_convert_fusion
  489.1 15.2 %collective-permute-done.7 = bf16[4,80,2560]{2,1,0:T(8,128)(2,1)} collective-permute-done((bf16[4,80,2560]{2,1,0:T(8,128)(2,1)}, bf16[4,80,2560]{2,1,0:T(8,128)(2,1)}, u32[]{:S(2)}, u32[]{:S(2)}) %collective-permute-start.7) | collective-permute-done | bytes 1638432 | tf_op jit(solution)/shard_map/ppermute | solution.py:474
  508.0 13.1 %g_out.1 = (bf16[8,80,1280]{2,1,0:T(8,128)(2,1)}, bf16[4,80,1280]{2,1,0:T(8,128)(2,1)}, bf16[4,80,1280]{2,1,0:T(8,128)(2,1)}) custom-call(s32[2]{0:T(128)} %pad_add_fusion.refs_0_, bf16[2112,1280]{1,0:T(8,128)(2,1)} %bitcast.36, bf16[2112,1280]{1,0:T(8,128)(2,1)} %bitcast.59), custom_call_target="tpu_custom_call" | custom-call | flops 8650752000 | bytes 14090240 | tf_op jit(solution)/shard_map/g_out/pallas_call | solution.py:378
  528.7 53.2 %attention_back.1 = (bf16[8,264,3840]{2,1,0:T(8,128)(2,1)}, f32[8,2560]{1,0:T(8,128)}) custom-call(bf16[8,264,3840]{2,1,0:T(8,128)(2,1)} %qkv.1.packed_ref, bf16[8,264,1280]{2,1,0:T(8,128)(2,1)} %get-tuple-element.87.mixed_ref, bf16[8,264,1280]{2,1,0:T(8,128)(2,1)} %get-tuple-element.118.dmixed_ref, f32[8,16,264]{2,1,0:T(8,128)} %get-tuple-element.119.lse_ref), custom_call_target="tpu_custom_call" | custom-call | flops 4730880000 | bytes 43470848 | tf_op jit(solution)/shard_map/attention_back/pallas_call | solution.py:61
  587.6 30.0 %g_qkv.1 = (bf16[8,80,3840]{2,1,0:T(8,128)(2,1)}, bf16[4,80,3840]{2,1,0:T(8,128)(2,1)}, bf16[4,80,3840]{2,1,0:T(8,128)(2,1)}) custom-call(s32[2]{0:T(128)} %pad_add_fusion.refs_0_, bf16[2112,1280]{1,0:T(8,128)(2,1)} %bitcast.50, bf16[2112,3840]{1,0:T(8,128)(2,1)} %bitcast.49), custom_call_target="tpu_custom_call" | custom-call | flops 25952256000 | bytes 31457280 | tf_op jit(solution)/shard_map/g_qkv/pallas_call | solution.py:378
  621.6 7.0 collective-permute-done.11
  633.5 41.8 %qkv_back.1 = (f32[2056,1280]{1,0:T(8,128)}, f32[8,1280]{1,0:T(8,128)}, f32[8,1280]{1,0:T(8,128)}) custom-call(bf16[1280,3840]{1,0:T(8,128)(2,1)} %all-gather.4.cloned.1.call-done.w_ref, bf16[8,264,3840]{2,1,0:T(8,128)(2,1)} %get-tuple-element.130.dpacked_ref, bf16[8,264,1280]{2,1,0:T(8,128)(2,1)} %get-tuple-element.86.x_ref, ...), custom_call_target="tpu_custom_call" | custom-call | flops 31142707200 | bytes 52884480 | tf_op jit(solution)/shard_map/qkv_back/pallas_call | solution.py:61
  678.3 9.4 %collective-permute-done.12 = bf16[4,80,3840]{2,1,0:T(8,128)(2,1)} collective-permute-done((bf16[4,80,3840]{2,1,0:T(8,128)(2,1)}, bf16[4,80,3840]{2,1,0:T(8,128)(2,1)}, u32[]{:S(2)}, u32[]{:S(2)}) %collective-permute-start.12) | collective-permute-done | bytes 2457632 | tf_op jit(solution)/shard_map/ppermute | solution.py:474
  694.4 10.7 %collective-permute-done.14 = bf16[320,1280]{1,0:T(8,128)(2,1)S(1)} collective-permute-done((bf16[320,1280]{1,0:T(8,128)(2,1)S(1)}, bf16[320,1280]{1,0:T(8,128)(2,1)S(1)}, u32[]{:S(2)}, u32[]{:S(2)}) %collective-permute-start.14) | collective-permute-done | bytes 819232 | tf_op jit(solution)/shard_map/ppermute | solution.py:409
  707.9 42.2 %down.1 = f32[2056,1280]{1,0:T(8,128)} custom-call(bf16[5120,1280]{1,0:T(8,128)(2,1)} %all-gather.6.cloned.1.call-done.w_ref, bf16[8,264,5120]{2,1,0:T(8,128)(2,1)} %get-tuple-element.135.active_ref, f32[8,264,1280]{2,1,0:T(8,128)} %get-tuple-element.108.hidden_ref, f32[1,1280]{1,0:T(1,128)} %reshape.242.bias_ref), custom_call_target="tpu_custom_call" | custom-call | flops 34603008000 | bytes 56079360 | tf_op jit(solution)/shard_map/down/pallas_call | solution.py:61
  767.9 8.2 %collective-permute-done.21 = f32[960]{0:T(1024)S(1)} collective-permute-done((f32[960]{0:T(1024)S(1)}, f32[960]{0:T(1024)S(1)}, u32[]{:S(2)}, u32[]{:S(2)}) %collective-permute-start.21) | collective-permute-done | bytes 3872 | tf_op jit(solution)/shard_map/ppermute | solution.py:502
  (177 shorter events, 108.3 us)
Async XLA Ops:
  7.2 90.3 %all-gather.4.cloned.1.call-start = ((), (), s32[]{:S(2)}) async-start(), calls=%async_computation.4 | async-start | bytes 10444800 | tf_op jit(solution)/shard_map/all_gather | solution.py:448
  7.9 215.0 %all-gather.8.cloned.1.call-start = ((), (), s32[]{:S(2)}) async-start(), calls=%async_computation.6 | async-start | bytes 17408000 | tf_op jit(solution)/shard_map/all_gather | solution.py:448
  14.8 4.5 collective-permute-start.1
  23.2 14.9 %collective-permute-start.3 = (bf16[8,960]{1,0:T(8,128)(2,1)S(1)}, bf16[8,960]{1,0:T(8,128)(2,1)S(1)}, u32[]{:S(2)}, u32[]{:S(2)}) collective-permute-start(bf16[8,960]{1,0:T(8,128)(2,1)S(1)} %pad_maximum_fusion.5), channel_id=1, source_target_pairs={{0,8},{4,12},{8,0},{12,4},{1,9},{5,13},{9,1},{13,5},{2,10},{6,14},... | collective-permute-start | bytes 46088 | tf_op jit(solution)/shard_map/ppermute | solution.py:454
  53.7 277.7 %all-gather.6.cloned.1.call-start = ((), (), s32[]{:S(2)}) async-start(), calls=%async_computation.5 | async-start | bytes 13926400 | tf_op jit(solution)/shard_map/all_gather | solution.py:448
  124.7 457.2 %reduce-scatter.5.cloned.1.call-start = ((), (), s32[]{:S(2)}) async-start(), calls=%async_computation.7 | async-start | bytes 4096000 | tf_op jit(solution)/shard_map/reduce_scatter | solution.py:481
  321.6 47.7 %collective-permute-start.4 = (bf16[8,320,1280]{2,1,0:T(8,128)(2,1)}, bf16[8,320,1280]{2,1,0:T(8,128)(2,1)}, u32[]{:S(2)}, u32[]{:S(2)}) collective-permute-start(bf16[8,320,1280]{2,1,0:T(8,128)(2,1)} %get-tuple-element.91), channel_id=1, source_target_pairs={{0,1},{1,0},{2,3},{3,2},{4,5},{5,4},{6,7},{7,6},{8,9},{9,8},{10,11... | collective-permute-start | bytes 19660808 | tf_op jit(solution)/shard_map/ppermute | solution.py:468
  395.5 21.9 %collective-permute-start.5 = (bf16[8,80,2560]{2,1,0:T(8,128)(2,1)}, bf16[8,80,2560]{2,1,0:T(8,128)(2,1)S(1)}, u32[]{:S(2)}, u32[]{:S(2)}) collective-permute-start(bf16[8,80,2560]{2,1,0:T(8,128)(2,1)} %get-tuple-element.99), channel_id=1, source_target_pairs={{0,1},{1,0},{2,3},{3,2},{4,5},{5,4},{6,7},{7,6},{8,9},{9,8},{10,11... | collective-permute-start | bytes 9830408 | tf_op jit(solution)/shard_map/ppermute | solution.py:468
  395.8 86.5 %collective-permute-start.6 = (bf16[4,320,1280]{2,1,0:T(8,128)(2,1)}, bf16[4,320,1280]{2,1,0:T(8,128)(2,1)}, u32[]{:S(2)}, u32[]{:S(2)}) collective-permute-start(bf16[4,320,1280]{2,1,0:T(8,128)(2,1)} %slice_add_fusion), channel_id=1, source_target_pairs={{0,2},{2,0},{1,3},{3,1},{4,6},{6,4},{5,7},{7,5},{8,10},{10,8},{9,1... | collective-permute-start | bytes 9830408 | tf_op jit(solution)/shard_map/ppermute | solution.py:474
  417.2 104.1 %collective-permute-start.8 = (bf16[8,80,2560]{2,1,0:T(8,128)(2,1)}, bf16[8,80,2560]{2,1,0:T(8,128)(2,1)}, u32[]{:S(2)}, u32[]{:S(2)}) collective-permute-start(bf16[8,80,2560]{2,1,0:T(8,128)(2,1)} %get-tuple-element.103), channel_id=1, source_target_pairs={{0,1},{1,0},{2,3},{3,2},{4,5},{5,4},{6,7},{7,6},{8,9},{9,8},{10,11... | collective-permute-start | bytes 9830408 | tf_op jit(solution)/shard_map/ppermute | solution.py:468
  421.9 82.4 %collective-permute-start.7 = (bf16[4,80,2560]{2,1,0:T(8,128)(2,1)}, bf16[4,80,2560]{2,1,0:T(8,128)(2,1)}, u32[]{:S(2)}, u32[]{:S(2)}) collective-permute-start(bf16[4,80,2560]{2,1,0:T(8,128)(2,1)} %slice_add_fusion.3), channel_id=1, source_target_pairs={{0,2},{2,0},{1,3},{3,1},{4,6},{6,4},{5,7},{7,5},{8,10},{10,8},{9,1... | collective-permute-start | bytes 4915208 | tf_op jit(solution)/shard_map/ppermute | solution.py:474
  489.1 131.0 %reduce-scatter.7.cloned.1.call-start = ((), (), s32[]{:S(2)}) async-start(), calls=%async_computation.8 | async-start | bytes 2048000 | tf_op jit(solution)/shard_map/reduce_scatter | solution.py:481
  526.7 55.7 %collective-permute-start.10 = (bf16[4,80,3840]{2,1,0:T(8,128)(2,1)}, bf16[4,80,3840]{2,1,0:T(8,128)(2,1)}, u32[]{:S(2)}, u32[]{:S(2)}) collective-permute-start(bf16[4,80,3840]{2,1,0:T(8,128)(2,1)} %pad_maximum_fusion.1), channel_id=1, source_target_pairs={{0,2},{2,0},{1,3},{3,1},{4,6},{6,4},{5,7},{7,5},{8,10},{10,8},{9,1... | collective-permute-start | bytes 7372808 | tf_op jit(solution)/shard_map/ppermute | solution.py:474
  581.9 93.4 %reduce-scatter.9.cloned.1.call-start = ((), (), s32[]{:S(2)}) async-start(), calls=%async_computation.9 | async-start | bytes 3072000 | tf_op jit(solution)/shard_map/reduce_scatter | solution.py:481
  620.1 8.5 %collective-permute-start.11 = (bf16[8,80,3840]{2,1,0:T(8,128)(2,1)}, bf16[8,80,3840]{2,1,0:T(8,128)(2,1)}, u32[]{:S(2)}, u32[]{:S(2)}) collective-permute-start(bf16[8,80,3840]{2,1,0:T(8,128)(2,1)} %get-tuple-element.129), channel_id=1, source_target_pairs={{0,1},{1,0},{2,3},{3,2},{4,5},{5,4},{6,7},{7,6},{8,9},{9,8},{10,11... | collective-permute-start | bytes 14745608 | tf_op jit(solution)/shard_map/ppermute | solution.py:468
  620.1 131.2 %reduce-scatter.11.cloned.1.call-start = ((), (), s32[]{:S(2)}) async-start(), calls=%async_computation.10 | async-start | bytes 3072000 | tf_op jit(solution)/shard_map/reduce_scatter | solution.py:481
  632.0 55.7 %collective-permute-start.12 = (bf16[4,80,3840]{2,1,0:T(8,128)(2,1)}, bf16[4,80,3840]{2,1,0:T(8,128)(2,1)}, u32[]{:S(2)}, u32[]{:S(2)}) collective-permute-start(bf16[4,80,3840]{2,1,0:T(8,128)(2,1)} %slice_add_fusion.1), channel_id=1, source_target_pairs={{0,2},{2,0},{1,3},{3,1},{4,6},{6,4},{5,7},{7,5},{8,10},{10,8},{9,1... | collective-permute-start | bytes 7372808 | tf_op jit(solution)/shard_map/ppermute | solution.py:474
  676.2 17.0 %collective-permute-start.15 = (bf16[80,2560]{1,0:T(8,128)(2,1)S(1)}, bf16[80,2560]{1,0:T(8,128)(2,1)}, u32[]{:S(2)}, u32[]{:S(2)}) collective-permute-start(bf16[80,2560]{1,0:T(8,128)(2,1)S(1)} %bitcast.43), channel_id=1, source_target_pairs={{0,16},{16,0},{1,17},{17,1},{2,18},{18,2},{3,19},{19,3},{4,20},{20... | collective-permute-start | bytes 1228808 | tf_op jit(solution)/shard_map/ppermute | solution.py:409
  677.8 27.3 %collective-permute-start.14 = (bf16[320,1280]{1,0:T(8,128)(2,1)S(1)}, bf16[320,1280]{1,0:T(8,128)(2,1)S(1)}, u32[]{:S(2)}, u32[]{:S(2)}) collective-permute-start(bf16[320,1280]{1,0:T(8,128)(2,1)S(1)} %bitcast.39), channel_id=1, source_target_pairs={{0,16},{16,0},{1,17},{17,1},{2,18},{18,2},{3,19},{19,3},{4,20},{20... | collective-permute-start | bytes 2457608 | tf_op jit(solution)/shard_map/ppermute | solution.py:409
  706.4 43.7 %collective-permute-start.13 = (bf16[80,3840]{1,0:T(8,128)(2,1)}, bf16[80,3840]{1,0:T(8,128)(2,1)S(1)}, u32[]{:S(2)}, u32[]{:S(2)}) collective-permute-start(bf16[80,3840]{1,0:T(8,128)(2,1)} %bitcast.13), channel_id=1, source_target_pairs={{0,16},{16,0},{1,17},{17,1},{2,18},{18,2},{3,19},{19,3},{4,20},{20... | collective-permute-start | bytes 1843208 | tf_op jit(solution)/shard_map/ppermute | solution.py:409
  753.1 3.8 collective-permute-start.18
  757.0 4.6 collective-permute-start.19
  762.4 15.5 %collective-permute-start.16 = (bf16[80,3840]{1,0:T(8,128)(2,1)}, bf16[80,3840]{1,0:T(8,128)(2,1)S(1)}, u32[]{:S(2)}, u32[]{:S(2)}) collective-permute-start(bf16[80,3840]{1,0:T(8,128)(2,1)} %bitcast.41), channel_id=1, source_target_pairs={{0,16},{16,0},{1,17},{17,1},{2,18},{18,2},{3,19},{19,3},{4,20},{20... | collective-permute-start | bytes 1843208 | tf_op jit(solution)/shard_map/ppermute | solution.py:409
  765.3 10.8 %collective-permute-start.21 = (f32[960]{0:T(1024)S(1)}, f32[960]{0:T(1024)S(1)}, u32[]{:S(2)}, u32[]{:S(2)}) collective-permute-start(f32[960]{0:T(1024)S(1)} %bitcast.46), channel_id=1, source_target_pairs={{0,16},{16,0},{1,17},{17,1},{2,18},{18,2},{3,19},{19,3},{4,20},{20... | collective-permute-start | bytes 11528 | tf_op jit(solution)/shard_map/ppermute | solution.py:502
  (26 other events, 489.0 us)
Sparse Core Ops, SparseCore 0:
  10.3 87.1 all-gather.3
  100.4 122.5 all-gather.7
  225.2 106.1 all-gather.5
  489.2 62.9 reduce-scatter.4
  582.0 38.0 reduce-scatter.6
  622.4 48.5 reduce-scatter.8
  693.4 48.9 reduce-scatter.10

commit v5 on v4

--- a/solution.py
+++ b/solution.py
@@ -600,12 +600,12 @@
         [whole(full_qkv), image(after(d_packed, last[0])), image(xpad), image(d_hidden), whole(gain_one)],
         [untouched(sds(SEQ * n, D, dtype=F32)), sums(D), sums(D)], "qkv_back", 3 * D * 3 * D * n * SP, staging)
     g_down, g_up = both_groups(after(p_down, last[0])), both_groups(after(p_up, last[0]))
-    last = links.second_stage(last, d_images, rest)
+    last = links.second_stage(last, d_images, rest, g_down, g_up)
     result, = call(
         down_kernel, n, [whole(full_down), image(after(active, last)), image(hidden), whole(b_down)],
         [untouched(sds(SEQ * n, D, dtype=F32))], "down", 2.5 * D * FF * n * SP, staging)
     rest = both_groups(after(rest, last))
-    last, rest, g_down, g_up, s_gain_one = after((links.third_stage(last), rest, g_down, g_up, s_gain_one), result)
+    last, rest, s_gain_one = after((links.third_stage(last), rest, s_gain_one), result)
     g_qkv = both_groups(last)
     g_up2, g_out = rest[:, :FF // 2], rest[:, FF // 2:]
     result, d_images = [jnp.transpose(a.reshape(SEQ, n, D), (1, 0, 2)) for a in (result, d_images)]

time: 792 us -> 783 us (0.989)
  waiting for transfers between devices: 169 us -> 156 us
    ppermute x4, waiting for transfers between devices: 10.7 us -> 0.01 us  [both_groups(): return shard.astype(F32) + lax.ppermute(shard, 'dp', SWAP).astype(F32)]
where the time goes in v5:
time: 783 us; the launch traced here: 777 us
  Pallas kernels  507 us (65%)
  waiting for transfers between devices  156 us (20%)
  other arithmetic  49.2 us (6%)
  local copies, waits for them, and re-layouts  25.3 us (3%)
  starting transfers between devices  24.7 us (3%)
  between operations  14.9 us (2%)
    pallas_call x10, Pallas kernels, grid_call(): pl.pallas_call(kernel, grid=grid, in_specs=[spec for _, spec in ins], out...  384 us
    pallas_call x5, Pallas kernels, weight_gradient(): pl.pallas_call(kernel, grid=(left.shape[1] // block, width // cols), in_s...  123 us
    all_gather x3, waiting for transfers between devices, gather(): return lax.all_gather(w, ('z', 'x', 'core'), axis=0, tiled=True)  99.2 us
    ppermute x4, waiting for transfers between devices, second_stage(): got_x = lax.ppermute(passed, 'x', SWAP)  22.4 us
    convert_element_type x4, other arithmetic, second_stage(): (keep.astype(F32) + got[:half].astype(F32) + got_x.astype(F32)).astype(BF)  21.1 us
  transfers between devices with their start and end apart: 29, of which 18 were waited for; matrix products, arithmetic and copies ran while one was open for 8% of the time, Pallas kernels for 62%

profile of v5, /device:TPU:0, one launch (start us, length us, event | category | flops | bytes accessed | tf_op | source)
XLA Modules:
  0.0 777.0 jit_solution(11293155128008242606)
XLA Ops:
  28.5 6.1 copy.28.x_ref
  40.1 13.6 %prepare.1 = (bf16[8,264,1280]{2,1,0:T(8,128)(2,1)}, bf16[8,264,1280]{2,1,0:T(8,128)(2,1)}, bf16[8,264,1280]{2,1,0:T(8,128)(2,1)}, f32[8,1280]{1,0:T(8,128)}) custom-call(bf16[8,257,1280]{2,1,0:T(8,128)(2,1)} %copy.28.x_ref, bf16[8,257,1280]{2,1,0:T(8,128)(2,1)} %copy.29.c_ref, f32[1,1280]{1,0:T(1,128)} %reshape.235.gain_ref, f32[1,1280]{1,0:T(1,128)} %reshape.236.shift_ref), custom_call_target="tpu_custom_call" | custom-call | flops 1081344000 | bytes 26798080 | tf_op jit(solution)/shard_map/prepare/pallas_call | solution.py:61
  54.5 43.0 %all-gather.4.cloned.1.call-done.w_ref = bf16[1280,3840]{1,0:T(8,128)(2,1)} async-done(((bf16[80,3840]{1,0:T(8,128)(2,1)}), bf16[1280,3840]{1,0:T(8,128)(2,1)}) %all-gather.4.cloned.1.call-update) | async-done | bytes 9830416 | tf_op jit(solution)/shard_map/all_gather | solution.py:448
  97.5 27.1 %qkv.1.packed_ref = bf16[8,264,3840]{2,1,0:T(8,128)(2,1)} custom-call(bf16[1280,3840]{1,0:T(8,128)(2,1)} %all-gather.4.cloned.1.call-done.w_ref, bf16[8,264,1280]{2,1,0:T(8,128)(2,1)} %get-tuple-element.81.normed_ref, f32[1,3840]{1,0:T(1,128)} %fusion.bias_ref), custom_call_target="tpu_custom_call" | custom-call | flops 25952256000 | bytes 31472640 | tf_op jit(solution)/shard_map/qkv/pallas_call | solution.py:61
  128.3 48.0 %attention.1 = (bf16[8,264,1280]{2,1,0:T(8,128)(2,1)}, f32[8,16,264]{2,1,0:T(8,128)}) custom-call(bf16[8,264,3840]{2,1,0:T(8,128)(2,1)} %qkv.1.packed_ref), custom_call_target="tpu_custom_call" | custom-call | flops 3379200000 | bytes 21762048 | tf_op jit(solution)/shard_map/attention/pallas_call | solution.py:61
  176.2 46.7 %all-gather.8.cloned.1.call-done.w_ref.w_up_ref.w_out_ref = bf16[1280,6400]{1,0:T(8,128)(2,1)} async-done(((bf16[80,6400]{1,0:T(8,128)(2,1)}), bf16[1280,6400]{1,0:T(8,128)(2,1)}) %all-gather.8.cloned.1.call-update) | async-done | bytes 16384016 | tf_op jit(solution)/shard_map/all_gather | solution.py:448
  222.9 15.9 %out.1 = (f32[8,264,1280]{2,1,0:T(8,128)}, bf16[8,264,1280]{2,1,0:T(8,128)(2,1)}) custom-call(bf16[1280,6400]{1,0:T(8,128)(2,1)} %all-gather.8.cloned.1.call-done.w_ref.w_up_ref.w_out_ref, bf16[8,264,1280]{2,1,0:T(8,128)(2,1)} %get-tuple-element.84.x_ref, bf16[8,264,1280]{2,1,0:T(8,128)(2,1)} %get-tuple-element.85.mixed_ref, f32[1,1280]{1,0:T(1,128)} %reshape.238.bias_ref, ...), custom_call_target="tpu_custom_call" | custom-call | flops 10380902400 | bytes 43432960 | tf_op jit(solution)/shard_map/out/pallas_call | solution.py:61
  238.9 45.7 %up.1 = (bf16[8,264,5120]{2,1,0:T(8,128)(2,1)}, bf16[8,264,5120]{2,1,0:T(8,128)(2,1)}) custom-call(bf16[1280,6400]{1,0:T(8,128)(2,1)} %all-gather.8.cloned.1.call-done.w_ref.w_up_ref.w_out_ref, bf16[8,264,1280]{2,1,0:T(8,128)(2,1)} %get-tuple-element.86.normed_ref, f32[1,5120]{1,0:T(1,128)} %reshape.241.bias_ref), custom_call_target="tpu_custom_call" | custom-call | flops 55364812800 | bytes 65064960 | tf_op jit(solution)/shard_map/up/pallas_call | solution.py:61
  284.6 37.0 %g_down.1 = (bf16[8,320,1280]{2,1,0:T(8,128)(2,1)}, bf16[4,320,1280]{2,1,0:T(8,128)(2,1)}, bf16[4,320,1280]{2,1,0:T(8,128)(2,1)}) custom-call(s32[2]{0:T(128)} %pad_add_fusion.refs_0_, bf16[2112,5120]{1,0:T(8,128)(2,1)} %bitcast.52, bf16[2112,1280]{1,0:T(8,128)(2,1)} %bitcast.51), custom_call_target="tpu_custom_call" | custom-call | flops 34603008000 | bytes 40140800 | tf_op jit(solution)/shard_map/g_down/pallas_call | solution.py:378
  322.0 9.5 %all-gather.6.cloned.1.call-done.w_ref = bf16[5120,1280]{1,0:T(8,128)(2,1)} async-done(((bf16[320,1280]{1,0:T(8,128)(2,1)}), bf16[5120,1280]{1,0:T(8,128)(2,1)}) %all-gather.6.cloned.1.call-update) | async-done | bytes 13107216 | tf_op jit(solution)/shard_map/all_gather | solution.py:448
  331.5 37.8 %down_back.1 = (bf16[8,264,5120]{2,1,0:T(8,128)(2,1)}, f32[8,5120]{1,0:T(8,128)}) custom-call(bf16[5120,1280]{1,0:T(8,128)(2,1)} %all-gather.6.cloned.1.call-done.w_ref, bf16[8,264,1280]{2,1,0:T(8,128)(2,1)} %get-tuple-element.92.c_ref, bf16[8,264,5120]{2,1,0:T(8,128)(2,1)} %get-tuple-element.93.slope_ref), custom_call_target="tpu_custom_call" | custom-call | flops 41523609600 | bytes 61931520 | tf_op jit(solution)/shard_map/down_back/pallas_call | solution.py:61
  374.3 21.2 %g_up_low.1 = (bf16[8,80,2560]{2,1,0:T(8,128)(2,1)}, bf16[4,80,2560]{2,1,0:T(8,128)(2,1)}, bf16[4,80,2560]{2,1,0:T(8,128)(2,1)}) custom-call(s32[2]{0:T(128)} %pad_add_fusion.refs_0_, bf16[2112,1280]{1,0:T(8,128)(2,1)} %bitcast.57, bf16[2112,5120]{1,0:T(8,128)(2,1)} %bitcast.53), custom_call_target="tpu_custom_call" | custom-call | flops 17301504000 | bytes 33587200 | tf_op jit(solution)/shard_map/g_up_low/pallas_call | solution.py:378
  395.8 21.3 %g_up_high.1 = (bf16[8,80,2560]{2,1,0:T(8,128)(2,1)}, bf16[4,80,2560]{2,1,0:T(8,128)(2,1)}, bf16[4,80,2560]{2,1,0:T(8,128)(2,1)}) custom-call(s32[2]{0:T(128)} %pad_add_fusion.refs_0_, bf16[2112,1280]{1,0:T(8,128)(2,1)} %bitcast.58, bf16[2112,5120]{1,0:T(8,128)(2,1)} %bitcast.54), custom_call_target="tpu_custom_call" | custom-call | flops 17301504000 | bytes 33587200 | tf_op jit(solution)/shard_map/g_up_high/pallas_call | solution.py:378
  423.8 58.5 %up_back.1 = (f32[8,264,1280]{2,1,0:T(8,128)}, bf16[8,264,1280]{2,1,0:T(8,128)(2,1)}, bf16[8,264,1280]{2,1,0:T(8,128)(2,1)}, f32[8,1280]{1,0:T(8,128)}, f32[8,1280]{1,0:T(8,128)}, /*index=5*/f32[8,1280]{1,0:T(8,128)}) custom-call(bf16[1280,6400]{1,0:T(8,128)(2,1)} %all-gather.8.cloned.1.call-done.w_ref.w_up_ref.w_out_ref, ...), custom_call_target="tpu_custom_call" | custom-call | flops 51904512000 | bytes 92369920 | tf_op jit(solution)/shard_map/up_back/pallas_call | solution.py:61
  482.3 6.8 add_convert_fusion
  489.1 15.2 %collective-permute-done.7 = bf16[4,80,2560]{2,1,0:T(8,128)(2,1)} collective-permute-done((bf16[4,80,2560]{2,1,0:T(8,128)(2,1)}, bf16[4,80,2560]{2,1,0:T(8,128)(2,1)}, u32[]{:S(2)}, u32[]{:S(2)}) %collective-permute-start.7) | collective-permute-done | bytes 1638432 | tf_op jit(solution)/shard_map/ppermute | solution.py:474
  508.0 13.1 %g_out.1 = (bf16[8,80,1280]{2,1,0:T(8,128)(2,1)}, bf16[4,80,1280]{2,1,0:T(8,128)(2,1)}, bf16[4,80,1280]{2,1,0:T(8,128)(2,1)}) custom-call(s32[2]{0:T(128)} %pad_add_fusion.refs_0_, bf16[2112,1280]{1,0:T(8,128)(2,1)} %bitcast.36, bf16[2112,1280]{1,0:T(8,128)(2,1)} %bitcast.59), custom_call_target="tpu_custom_call" | custom-call | flops 8650752000 | bytes 14090240 | tf_op jit(solution)/shard_map/g_out/pallas_call | solution.py:378
  528.7 53.2 %attention_back.1 = (bf16[8,264,3840]{2,1,0:T(8,128)(2,1)}, f32[8,2560]{1,0:T(8,128)}) custom-call(bf16[8,264,3840]{2,1,0:T(8,128)(2,1)} %qkv.1.packed_ref, bf16[8,264,1280]{2,1,0:T(8,128)(2,1)} %get-tuple-element.85.mixed_ref, bf16[8,264,1280]{2,1,0:T(8,128)(2,1)} %get-tuple-element.116.dmixed_ref, f32[8,16,264]{2,1,0:T(8,128)} %get-tuple-element.117.lse_ref), custom_call_target="tpu_custom_call" | custom-call | flops 4730880000 | bytes 43470848 | tf_op jit(solution)/shard_map/attention_back/pallas_call | solution.py:61
  587.6 29.9 %g_qkv.1 = (bf16[8,80,3840]{2,1,0:T(8,128)(2,1)}, bf16[4,80,3840]{2,1,0:T(8,128)(2,1)}, bf16[4,80,3840]{2,1,0:T(8,128)(2,1)}) custom-call(s32[2]{0:T(128)} %pad_add_fusion.refs_0_, bf16[2112,1280]{1,0:T(8,128)(2,1)} %bitcast.50, bf16[2112,3840]{1,0:T(8,128)(2,1)} %bitcast.49), custom_call_target="tpu_custom_call" | custom-call | flops 25952256000 | bytes 31457280 | tf_op jit(solution)/shard_map/g_qkv/pallas_call | solution.py:378
  620.2 8.4 %collective-permute-done.11 = bf16[8,80,3840]{2,1,0:T(8,128)(2,1)} collective-permute-done((bf16[8,80,3840]{2,1,0:T(8,128)(2,1)}, bf16[8,80,3840]{2,1,0:T(8,128)(2,1)}, u32[]{:S(2)}, u32[]{:S(2)}) %collective-permute-start.11) | collective-permute-done | bytes 4915232 | tf_op jit(solution)/shard_map/ppermute | solution.py:468
  635.5 41.6 %qkv_back.1 = (f32[2056,1280]{1,0:T(8,128)}, f32[8,1280]{1,0:T(8,128)}, f32[8,1280]{1,0:T(8,128)}) custom-call(bf16[1280,3840]{1,0:T(8,128)(2,1)} %all-gather.4.cloned.1.call-done.w_ref, bf16[8,264,3840]{2,1,0:T(8,128)(2,1)} %get-tuple-element.128.dpacked_ref, bf16[8,264,1280]{2,1,0:T(8,128)(2,1)} %get-tuple-element.84.x_ref, ...), custom_call_target="tpu_custom_call" | custom-call | flops 31142707200 | bytes 52884480 | tf_op jit(solution)/shard_map/qkv_back/pallas_call | solution.py:61
  680.9 6.8 collective-permute-done.14
  696.3 42.6 %down.1 = f32[2056,1280]{1,0:T(8,128)} custom-call(bf16[5120,1280]{1,0:T(8,128)(2,1)} %all-gather.6.cloned.1.call-done.w_ref, bf16[8,264,5120]{2,1,0:T(8,128)(2,1)} %get-tuple-element.135.active_ref, f32[8,264,1280]{2,1,0:T(8,128)} %get-tuple-element.106.hidden_ref, f32[1,1280]{1,0:T(1,128)} %reshape.242.bias_ref), custom_call_target="tpu_custom_call" | custom-call | flops 34603008000 | bytes 56079360 | tf_op jit(solution)/shard_map/down/pallas_call | solution.py:61
  759.9 7.0 collective-permute-done.21
  (177 shorter events, 106.0 us)
Async XLA Ops:
  7.2 90.3 %all-gather.4.cloned.1.call-start = ((), (), s32[]{:S(2)}) async-start(), calls=%async_computation.4 | async-start | bytes 10444800 | tf_op jit(solution)/shard_map/all_gather | solution.py:448
  7.9 215.0 %all-gather.8.cloned.1.call-start = ((), (), s32[]{:S(2)}) async-start(), calls=%async_computation.6 | async-start | bytes 17408000 | tf_op jit(solution)/shard_map/all_gather | solution.py:448
  14.8 4.5 collective-permute-start.1
  23.2 14.9 %collective-permute-start.3 = (bf16[8,960]{1,0:T(8,128)(2,1)S(1)}, bf16[8,960]{1,0:T(8,128)(2,1)S(1)}, u32[]{:S(2)}, u32[]{:S(2)}) collective-permute-start(bf16[8,960]{1,0:T(8,128)(2,1)S(1)} %pad_maximum_fusion.5), channel_id=1, source_target_pairs={{0,8},{4,12},{8,0},{12,4},{1,9},{5,13},{9,1},{13,5},{2,10},{6,14},... | collective-permute-start | bytes 46088 | tf_op jit(solution)/shard_map/ppermute | solution.py:454
  53.7 277.7 %all-gather.6.cloned.1.call-start = ((), (), s32[]{:S(2)}) async-start(), calls=%async_computation.5 | async-start | bytes 13926400 | tf_op jit(solution)/shard_map/all_gather | solution.py:448
  124.7 457.2 %reduce-scatter.5.cloned.1.call-start = ((), (), s32[]{:S(2)}) async-start(), calls=%async_computation.7 | async-start | bytes 4096000 | tf_op jit(solution)/shard_map/reduce_scatter | solution.py:481
  321.6 47.7 %collective-permute-start.4 = (bf16[8,320,1280]{2,1,0:T(8,128)(2,1)}, bf16[8,320,1280]{2,1,0:T(8,128)(2,1)}, u32[]{:S(2)}, u32[]{:S(2)}) collective-permute-start(bf16[8,320,1280]{2,1,0:T(8,128)(2,1)} %get-tuple-element.89), channel_id=1, source_target_pairs={{0,1},{1,0},{2,3},{3,2},{4,5},{5,4},{6,7},{7,6},{8,9},{9,8},{10,11... | collective-permute-start | bytes 19660808 | tf_op jit(solution)/shard_map/ppermute | solution.py:468
  395.5 21.9 %collective-permute-start.5 = (bf16[8,80,2560]{2,1,0:T(8,128)(2,1)}, bf16[8,80,2560]{2,1,0:T(8,128)(2,1)S(1)}, u32[]{:S(2)}, u32[]{:S(2)}) collective-permute-start(bf16[8,80,2560]{2,1,0:T(8,128)(2,1)} %get-tuple-element.97), channel_id=1, source_target_pairs={{0,1},{1,0},{2,3},{3,2},{4,5},{5,4},{6,7},{7,6},{8,9},{9,8},{10,11... | collective-permute-start | bytes 9830408 | tf_op jit(solution)/shard_map/ppermute | solution.py:468
  395.8 86.5 %collective-permute-start.6 = (bf16[4,320,1280]{2,1,0:T(8,128)(2,1)}, bf16[4,320,1280]{2,1,0:T(8,128)(2,1)}, u32[]{:S(2)}, u32[]{:S(2)}) collective-permute-start(bf16[4,320,1280]{2,1,0:T(8,128)(2,1)} %slice_add_fusion), channel_id=1, source_target_pairs={{0,2},{2,0},{1,3},{3,1},{4,6},{6,4},{5,7},{7,5},{8,10},{10,8},{9,1... | collective-permute-start | bytes 9830408 | tf_op jit(solution)/shard_map/ppermute | solution.py:474
  417.2 104.1 %collective-permute-start.8 = (bf16[8,80,2560]{2,1,0:T(8,128)(2,1)}, bf16[8,80,2560]{2,1,0:T(8,128)(2,1)}, u32[]{:S(2)}, u32[]{:S(2)}) collective-permute-start(bf16[8,80,2560]{2,1,0:T(8,128)(2,1)} %get-tuple-element.101), channel_id=1, source_target_pairs={{0,1},{1,0},{2,3},{3,2},{4,5},{5,4},{6,7},{7,6},{8,9},{9,8},{10,11... | collective-permute-start | bytes 9830408 | tf_op jit(solution)/shard_map/ppermute | solution.py:468
  421.9 82.4 %collective-permute-start.7 = (bf16[4,80,2560]{2,1,0:T(8,128)(2,1)}, bf16[4,80,2560]{2,1,0:T(8,128)(2,1)}, u32[]{:S(2)}, u32[]{:S(2)}) collective-permute-start(bf16[4,80,2560]{2,1,0:T(8,128)(2,1)} %slice_add_fusion.3), channel_id=1, source_target_pairs={{0,2},{2,0},{1,3},{3,1},{4,6},{6,4},{5,7},{7,5},{8,10},{10,8},{9,1... | collective-permute-start | bytes 4915208 | tf_op jit(solution)/shard_map/ppermute | solution.py:474
  489.1 131.0 %reduce-scatter.7.cloned.1.call-start = ((), (), s32[]{:S(2)}) async-start(), calls=%async_computation.8 | async-start | bytes 2048000 | tf_op jit(solution)/shard_map/reduce_scatter | solution.py:481
  526.7 55.7 %collective-permute-start.10 = (bf16[4,80,3840]{2,1,0:T(8,128)(2,1)}, bf16[4,80,3840]{2,1,0:T(8,128)(2,1)}, u32[]{:S(2)}, u32[]{:S(2)}) collective-permute-start(bf16[4,80,3840]{2,1,0:T(8,128)(2,1)} %pad_maximum_fusion.1), channel_id=1, source_target_pairs={{0,2},{2,0},{1,3},{3,1},{4,6},{6,4},{5,7},{7,5},{8,10},{10,8},{9,1... | collective-permute-start | bytes 7372808 | tf_op jit(solution)/shard_map/ppermute | solution.py:474
  581.9 99.0 %reduce-scatter.9.cloned.1.call-start = ((), (), s32[]{:S(2)}) async-start(), calls=%async_computation.9 | async-start | bytes 3072000 | tf_op jit(solution)/shard_map/reduce_scatter | solution.py:481
  620.1 8.5 %collective-permute-start.11 = (bf16[8,80,3840]{2,1,0:T(8,128)(2,1)}, bf16[8,80,3840]{2,1,0:T(8,128)(2,1)}, u32[]{:S(2)}, u32[]{:S(2)}) collective-permute-start(bf16[8,80,3840]{2,1,0:T(8,128)(2,1)} %get-tuple-element.127), channel_id=1, source_target_pairs={{0,1},{1,0},{2,3},{3,2},{4,5},{5,4},{6,7},{7,6},{8,9},{9,8},{10,11... | collective-permute-start | bytes 14745608 | tf_op jit(solution)/shard_map/ppermute | solution.py:468
  620.1 122.2 %reduce-scatter.11.cloned.1.call-start = ((), (), s32[]{:S(2)}) async-start(), calls=%async_computation.10 | async-start | bytes 3072000 | tf_op jit(solution)/shard_map/reduce_scatter | solution.py:481
  632.0 55.7 %collective-permute-start.14 = (bf16[4,80,3840]{2,1,0:T(8,128)(2,1)}, bf16[4,80,3840]{2,1,0:T(8,128)(2,1)}, u32[]{:S(2)}, u32[]{:S(2)}) collective-permute-start(bf16[4,80,3840]{2,1,0:T(8,128)(2,1)} %slice_add_fusion.1), channel_id=1, source_target_pairs={{0,2},{2,0},{1,3},{3,1},{4,6},{6,4},{5,7},{7,5},{8,10},{10,8},{9,1... | collective-permute-start | bytes 7372808 | tf_op jit(solution)/shard_map/ppermute | solution.py:474
  633.5 43.7 %collective-permute-start.13 = (bf16[80,2560]{1,0:T(8,128)(2,1)}, bf16[80,2560]{1,0:T(8,128)(2,1)}, u32[]{:S(2)}, u32[]{:S(2)}) collective-permute-start(bf16[80,2560]{1,0:T(8,128)(2,1)} %bitcast.12), channel_id=1, source_target_pairs={{0,16},{16,0},{1,17},{17,1},{2,18},{18,2},{3,19},{19,3},{4,20},{20... | collective-permute-start | bytes 1228808 | tf_op jit(solution)/shard_map/ppermute | solution.py:409
  635.0 43.4 %collective-permute-start.12 = (bf16[320,1280]{1,0:T(8,128)(2,1)S(1)}, bf16[320,1280]{1,0:T(8,128)(2,1)}, u32[]{:S(2)}, u32[]{:S(2)}) collective-permute-start(bf16[320,1280]{1,0:T(8,128)(2,1)S(1)} %bitcast.39), channel_id=1, source_target_pairs={{0,16},{16,0},{1,17},{17,1},{2,18},{18,2},{3,19},{19,3},{4,20},{20... | collective-permute-start | bytes 2457608 | tf_op jit(solution)/shard_map/ppermute | solution.py:409
  694.8 44.1 %collective-permute-start.15 = (bf16[80,3840]{1,0:T(8,128)(2,1)S(1)}, bf16[80,3840]{1,0:T(8,128)(2,1)}, u32[]{:S(2)}, u32[]{:S(2)}) collective-permute-start(bf16[80,3840]{1,0:T(8,128)(2,1)S(1)} %bitcast.43), channel_id=1, source_target_pairs={{0,16},{16,0},{1,17},{17,1},{2,18},{18,2},{3,19},{19,3},{4,20},{20... | collective-permute-start | bytes 1843208 | tf_op jit(solution)/shard_map/ppermute | solution.py:409
  744.1 3.8 collective-permute-start.18
  748.0 4.6 collective-permute-start.19
  753.2 15.5 %collective-permute-start.16 = (bf16[80,3840]{1,0:T(8,128)(2,1)}, bf16[80,3840]{1,0:T(8,128)(2,1)S(1)}, u32[]{:S(2)}, u32[]{:S(2)}) collective-permute-start(bf16[80,3840]{1,0:T(8,128)(2,1)} %bitcast.41), channel_id=1, source_target_pairs={{0,16},{16,0},{1,17},{17,1},{2,18},{18,2},{3,19},{19,3},{4,20},{20... | collective-permute-start | bytes 1843208 | tf_op jit(solution)/shard_map/ppermute | solution.py:409
  756.3 10.6 %collective-permute-start.21 = (f32[960]{0:T(1024)S(1)}, f32[960]{0:T(1024)S(1)}, u32[]{:S(2)}, u32[]{:S(2)}) collective-permute-start(f32[960]{0:T(1024)S(1)} %bitcast.46), channel_id=1, source_target_pairs={{0,16},{16,0},{1,17},{17,1},{2,18},{18,2},{3,19},{19,3},{4,20},{20... | collective-permute-start | bytes 11528 | tf_op jit(solution)/shard_map/ppermute | solution.py:502
  (26 other events, 288.5 us)
Sparse Core Ops, SparseCore 0:
  10.3 87.1 all-gather.3
  100.4 122.5 all-gather.7
  225.2 106.1 all-gather.5
  489.2 62.9 reduce-scatter.4
  582.0 38.0 reduce-scatter.6
  622.4 48.5 reduce-scatter.8
  693.4 48.9 reduce-scatter.10

commit v6 on v5

--- a/solution.py
+++ b/solution.py
@@ -362,7 +362,7 @@
 def weight_gradient(left, right, owners, place, relative, name, first=0, width=None):
     depth = left.shape[0] * left.shape[1]
     left, right = left.reshape(depth, -1), right.reshape(depth, -1)
-    block, cols, width = 640, 1280, width or right.shape[1]
+    block, cols, width = 640, 640, width or right.shape[1]
     if not relative:
         owners = left.shape[1] // block
     rows = left.shape[1] // owners

time: 783 us -> 791 us (1.010)
  Pallas kernels: 507 us -> 530 us
  waiting for transfers between devices: 156 us -> 141 us
    pallas_call x5, Pallas kernels: 123 us -> 146 us  [weight_gradient(): pl.pallas_call(kernel, grid=(left.shape[1] // block, width // cols), in_s...]
    all_gather x3, waiting for transfers between devices: 99.2 us -> 89.6 us  [gather(): return lax.all_gather(w, ('z', 'x', 'core'), axis=0, tiled=True)]
  transfers between devices with their start and end apart: 29 -> 29, of which waited for: 18 -> 16; matrix products, arithmetic and copies ran while one was open for 8% -> 8% of each run, Pallas kernels for 62% -> 64%
where the time goes in v6:
time: 791 us; the launch traced here: 785 us
  Pallas kernels  530 us (67%)
  waiting for transfers between devices  141 us (18%)
  other arithmetic  49.3 us (6%)
  local copies, waits for them, and re-layouts  25.3 us (3%)
  starting transfers between devices  24.9 us (3%)
  between operations  15 us (2%)
    pallas_call x10, Pallas kernels, grid_call(): pl.pallas_call(kernel, grid=grid, in_specs=[spec for _, spec in ins], out...  384 us
    pallas_call x5, Pallas kernels, weight_gradient(): pl.pallas_call(kernel, grid=(left.shape[1] // block, width // cols), in_s...  146 us
    all_gather x3, waiting for transfers between devices, gather(): return lax.all_gather(w, ('z', 'x', 'core'), axis=0, tiled=True)  89.6 us
    convert_element_type x4, other arithmetic, second_stage(): (keep.astype(F32) + got[:half].astype(F32) + got_x.astype(F32)).astype(BF)  21.2 us
    ppermute x4, waiting for transfers between devices, second_stage(): got_x = lax.ppermute(passed, 'x', SWAP)  18.9 us
  transfers between devices with their start and end apart: 29, of which 16 were waited for; matrix products, arithmetic and copies ran while one was open for 8% of the time, Pallas kernels for 64%

profile of v6, /device:TPU:0, one launch (start us, length us, event | category | flops | bytes accessed | tf_op | source)
XLA Modules:
  0.0 785.0 jit_solution(5848808212663897570)
XLA Ops:
  28.5 6.1 copy.28.x_ref
  40.1 13.6 %prepare.1 = (bf16[8,264,1280]{2,1,0:T(8,128)(2,1)}, bf16[8,264,1280]{2,1,0:T(8,128)(2,1)}, bf16[8,264,1280]{2,1,0:T(8,128)(2,1)}, f32[8,1280]{1,0:T(8,128)}) custom-call(bf16[8,257,1280]{2,1,0:T(8,128)(2,1)} %copy.28.x_ref, bf16[8,257,1280]{2,1,0:T(8,128)(2,1)} %copy.29.c_ref, f32[1,1280]{1,0:T(1,128)} %reshape.235.gain_ref, f32[1,1280]{1,0:T(1,128)} %reshape.236.shift_ref), custom_call_target="tpu_custom_call" | custom-call | flops 1081344000 | bytes 26798080 | tf_op jit(solution)/shard_map/prepare/pallas_call | solution.py:61
  54.5 43.0 %all-gather.4.cloned.1.call-done.w_ref = bf16[1280,3840]{1,0:T(8,128)(2,1)} async-done(((bf16[80,3840]{1,0:T(8,128)(2,1)}), bf16[1280,3840]{1,0:T(8,128)(2,1)}) %all-gather.4.cloned.1.call-update) | async-done | bytes 9830416 | tf_op jit(solution)/shard_map/all_gather | solution.py:448
  97.5 27.1 %qkv.1.packed_ref = bf16[8,264,3840]{2,1,0:T(8,128)(2,1)} custom-call(bf16[1280,3840]{1,0:T(8,128)(2,1)} %all-gather.4.cloned.1.call-done.w_ref, bf16[8,264,1280]{2,1,0:T(8,128)(2,1)} %get-tuple-element.81.normed_ref, f32[1,3840]{1,0:T(1,128)} %fusion.bias_ref), custom_call_target="tpu_custom_call" | custom-call | flops 25952256000 | bytes 31472640 | tf_op jit(solution)/shard_map/qkv/pallas_call | solution.py:61
  128.3 48.0 %attention.1 = (bf16[8,264,1280]{2,1,0:T(8,128)(2,1)}, f32[8,16,264]{2,1,0:T(8,128)}) custom-call(bf16[8,264,3840]{2,1,0:T(8,128)(2,1)} %qkv.1.packed_ref), custom_call_target="tpu_custom_call" | custom-call | flops 3379200000 | bytes 21762048 | tf_op jit(solution)/shard_map/attention/pallas_call | solution.py:61
  176.3 46.6 %all-gather.8.cloned.1.call-done.w_ref.w_up_ref.w_out_ref = bf16[1280,6400]{1,0:T(8,128)(2,1)} async-done(((bf16[80,6400]{1,0:T(8,128)(2,1)}), bf16[1280,6400]{1,0:T(8,128)(2,1)}) %all-gather.8.cloned.1.call-update) | async-done | bytes 16384016 | tf_op jit(solution)/shard_map/all_gather | solution.py:448
  222.9 15.9 %out.1 = (f32[8,264,1280]{2,1,0:T(8,128)}, bf16[8,264,1280]{2,1,0:T(8,128)(2,1)}) custom-call(bf16[1280,6400]{1,0:T(8,128)(2,1)} %all-gather.8.cloned.1.call-done.w_ref.w_up_ref.w_out_ref, bf16[8,264,1280]{2,1,0:T(8,128)(2,1)} %get-tuple-element.84.x_ref, bf16[8,264,1280]{2,1,0:T(8,128)(2,1)} %get-tuple-element.85.mixed_ref, f32[1,1280]{1,0:T(1,128)} %reshape.238.bias_ref, ...), custom_call_target="tpu_custom_call" | custom-call | flops 10380902400 | bytes 43432960 | tf_op jit(solution)/shard_map/out/pallas_call | solution.py:61
  238.9 45.7 %up.1 = (bf16[8,264,5120]{2,1,0:T(8,128)(2,1)}, bf16[8,264,5120]{2,1,0:T(8,128)(2,1)}) custom-call(bf16[1280,6400]{1,0:T(8,128)(2,1)} %all-gather.8.cloned.1.call-done.w_ref.w_up_ref.w_out_ref, bf16[8,264,1280]{2,1,0:T(8,128)(2,1)} %get-tuple-element.86.normed_ref, f32[1,5120]{1,0:T(1,128)} %reshape.241.bias_ref), custom_call_target="tpu_custom_call" | custom-call | flops 55364812800 | bytes 65064960 | tf_op jit(solution)/shard_map/up/pallas_call | solution.py:61
  284.6 46.6 %g_down.1 = (bf16[8,320,1280]{2,1,0:T(8,128)(2,1)}, bf16[4,320,1280]{2,1,0:T(8,128)(2,1)}, bf16[4,320,1280]{2,1,0:T(8,128)(2,1)}) custom-call(s32[2]{0:T(128)} %pad_add_fusion.refs_0_, bf16[2112,5120]{1,0:T(8,128)(2,1)} %bitcast.52, bf16[2112,1280]{1,0:T(8,128)(2,1)} %bitcast.51), custom_call_target="tpu_custom_call" | custom-call | flops 34603008000 | bytes 40140800 | tf_op jit(solution)/shard_map/g_down/pallas_call | solution.py:378
  331.4 37.9 %down_back.1 = (bf16[8,264,5120]{2,1,0:T(8,128)(2,1)}, f32[8,5120]{1,0:T(8,128)}) custom-call(bf16[5120,1280]{1,0:T(8,128)(2,1)} %all-gather.6.cloned.1.call-done.w_ref, bf16[8,264,1280]{2,1,0:T(8,128)(2,1)} %get-tuple-element.92.c_ref, bf16[8,264,5120]{2,1,0:T(8,128)(2,1)} %get-tuple-element.93.slope_ref), custom_call_target="tpu_custom_call" | custom-call | flops 41523609600 | bytes 61931520 | tf_op jit(solution)/shard_map/down_back/pallas_call | solution.py:61
  374.3 24.6 %g_up_low.1 = (bf16[8,80,2560]{2,1,0:T(8,128)(2,1)}, bf16[4,80,2560]{2,1,0:T(8,128)(2,1)}, bf16[4,80,2560]{2,1,0:T(8,128)(2,1)}) custom-call(s32[2]{0:T(128)} %pad_add_fusion.refs_0_, bf16[2112,1280]{1,0:T(8,128)(2,1)} %bitcast.57, bf16[2112,5120]{1,0:T(8,128)(2,1)} %bitcast.53), custom_call_target="tpu_custom_call" | custom-call | flops 17301504000 | bytes 33587200 | tf_op jit(solution)/shard_map/g_up_low/pallas_call | solution.py:378
  399.9 24.6 %g_up_high.1 = (bf16[8,80,2560]{2,1,0:T(8,128)(2,1)}, bf16[4,80,2560]{2,1,0:T(8,128)(2,1)}, bf16[4,80,2560]{2,1,0:T(8,128)(2,1)}) custom-call(s32[2]{0:T(128)} %pad_add_fusion.refs_0_, bf16[2112,1280]{1,0:T(8,128)(2,1)} %bitcast.58, bf16[2112,5120]{1,0:T(8,128)(2,1)} %bitcast.54), custom_call_target="tpu_custom_call" | custom-call | flops 17301504000 | bytes 33587200 | tf_op jit(solution)/shard_map/g_up_high/pallas_call | solution.py:378
  430.5 58.5 %up_back.1 = (f32[8,264,1280]{2,1,0:T(8,128)}, bf16[8,264,1280]{2,1,0:T(8,128)(2,1)}, bf16[8,264,1280]{2,1,0:T(8,128)(2,1)}, f32[8,1280]{1,0:T(8,128)}, f32[8,1280]{1,0:T(8,128)}, /*index=5*/f32[8,1280]{1,0:T(8,128)}) custom-call(bf16[1280,6400]{1,0:T(8,128)(2,1)} %all-gather.8.cloned.1.call-done.w_ref.w_up_ref.w_out_ref, ...), custom_call_target="tpu_custom_call" | custom-call | flops 51904512000 | bytes 92369920 | tf_op jit(solution)/shard_map/up_back/pallas_call | solution.py:61
  489.0 6.8 add_convert_fusion
  495.9 11.9 %collective-permute-done.7 = bf16[4,80,2560]{2,1,0:T(8,128)(2,1)} collective-permute-done((bf16[4,80,2560]{2,1,0:T(8,128)(2,1)}, bf16[4,80,2560]{2,1,0:T(8,128)(2,1)}, u32[]{:S(2)}, u32[]{:S(2)}) %collective-permute-start.7) | collective-permute-done | bytes 1638432 | tf_op jit(solution)/shard_map/ppermute | solution.py:474
  511.5 14.5 %g_out.1 = (bf16[8,80,1280]{2,1,0:T(8,128)(2,1)}, bf16[4,80,1280]{2,1,0:T(8,128)(2,1)}, bf16[4,80,1280]{2,1,0:T(8,128)(2,1)}) custom-call(s32[2]{0:T(128)} %pad_add_fusion.refs_0_, bf16[2112,1280]{1,0:T(8,128)(2,1)} %bitcast.36, bf16[2112,1280]{1,0:T(8,128)(2,1)} %bitcast.59), custom_call_target="tpu_custom_call" | custom-call | flops 8650752000 | bytes 14090240 | tf_op jit(solution)/shard_map/g_out/pallas_call | solution.py:378
  533.6 53.2 %attention_back.1 = (bf16[8,264,3840]{2,1,0:T(8,128)(2,1)}, f32[8,2560]{1,0:T(8,128)}) custom-call(bf16[8,264,3840]{2,1,0:T(8,128)(2,1)} %qkv.1.packed_ref, bf16[8,264,1280]{2,1,0:T(8,128)(2,1)} %get-tuple-element.85.mixed_ref, bf16[8,264,1280]{2,1,0:T(8,128)(2,1)} %get-tuple-element.116.dmixed_ref, f32[8,16,264]{2,1,0:T(8,128)} %get-tuple-element.117.lse_ref), custom_call_target="tpu_custom_call" | custom-call | flops 4730880000 | bytes 43470848 | tf_op jit(solution)/shard_map/attention_back/pallas_call | solution.py:61
  592.4 35.2 %g_qkv.1 = (bf16[8,80,3840]{2,1,0:T(8,128)(2,1)}, bf16[4,80,3840]{2,1,0:T(8,128)(2,1)}, bf16[4,80,3840]{2,1,0:T(8,128)(2,1)}) custom-call(s32[2]{0:T(128)} %pad_add_fusion.refs_0_, bf16[2112,1280]{1,0:T(8,128)(2,1)} %bitcast.50, bf16[2112,3840]{1,0:T(8,128)(2,1)} %bitcast.49), custom_call_target="tpu_custom_call" | custom-call | flops 25952256000 | bytes 31457280 | tf_op jit(solution)/shard_map/g_qkv/pallas_call | solution.py:378
  627.8 8.4 %collective-permute-done.11 = bf16[8,80,3840]{2,1,0:T(8,128)(2,1)} collective-permute-done((bf16[8,80,3840]{2,1,0:T(8,128)(2,1)}, bf16[8,80,3840]{2,1,0:T(8,128)(2,1)}, u32[]{:S(2)}, u32[]{:S(2)}) %collective-permute-start.11) | collective-permute-done | bytes 4915232 | tf_op jit(solution)/shard_map/ppermute | solution.py:468
  643.1 41.7 %qkv_back.1 = (f32[2056,1280]{1,0:T(8,128)}, f32[8,1280]{1,0:T(8,128)}, f32[8,1280]{1,0:T(8,128)}) custom-call(bf16[1280,3840]{1,0:T(8,128)(2,1)} %all-gather.4.cloned.1.call-done.w_ref, bf16[8,264,3840]{2,1,0:T(8,128)(2,1)} %get-tuple-element.128.dpacked_ref, bf16[8,264,1280]{2,1,0:T(8,128)(2,1)} %get-tuple-element.84.x_ref, ...), custom_call_target="tpu_custom_call" | custom-call | flops 31142707200 | bytes 52884480 | tf_op jit(solution)/shard_map/qkv_back/pallas_call | solution.py:61
  688.6 6.8 collective-permute-done.14
  695.4 5.5 add_convert_fusion.1
  704.2 42.6 %down.1 = f32[2056,1280]{1,0:T(8,128)} custom-call(bf16[5120,1280]{1,0:T(8,128)(2,1)} %all-gather.6.cloned.1.call-done.w_ref, bf16[8,264,5120]{2,1,0:T(8,128)(2,1)} %get-tuple-element.135.active_ref, f32[8,264,1280]{2,1,0:T(8,128)} %get-tuple-element.106.hidden_ref, f32[1,1280]{1,0:T(1,128)} %reshape.242.bias_ref), custom_call_target="tpu_custom_call" | custom-call | flops 34603008000 | bytes 56079360 | tf_op jit(solution)/shard_map/down/pallas_call | solution.py:61
  767.9 7.0 collective-permute-done.21
  (177 shorter events, 98.3 us)
Async XLA Ops:
  7.2 90.3 %all-gather.4.cloned.1.call-start = ((), (), s32[]{:S(2)}) async-start(), calls=%async_computation.4 | async-start | bytes 10444800 | tf_op jit(solution)/shard_map/all_gather | solution.py:448
  7.9 215.0 %all-gather.8.cloned.1.call-start = ((), (), s32[]{:S(2)}) async-start(), calls=%async_computation.6 | async-start | bytes 17408000 | tf_op jit(solution)/shard_map/all_gather | solution.py:448
  14.8 4.5 collective-permute-start.1
  23.2 14.9 %collective-permute-start.3 = (bf16[8,960]{1,0:T(8,128)(2,1)S(1)}, bf16[8,960]{1,0:T(8,128)(2,1)S(1)}, u32[]{:S(2)}, u32[]{:S(2)}) collective-permute-start(bf16[8,960]{1,0:T(8,128)(2,1)S(1)} %pad_maximum_fusion.5), channel_id=1, source_target_pairs={{0,8},{4,12},{8,0},{12,4},{1,9},{5,13},{9,1},{13,5},{2,10},{6,14},... | collective-permute-start | bytes 46088 | tf_op jit(solution)/shard_map/ppermute | solution.py:454
  53.7 277.7 %all-gather.6.cloned.1.call-start = ((), (), s32[]{:S(2)}) async-start(), calls=%async_computation.5 | async-start | bytes 13926400 | tf_op jit(solution)/shard_map/all_gather | solution.py:448
  124.7 462.2 %reduce-scatter.5.cloned.1.call-start = ((), (), s32[]{:S(2)}) async-start(), calls=%async_computation.7 | async-start | bytes 4096000 | tf_op jit(solution)/shard_map/reduce_scatter | solution.py:481
  331.2 38.1 %collective-permute-start.4 = (bf16[8,320,1280]{2,1,0:T(8,128)(2,1)}, bf16[8,320,1280]{2,1,0:T(8,128)(2,1)}, u32[]{:S(2)}, u32[]{:S(2)}) collective-permute-start(bf16[8,320,1280]{2,1,0:T(8,128)(2,1)} %get-tuple-element.89), channel_id=1, source_target_pairs={{0,1},{1,0},{2,3},{3,2},{4,5},{5,4},{6,7},{7,6},{8,9},{9,8},{10,11... | collective-permute-start | bytes 19660808 | tf_op jit(solution)/shard_map/ppermute | solution.py:468
  398.9 25.7 %collective-permute-start.5 = (bf16[8,80,2560]{2,1,0:T(8,128)(2,1)}, bf16[8,80,2560]{2,1,0:T(8,128)(2,1)S(1)}, u32[]{:S(2)}, u32[]{:S(2)}) collective-permute-start(bf16[8,80,2560]{2,1,0:T(8,128)(2,1)} %get-tuple-element.97), channel_id=1, source_target_pairs={{0,1},{1,0},{2,3},{3,2},{4,5},{5,4},{6,7},{7,6},{8,9},{9,8},{10,11... | collective-permute-start | bytes 9830408 | tf_op jit(solution)/shard_map/ppermute | solution.py:468
  399.2 89.8 %collective-permute-start.6 = (bf16[4,320,1280]{2,1,0:T(8,128)(2,1)}, bf16[4,320,1280]{2,1,0:T(8,128)(2,1)}, u32[]{:S(2)}, u32[]{:S(2)}) collective-permute-start(bf16[4,320,1280]{2,1,0:T(8,128)(2,1)} %slice_add_fusion), channel_id=1, source_target_pairs={{0,2},{2,0},{1,3},{3,1},{4,6},{6,4},{5,7},{7,5},{8,10},{10,8},{9,1... | collective-permute-start | bytes 9830408 | tf_op jit(solution)/shard_map/ppermute | solution.py:474
  424.6 101.5 %collective-permute-start.8 = (bf16[8,80,2560]{2,1,0:T(8,128)(2,1)}, bf16[8,80,2560]{2,1,0:T(8,128)(2,1)}, u32[]{:S(2)}, u32[]{:S(2)}) collective-permute-start(bf16[8,80,2560]{2,1,0:T(8,128)(2,1)} %get-tuple-element.101), channel_id=1, source_target_pairs={{0,1},{1,0},{2,3},{3,2},{4,5},{5,4},{6,7},{7,6},{8,9},{9,8},{10,11... | collective-permute-start | bytes 9830408 | tf_op jit(solution)/shard_map/ppermute | solution.py:468
  429.1 78.6 %collective-permute-start.7 = (bf16[4,80,2560]{2,1,0:T(8,128)(2,1)}, bf16[4,80,2560]{2,1,0:T(8,128)(2,1)}, u32[]{:S(2)}, u32[]{:S(2)}) collective-permute-start(bf16[4,80,2560]{2,1,0:T(8,128)(2,1)} %slice_add_fusion.3), channel_id=1, source_target_pairs={{0,2},{2,0},{1,3},{3,1},{4,6},{6,4},{5,7},{7,5},{8,10},{10,8},{9,1... | collective-permute-start | bytes 4915208 | tf_op jit(solution)/shard_map/ppermute | solution.py:474
  495.8 131.8 %reduce-scatter.7.cloned.1.call-start = ((), (), s32[]{:S(2)}) async-start(), calls=%async_computation.8 | async-start | bytes 2048000 | tf_op jit(solution)/shard_map/reduce_scatter | solution.py:481
  531.5 55.7 %collective-permute-start.10 = (bf16[4,80,3840]{2,1,0:T(8,128)(2,1)}, bf16[4,80,3840]{2,1,0:T(8,128)(2,1)}, u32[]{:S(2)}, u32[]{:S(2)}) collective-permute-start(bf16[4,80,3840]{2,1,0:T(8,128)(2,1)} %pad_maximum_fusion.1), channel_id=1, source_target_pairs={{0,2},{2,0},{1,3},{3,1},{4,6},{6,4},{5,7},{7,5},{8,10},{10,8},{9,1... | collective-permute-start | bytes 7372808 | tf_op jit(solution)/shard_map/ppermute | solution.py:474
  586.9 101.7 %reduce-scatter.9.cloned.1.call-start = ((), (), s32[]{:S(2)}) async-start(), calls=%async_computation.9 | async-start | bytes 3072000 | tf_op jit(solution)/shard_map/reduce_scatter | solution.py:481
  627.7 8.6 %collective-permute-start.11 = (bf16[8,80,3840]{2,1,0:T(8,128)(2,1)}, bf16[8,80,3840]{2,1,0:T(8,128)(2,1)}, u32[]{:S(2)}, u32[]{:S(2)}) collective-permute-start(bf16[8,80,3840]{2,1,0:T(8,128)(2,1)} %get-tuple-element.127), channel_id=1, source_target_pairs={{0,1},{1,0},{2,3},{3,2},{4,5},{5,4},{6,7},{7,6},{8,9},{9,8},{10,11... | collective-permute-start | bytes 14745608 | tf_op jit(solution)/shard_map/ppermute | solution.py:468
  627.8 122.5 %reduce-scatter.11.cloned.1.call-start = ((), (), s32[]{:S(2)}) async-start(), calls=%async_computation.10 | async-start | bytes 3072000 | tf_op jit(solution)/shard_map/reduce_scatter | solution.py:481
  639.7 55.7 %collective-permute-start.14 = (bf16[4,80,3840]{2,1,0:T(8,128)(2,1)}, bf16[4,80,3840]{2,1,0:T(8,128)(2,1)}, u32[]{:S(2)}, u32[]{:S(2)}) collective-permute-start(bf16[4,80,3840]{2,1,0:T(8,128)(2,1)} %slice_add_fusion.1), channel_id=1, source_target_pairs={{0,2},{2,0},{1,3},{3,1},{4,6},{6,4},{5,7},{7,5},{8,10},{10,8},{9,1... | collective-permute-start | bytes 7372808 | tf_op jit(solution)/shard_map/ppermute | solution.py:474
  641.1 43.7 %collective-permute-start.13 = (bf16[80,2560]{1,0:T(8,128)(2,1)}, bf16[80,2560]{1,0:T(8,128)(2,1)}, u32[]{:S(2)}, u32[]{:S(2)}) collective-permute-start(bf16[80,2560]{1,0:T(8,128)(2,1)} %bitcast.12), channel_id=1, source_target_pairs={{0,16},{16,0},{1,17},{17,1},{2,18},{18,2},{3,19},{19,3},{4,20},{20... | collective-permute-start | bytes 1228808 | tf_op jit(solution)/shard_map/ppermute | solution.py:409
  642.6 43.5 %collective-permute-start.12 = (bf16[320,1280]{1,0:T(8,128)(2,1)S(1)}, bf16[320,1280]{1,0:T(8,128)(2,1)}, u32[]{:S(2)}, u32[]{:S(2)}) collective-permute-start(bf16[320,1280]{1,0:T(8,128)(2,1)S(1)} %bitcast.39), channel_id=1, source_target_pairs={{0,16},{16,0},{1,17},{17,1},{2,18},{18,2},{3,19},{19,3},{4,20},{20... | collective-permute-start | bytes 2457608 | tf_op jit(solution)/shard_map/ppermute | solution.py:409
  702.5 44.3 %collective-permute-start.15 = (bf16[80,3840]{1,0:T(8,128)(2,1)S(1)}, bf16[80,3840]{1,0:T(8,128)(2,1)}, u32[]{:S(2)}, u32[]{:S(2)}) collective-permute-start(bf16[80,3840]{1,0:T(8,128)(2,1)S(1)} %bitcast.43), channel_id=1, source_target_pairs={{0,16},{16,0},{1,17},{17,1},{2,18},{18,2},{3,19},{19,3},{4,20},{20... | collective-permute-start | bytes 1843208 | tf_op jit(solution)/shard_map/ppermute | solution.py:409
  752.1 3.8 collective-permute-start.18
  756.0 4.7 collective-permute-start.19
  761.2 15.5 %collective-permute-start.16 = (bf16[80,3840]{1,0:T(8,128)(2,1)}, bf16[80,3840]{1,0:T(8,128)(2,1)S(1)}, u32[]{:S(2)}, u32[]{:S(2)}) collective-permute-start(bf16[80,3840]{1,0:T(8,128)(2,1)} %bitcast.41), channel_id=1, source_target_pairs={{0,16},{16,0},{1,17},{17,1},{2,18},{18,2},{3,19},{19,3},{4,20},{20... | collective-permute-start | bytes 1843208 | tf_op jit(solution)/shard_map/ppermute | solution.py:409
  764.3 10.6 %collective-permute-start.21 = (f32[960]{0:T(1024)S(1)}, f32[960]{0:T(1024)S(1)}, u32[]{:S(2)}, u32[]{:S(2)}) collective-permute-start(f32[960]{0:T(1024)S(1)} %bitcast.46), channel_id=1, source_target_pairs={{0,16},{16,0},{1,17},{17,1},{2,18},{18,2},{3,19},{19,3},{4,20},{20... | collective-permute-start | bytes 11528 | tf_op jit(solution)/shard_map/ppermute | solution.py:502
  (26 other events, 284.4 us)
Sparse Core Ops, SparseCore 0:
  10.3 87.1 all-gather.3
  100.4 122.5 all-gather.7
  225.2 102.1 all-gather.5
  496.0 61.2 reduce-scatter.4
  587.0 36.1 reduce-scatter.6
  627.9 49.4 reduce-scatter.8
  701.0 49.2 reduce-scatter.10
